TPU v7x, 32 devices: a whole 2x2x4 slice. The times are simulated.
32 devices in a mesh: groups: 2 (over y), phi: 4 (over z), ev: 4 (over x, core).
Axes of the slice: x: 2, y: 2, z: 4, core: 2. Of those that a mesh axis runs over, the one named last changes fastest.
Arguments:
- cell_feats: bfloat16 [8, 1024, 256], P(('groups', 'ev'), 'phi'), parts along dimension 0, may hold values from -3 to 3
- neighbours: int32 [8, 8, 4], P(('groups', 'ev'), 'phi'), parts along dimension 0, may hold values from 0 to 3
- member_cell: int32 [8, 512], P(('groups', 'ev'), 'phi'), parts along dimension 0, may hold values from 0 to 255, as said below
- member_jet: int32 [8, 512, 1], P(('groups', 'ev'), 'phi'), parts along dimension 0, may hold values from 0 to 15, as said below
- cotangent: bfloat16 [8, 1024, 256], P(('groups', 'ev'), 'phi'), parts along dimension 0, may hold values from -3 to 3
- message_weight: bfloat16 [256, 256], replicated, may hold values from -0.375 to 0.375
- query_weight: bfloat16 [256, 256], replicated, may hold values from -4 to 4
- key_weight: bfloat16 [256, 256], replicated, may hold values from -4 to 4
- value_weight: bfloat16 [256, 256], replicated, may hold values from -0.375 to 0.375
- output_weight: bfloat16 [256, 256], replicated, may hold values from -0.375 to 0.375
Outputs:
- out_cells: bfloat16 [8, 1024, 256], P(('groups', 'ev'), 'phi'), parts along dimension 0
- grad_cells: bfloat16 [8, 1024, 256], P(('groups', 'ev'), 'phi'), parts along dimension 0
- grad_message: float32 [512, 256], P('groups'), parts along dimension 0
- grad_query: float32 [512, 256], P('groups'), parts along dimension 0
- grad_key: float32 [512, 256], P('groups'), parts along dimension 0
- grad_value: float32 [512, 256], P('groups'), parts along dimension 0
- grad_output: float32 [512, 256], P('groups'), parts along dimension 0
There are 2 independent parts, one for each index of `groups`. A program takes and returns all parts, laid end to end along the dimension named above; an argument that names none is the same for every part. Nothing has to cross between parts.
Inputs may be any that keep to these rules, and one draw needn't show every extreme that they name: `member_cell`: within one sector's 128 constituents of an event the cells are distinct. `member_jet`: A constituent of sector p belongs to a jet owned by one of the sectors p - 1 to p + 1 on the loop (jet j is owned by sector j // 4). Among one sector's 128 constituents of an event at most 21 belong to one jet, and some jet has exactly 21 of them.
All inputs are finite; a program needn't handle non-finite values.
Results may differ from a plain program's by a relative error of at most 0.0065.
The roundings to bfloat16 on the way count: a program that leaves them out, or rounds other values in their place, can miss the bound.
Values may be sent and summed in bfloat16 or wider, within the bound.
No kernel may reach another device: no remote copies, remote signals or barrier semaphores. Data moves between devices by JAX's collectives and lax.ppermute only.
A program may use at most 64 MiB of HBM per device.

v0:
```python
import math

import jax
import jax.numpy as jnp
from jax import lax
from jax.sharding import PartitionSpec as P

HEADS = 8
BLOCK = 128
NBRS = 4
JET_DEV = 4


def extended_2(cells, sides, width):
    for axis, dim in sides:
        count = lax.axis_size(axis)
        head = lax.slice_in_dim(cells, 0, width, axis=dim)
        tail = lax.slice_in_dim(cells, cells.shape[dim] - width, cells.shape[dim], axis=dim)
        cells = jnp.concatenate(
            [
                lax.ppermute(tail, axis, [(i, (i + 1) % count) for i in range(count)]),
                cells,
                lax.ppermute(head, axis, [((i + 1) % count, i) for i in range(count)]),
            ],
            axis=dim,
        )
    return cells


def shortened(value):
    return jax.tree.map(lambda a: a.astype(jnp.bfloat16) if a.dtype == jnp.float32 else a, value)


def passed_along(block, axis, distance):
    devices = range(lax.axis_size(axis))
    route = [((i - distance) % len(devices), i) for i in devices]
    return lax.ppermute(block, axis, route)


def silu_slope(values):
    sigmoid = jax.nn.sigmoid(values)
    return sigmoid * (1.0 + values * (1.0 - sigmoid))


def attend_forward(members, present, query_weight, key_weight, value_weight, output_weight):
    jet_count, slot_count, channels = members.shape
    head_size = channels // HEADS
    score_scale = 1.0 / math.sqrt(head_size)
    flat_members = members.reshape(jet_count * slot_count, channels)

    def project(weight):
        result = jnp.dot(flat_members, weight, preferred_element_type=jnp.float32)
        return result.astype(jnp.bfloat16).reshape(jet_count, slot_count, HEADS, head_size)

    queries = project(query_weight)
    keyed = project(key_weight)
    valued = project(value_weight)
    scores = jnp.einsum("jqnd,jknd->jnqk", queries, keyed, preferred_element_type=jnp.float32)
    scores = jnp.where(present[:, None, None, :] > 0.5, scores * score_scale, -1e30)
    largest = jnp.max(scores, axis=-1, keepdims=True)
    powers = jnp.exp(scores - largest)
    chances = powers / jnp.sum(powers, axis=-1, keepdims=True)
    chances_low = chances.astype(jnp.bfloat16)
    mixture = jnp.einsum("jnqk,jknd->jqnd", chances_low, valued, preferred_element_type=jnp.float32)
    mixture = mixture.astype(jnp.bfloat16).reshape(jet_count * slot_count, channels)
    attended = jnp.dot(mixture, output_weight, preferred_element_type=jnp.float32).astype(
        jnp.bfloat16
    )
    return (
        attended.reshape(jet_count, slot_count, channels),
        (queries, keyed, valued, chances, chances_low, mixture),
    )


def attend_backward(
    members, saved, upstream, query_weight, key_weight, value_weight, output_weight
):
    queries, keyed, valued, chances, chances_low, mixture = saved
    jet_count, slot_count, channels = members.shape
    head_size = channels // HEADS
    score_scale = 1.0 / math.sqrt(head_size)
    flat_members = members.reshape(jet_count * slot_count, channels)
    flat_upstream = upstream.reshape(jet_count * slot_count, channels)
    output_term = jnp.dot(mixture.T, flat_upstream, preferred_element_type=jnp.float32)
    grad_mix = jnp.dot(flat_upstream, output_weight.T, preferred_element_type=jnp.float32)
    grad_mix = grad_mix.astype(jnp.bfloat16).reshape(jet_count, slot_count, HEADS, head_size)
    grad_chances = jnp.einsum(
        "jqnd,jknd->jnqk", grad_mix, valued, preferred_element_type=jnp.float32
    )
    grad_vals = jnp.einsum(
        "jnqk,jqnd->jknd", chances_low, grad_mix, preferred_element_type=jnp.float32
    )
    grad_vals = grad_vals.astype(jnp.bfloat16)
    inner_sum = jnp.sum(chances * grad_chances, axis=-1, keepdims=True)
    grad_scores = (chances * (grad_chances - inner_sum) * score_scale).astype(jnp.bfloat16)
    grad_queries = jnp.einsum(
        "jnqk,jknd->jqnd", grad_scores, keyed, preferred_element_type=jnp.float32
    )
    grad_keys = jnp.einsum(
        "jnqk,jqnd->jknd", grad_scores, queries, preferred_element_type=jnp.float32
    )
    flat_queries = grad_queries.astype(jnp.bfloat16).reshape(jet_count * slot_count, channels)
    flat_keys = grad_keys.astype(jnp.bfloat16).reshape(jet_count * slot_count, channels)
    flat_vals = grad_vals.reshape(jet_count * slot_count, channels)
    query_term = jnp.dot(flat_members.T, flat_queries, preferred_element_type=jnp.float32)
    key_term = jnp.dot(flat_members.T, flat_keys, preferred_element_type=jnp.float32)
    value_term = jnp.dot(flat_members.T, flat_vals, preferred_element_type=jnp.float32)
    grad_members = jnp.dot(flat_queries, query_weight.T, preferred_element_type=jnp.float32)
    grad_members = grad_members + jnp.dot(
        flat_keys, key_weight.T, preferred_element_type=jnp.float32
    )
    grad_members = grad_members + jnp.dot(
        flat_vals, value_weight.T, preferred_element_type=jnp.float32
    )
    grad_members = grad_members.astype(jnp.bfloat16).reshape(jet_count, slot_count, channels)
    return (grad_members, (query_term, key_term, value_term, output_term))


def direct_route(entries, mover):
    radius = (len(entries) - 1) // 2
    routed = []
    for slot_index in range(len(entries)):
        if slot_index == radius:
            routed.append(entries[radius])
        else:
            routed.append(mover(entries[2 * radius - slot_index], radius - slot_index))
    return routed


def on_device(
    cell_feats,
    neighbours,
    member_cell,
    member_jet,
    cotangent,
    message_weight,
    query_weight,
    key_weight,
    value_weight,
    output_weight,
):
    events, per_device, channels = cell_feats.shape
    sectors = lax.axis_size("phi")
    sector = lax.axis_index("phi")
    blocks = per_device // BLOCK
    members_dev = member_cell.shape[1]
    radius = min(4, (sectors - 1) // 2)
    window = 2 * radius + 1
    capacity = max(2, 2 * members_dev // (JET_DEV * window))
    slot_count = window * capacity
    window_jets = window * JET_DEV
    tiles = cell_feats.reshape(events, blocks, BLOCK, channels)
    extended = extended_2(tiles, (("phi", 1),), 1)
    counts = jnp.sum(
        (neighbours[..., None] == jnp.arange(blocks + 2, dtype=jnp.int32)).astype(jnp.bfloat16),
        axis=2,
    )
    gathered = jnp.einsum(
        "ebj,ejch->ebch", counts, extended, preferred_element_type=jnp.float32
    ) * (1.0 / NBRS)
    flat_gathered = gathered.astype(jnp.bfloat16).reshape(events * per_device, channels)
    before_act = jnp.dot(flat_gathered, message_weight, preferred_element_type=jnp.float32)
    hidden = (
        cell_feats.reshape(-1, channels).astype(jnp.float32) + jax.nn.silu(before_act)
    ).astype(jnp.bfloat16)
    hidden = hidden.reshape(events, per_device, channels)
    jet_ids = member_jet[..., 0]
    owner = jet_ids // JET_DEV
    offset_slot = (owner - sector + radius + sectors) % sectors
    local_ids = offset_slot * JET_DEV + jet_ids % JET_DEV
    positions = jnp.arange(members_dev, dtype=jnp.int32)
    jet_match = local_ids[..., None] == jnp.arange(window_jets, dtype=jnp.int32)
    earlier = (positions[:, None] > positions[None, :]).astype(jnp.bfloat16)
    prior = jnp.einsum(
        "ik,ekj->eij", earlier, jet_match.astype(jnp.bfloat16), preferred_element_type=jnp.float32
    )
    ranks = jnp.sum(jnp.where(jet_match, prior, 0.0), axis=-1).astype(jnp.int32)
    targets = local_ids * capacity + ranks
    slot_ids = jnp.arange(window_jets * capacity, dtype=jnp.int32)
    occupant = (
        jnp.sum(jnp.where(targets[..., None] == slot_ids, positions[None, :, None] + 1, 0), axis=1)
        - 1
    )
    picked = jnp.where(occupant >= 0, occupant, members_dev)
    cell_ids = jnp.arange(per_device, dtype=jnp.int32)
    holder = (
        jnp.sum(
            jnp.where(member_cell[..., None] == cell_ids, positions[None, :, None] + 1, 0), axis=1
        )
        - 1
    )
    holder_pick = jnp.where(holder >= 0, holder, members_dev)

    def to_slots(source):
        chosen = jnp.take_along_axis(source, member_cell[..., None], axis=1)
        padded = jnp.concatenate([chosen, jnp.zeros((events, 1, channels), chosen.dtype)], axis=1)
        placed_rows = jnp.take_along_axis(padded, picked[..., None], axis=1)
        return placed_rows.reshape(events, window, JET_DEV, capacity, channels)

    def to_cells(arrived_rows):
        flattened = arrived_rows.reshape(events, window_jets * capacity, channels)
        returned = jnp.take_along_axis(flattened, targets[..., None], axis=1)
        padded = jnp.concatenate(
            [returned, jnp.zeros((events, 1, channels), returned.dtype)], axis=1
        )
        return jnp.take_along_axis(padded, holder_pick[..., None], axis=1)

    feature_slots = to_slots(hidden)
    grad_slots = to_slots(cotangent)
    mask_slots = (occupant >= 0).astype(jnp.bfloat16).reshape(events, window, JET_DEV, capacity)
    outgoing = [
        (feature_slots[:, slot_index], grad_slots[:, slot_index], mask_slots[:, slot_index])
        for slot_index in range(window)
    ]
    arrived = direct_route(
        outgoing,
        lambda bundle, distance: jax.tree.map(
            lambda part, own: part.astype(own.dtype),
            passed_along(shortened(bundle), "phi", distance),
            bundle,
        ),
    )
    members = jnp.stack([entry[0] for entry in arrived], axis=2).reshape(
        events * JET_DEV, slot_count, channels
    )
    upstream = jnp.stack([entry[1] for entry in arrived], axis=2).reshape(
        events * JET_DEV, slot_count, channels
    )
    present = jnp.stack([entry[2] for entry in arrived], axis=2).reshape(
        events * JET_DEV, slot_count
    )
    attended, saved = attend_forward(
        members, present, query_weight, key_weight, value_weight, output_weight
    )
    grad_members, weight_terms = attend_backward(
        members, saved, upstream, query_weight, key_weight, value_weight, output_weight
    )
    attended_view = attended.reshape(events, JET_DEV, window, capacity, channels)
    grad_view = grad_members.reshape(events, JET_DEV, window, capacity, channels)
    returning = [
        (attended_view[:, :, slot_index], grad_view[:, :, slot_index])
        for slot_index in range(window)
    ]
    delivered = direct_route(
        returning,
        lambda bundle, distance: jax.tree.map(
            lambda part, own: part.astype(own.dtype),
            passed_along(shortened(bundle), "phi", distance),
            bundle,
        ),
    )
    returned_out = jnp.stack([entry[0] for entry in delivered], axis=1)
    returned_grad = jnp.stack([entry[1] for entry in delivered], axis=1)
    out_cells = (hidden.astype(jnp.float32) + to_cells(returned_out).astype(jnp.float32)).astype(
        jnp.bfloat16
    )
    grad_hidden = cotangent.astype(jnp.float32) + to_cells(returned_grad).astype(jnp.float32)
    grad_before = (grad_hidden.reshape(-1, channels) * silu_slope(before_act)).astype(jnp.bfloat16)
    message_term = jnp.dot(flat_gathered.T, grad_before, preferred_element_type=jnp.float32)
    grad_gathered = jnp.dot(
        grad_before, message_weight.T, preferred_element_type=jnp.float32
    ).astype(jnp.bfloat16)
    grad_gathered = grad_gathered.reshape(events, blocks, BLOCK, channels)
    grad_extended = jnp.einsum(
        "ebj,ebch->ejch", counts, grad_gathered, preferred_element_type=jnp.float32
    ) * (1.0 / NBRS)
    grad_extended = grad_extended.astype(jnp.bfloat16)
    from_lower = passed_along(grad_extended[:, blocks + 1 :], "phi", 1)
    from_upper = passed_along(grad_extended[:, :1], "phi", -1)
    summed = grad_hidden.reshape(events, blocks, BLOCK, channels) + grad_extended[
        :, 1 : blocks + 1
    ].astype(jnp.float32)
    summed = summed + jnp.pad(
        from_lower.astype(jnp.float32), ((0, 0), (0, blocks - 1), (0, 0), (0, 0))
    )
    summed = summed + jnp.pad(
        from_upper.astype(jnp.float32), ((0, 0), (blocks - 1, 0), (0, 0), (0, 0))
    )
    grad_cells = summed.astype(jnp.bfloat16).reshape(events, per_device, channels)
    totals = lax.psum(
        (message_term, weight_terms[0], weight_terms[1], weight_terms[2], weight_terms[3]),
        ("phi", "ev"),
    )
    squares = jnp.sum(jnp.stack([jnp.sum(matrix * matrix) for matrix in totals]))
    bound = math.sqrt(5.0) * channels
    factor = bound / jnp.maximum(jnp.sqrt(squares), bound)
    return (
        out_cells,
        grad_cells,
        totals[0] * factor,
        totals[1] * factor,
        totals[2] * factor,
        totals[3] * factor,
        totals[4] * factor,
    )


def solution(mesh):
    in_specs = (
        P(("groups", "ev"), "phi", None),
        P(("groups", "ev"), "phi", None),
        P(("groups", "ev"), "phi"),
        P(("groups", "ev"), "phi", None),
        P(("groups", "ev"), "phi", None),
        P(),
        P(),
        P(),
        P(),
        P(),
    )
    out_specs = (
        P(("groups", "ev"), "phi", None),
        P(("groups", "ev"), "phi", None),
        P("groups", None),
        P("groups", None),
        P("groups", None),
        P("groups", None),
        P("groups", None),
    )
    return jax.shard_map(
        on_device, mesh=mesh, in_specs=in_specs, out_specs=out_specs, check_vma=False
    )
```

profile of v0, /device:TPU:0, one launch (start us, length us, event | category | flops | bytes accessed | tf_op | source)
XLA Modules:
  0.0 195.5 jit_solution(7533739546687173720)
XLA Ops:
  8.2 4.6 %fusion.41 = s32[252]{0:T(256)S(1)} fusion(s32[128]{0:T(128)S(1)} %iota_add_fusion, s32[128]{0:T(128)S(1)} %get-tuple-element.42), kind=kLoop, calls=%fused_computation.93 | loop fusion | flops 96516 | bytes 2032 | tf_op jit(solution)/shard_map/reduce_sum | solution.py:181
  12.9 3.1 %collective-permute-start.4 = (bf16[1,4,21]{2,1,0:T(4,128)(2,1)S(1)}, bf16[1,4,21]{2,1,0:T(4,128)(2,1)S(1)}, u32[]{:S(2)}, u32[]{:S(2)}) collective-permute-start(bf16[1,4,21]{2,1,0:T(4,128)(2,1)S(1)} %get-tuple-element.38), channel_id=1, source_target_pairs={{12,0},{0,4},{4,8},{8,12},{13,1},{1,5},{5,9},{9,13},{14,2},{2,6},{... | collective-permute-start | bytes 512 | tf_op jit(solution)/shard_map/ppermute | solution.py:37
  16.0 2.1 %collective-permute-start.5 = (bf16[1,4,21]{2,1,0:T(4,128)(2,1)S(1)}, bf16[1,4,21]{2,1,0:T(4,128)(2,1)S(1)}, u32[]{:S(2)}, u32[]{:S(2)}) collective-permute-start(bf16[1,4,21]{2,1,0:T(4,128)(2,1)S(1)} %get-tuple-element.39), channel_id=1, source_target_pairs={{4,0},{8,4},{12,8},{0,12},{5,1},{9,5},{13,9},{1,13},{6,2},{10,6},{... | collective-permute-start | bytes 512 | tf_op jit(solution)/shard_map/ppermute | solution.py:37
  18.1 1.0 copy.103
  19.4 3.8 %collective-permute-start.1 = (bf16[1,1,128,256]{3,1,2,0:T(2,128)(2,1)S(1)}, bf16[1,1,128,256]{3,1,2,0:T(2,128)(2,1)S(1)}, u32[]{:S(2)}, u32[]{:S(2)}) collective-permute-start(bf16[1,1,128,256]{3,1,2,0:T(2,128)(2,1)S(1)} %get-tuple-element.37), channel_id=1, source_target_pairs={{4,0},{8,4},{12,8},{0,12},{5,1},{9,5},{13,9},{1,13},{6,2},{10,6},{... | collective-permute-start | bytes 196616 | tf_op jit(solution)/shard_map/ppermute | solution.py:23
  25.3 2.3 %collective-permute-done = bf16[1,1,128,256]{3,1,2,0:T(2,128)(2,1)S(1)} collective-permute-done((bf16[1,1,128,256]{3,1,2,0:T(2,128)(2,1)S(1)}, bf16[1,1,128,256]{3,1,2,0:T(2,128)(2,1)S(1)}, u32[]{:S(2)}, u32[]{:S(2)}) %collective-permute-start) | collective-permute-done | bytes 65568 | tf_op jit(solution)/shard_map/ppermute | solution.py:21
  30.2 1.1 gather_fusion.5
  31.3 1.1 gather_fusion.1
  33.2 3.3 %collective-permute-start.9 = (bf16[1,4,21,256]{3,2,1,0:T(8,128)(2,1)S(1)}, bf16[1,4,21,256]{3,2,1,0:T(8,128)(2,1)S(1)}, u32[]{:S(2)}, u32[]{:S(2)}) collective-permute-start(bf16[1,4,21,256]{3,2,1,0:T(8,128)(2,1)S(1)} %get-tuple-element.28), channel_id=1, source_target_pairs={{4,0},{8,4},{12,8},{0,12},{5,1},{9,5},{13,9},{1,13},{6,2},{10,6},{... | collective-permute-start | bytes 129032 | tf_op jit(solution)/shard_map/ppermute | solution.py:37
  36.7 3.8 %collective-permute-start.3 = (bf16[1,4,21,256]{3,2,1,0:T(8,128)(2,1)S(1)}, bf16[1,4,21,256]{3,2,1,0:T(8,128)(2,1)S(1)}, u32[]{:S(2)}, u32[]{:S(2)}) collective-permute-start(bf16[1,4,21,256]{3,2,1,0:T(8,128)(2,1)S(1)} %get-tuple-element.34), channel_id=1, source_target_pairs={{4,0},{8,4},{12,8},{0,12},{5,1},{9,5},{13,9},{1,13},{6,2},{10,6},{... | collective-permute-start | bytes 129032 | tf_op jit(solution)/shard_map/ppermute | solution.py:37
  46.8 2.5 %fusion.73 = (f32[4,8,63]{2,1,0:T(8,128)S(1)}, f32[4,8,63,63]{2,3,1,0:T(8,128)}) fusion(pred[4,63]{1,0:T(4,128)(4,1)S(1)} %gt.32, bf16[4,63,8,32]{1,0,3,2:T(4,128)(2,1)S(1)} %reshape.621, bf16[4,63,8,32]{1,0,3,2:T(4,128)(2,1)} %reshape.620), kind=kOutput, calls=%fused_computation.171 | convolution fusion | flops 8636606 | bytes 774396 | tf_op jit(solution)/shard_map/sub | solution.py:61
  49.3 2.8 %fusion.10 = bf16[4,63,8,32]{1,3,2,0:T(8,128)(2,1)} fusion(f32[4,8,63,63]{2,3,1,0:T(8,128)S(1)} %fusion.31, bf16[4,63,8,32]{1,0,3,2:T(4,128)(2,1)S(1)} %reshape.621, f32[4,8,63,63]{2,3,1,0:T(8,128)} %get-tuple-element.52, f32[4,8,63]{2,1,0:T(8,128)S(1)} %get-tuple-element.51), kind=kOutput, calls=%fused_computation.23 | convolution fusion | flops 9084158 | bytes 1282176 | tf_op jit(solution)/shard_map/jnqk,jknd->jqnd/dot_general | solution.py:96
  52.1 2.9 %fusion.11 = bf16[4,63,8,32]{1,3,2,0:T(8,128)(2,1)} fusion(f32[4,8,63,63]{2,3,1,0:T(8,128)S(1)} %fusion.31, bf16[4,63,8,32]{1,0,3,2:T(4,128)(2,1)} %reshape.620, f32[4,8,63,63]{2,3,1,0:T(8,128)} %get-tuple-element.52, f32[4,8,63]{2,1,0:T(8,128)S(1)} %get-tuple-element.51), kind=kOutput, calls=%fused_computation.24 | convolution fusion | flops 9084158 | bytes 1282176 | tf_op jit(solution)/shard_map/jnqk,jqnd->jknd/dot_general | solution.py:99
  54.9 1.7 fusion.12
  59.6 0.9 fusion.80
  62.4 3.9 %collective-permute-start.7 = (bf16[1,4,21,256]{3,2,1,0:T(8,128)(2,1)S(1)}, bf16[1,4,21,256]{3,2,1,0:T(8,128)(2,1)S(1)}, u32[]{:S(2)}, u32[]{:S(2)}) collective-permute-start(bf16[1,4,21,256]{3,2,1,0:T(8,128)(2,1)S(1)} %get-tuple-element.31), channel_id=1, source_target_pairs={{4,0},{8,4},{12,8},{0,12},{5,1},{9,5},{13,9},{1,13},{6,2},{10,6},{... | collective-permute-start | bytes 129032 | tf_op jit(solution)/shard_map/ppermute | solution.py:37
  68.7 3.8 %collective-permute-start.11 = (bf16[1,4,21,256]{3,2,1,0:T(8,128)(2,1)S(1)}, bf16[1,4,21,256]{3,2,1,0:T(8,128)(2,1)S(1)}, u32[]{:S(2)}, u32[]{:S(2)}) collective-permute-start(bf16[1,4,21,256]{3,2,1,0:T(8,128)(2,1)S(1)} %get-tuple-element.25), channel_id=1, source_target_pairs={{4,0},{8,4},{12,8},{0,12},{5,1},{9,5},{13,9},{1,13},{6,2},{10,6},{... | collective-permute-start | bytes 129032 | tf_op jit(solution)/shard_map/ppermute | solution.py:37
  72.6 2.0 %collective-permute-done.10 = bf16[1,4,21,256]{3,2,1,0:T(8,128)(2,1)S(1)} collective-permute-done((bf16[1,4,21,256]{3,2,1,0:T(8,128)(2,1)S(1)}, bf16[1,4,21,256]{3,2,1,0:T(8,128)(2,1)S(1)}, u32[]{:S(2)}, u32[]{:S(2)}) %collective-permute-start.10) | collective-permute-done | bytes 43040 | tf_op jit(solution)/shard_map/ppermute | solution.py:37
  76.5 1.2 gather_fusion.7
  79.0 1.2 gather_fusion.3
  80.7 3.9 %collective-permute-start.13 = (bf16[1,1,128,256]{3,2,1,0:T(8,128)(2,1)S(1)}, bf16[1,1,128,256]{3,2,1,0:T(8,128)(2,1)S(1)}, u32[]{:S(2)}, u32[]{:S(2)}) collective-permute-start(bf16[1,1,128,256]{3,2,1,0:T(8,128)(2,1)S(1)} %get-tuple-element.23), channel_id=1, source_target_pairs={{4,0},{8,4},{12,8},{0,12},{5,1},{9,5},{13,9},{1,13},{6,2},{10,6},{... | collective-permute-start | bytes 196616 | tf_op jit(solution)/shard_map/ppermute | solution.py:37
  85.3 1.4 collective-permute-done.12
  87.5 89.5 %all-reduce.9.cloned.1.call-done = (f32[256,256]{1,0:T(8,128)}, f32[256,256]{1,0:T(8,128)}, f32[256,256]{1,0:T(8,128)}, f32[256,256]{1,0:T(8,128)}, f32[256,256]{1,0:T(8,128)}) async-done(((f32[256,256]{1,0:T(8,128)}, f32[256,256]{1,0:T(8,128)}, f32[256,256]{1,0:T(8,128)}, f32[256,256]{1,0:T(8,128)}, f32[256,256]{1,0:T(8,128)}), (f32[256,256]{1,0:T(8,128)}, f32[256,256]{1,0:T(8,128)}, f32[256,256]{1,0:T(8,128)}, ...) | async-done | bytes 1310736 | tf_op jit(solution)/shard_map/psum | solution.py:280
  177.0 1.7 multiply_reduce_fusion.1
  (156 shorter events, 31.8 us)
Async XLA Ops:
  7.2 21.0 %copy-start = (bf16[256,256]{1,0:T(8,128)(2,1)S(1)}, bf16[256,256]{1,0:T(8,128)(2,1)}, u32[]{:S(2)}) copy-start(bf16[256,256]{1,0:T(8,128)(2,1)} %param.23) | copy-start | bytes 393220
  7.2 169.8 %all-reduce.9.cloned.1.call-start = ((), (), s32[]{:S(2)}) async-start(), calls=%async_computation | async-start | bytes 2621440 | tf_op jit(solution)/shard_map/psum | solution.py:280
  12.9 12.2 %collective-permute-start.4 = (bf16[1,4,21]{2,1,0:T(4,128)(2,1)S(1)}, bf16[1,4,21]{2,1,0:T(4,128)(2,1)S(1)}, u32[]{:S(2)}, u32[]{:S(2)}) collective-permute-start(bf16[1,4,21]{2,1,0:T(4,128)(2,1)S(1)} %get-tuple-element.38), channel_id=1, source_target_pairs={{12,0},{0,4},{4,8},{8,12},{13,1},{1,5},{5,9},{9,13},{14,2},{2,6},{... | collective-permute-start | bytes 512 | tf_op jit(solution)/shard_map/ppermute | solution.py:37
  16.0 9.2 %collective-permute-start.5 = (bf16[1,4,21]{2,1,0:T(4,128)(2,1)S(1)}, bf16[1,4,21]{2,1,0:T(4,128)(2,1)S(1)}, u32[]{:S(2)}, u32[]{:S(2)}) collective-permute-start(bf16[1,4,21]{2,1,0:T(4,128)(2,1)S(1)} %get-tuple-element.39), channel_id=1, source_target_pairs={{4,0},{8,4},{12,8},{0,12},{5,1},{9,5},{13,9},{1,13},{6,2},{10,6},{... | collective-permute-start | bytes 512 | tf_op jit(solution)/shard_map/ppermute | solution.py:37
  19.1 5.2 %copy-start.1 = (bf16[1,256,256]{2,1,0:T(8,128)(2,1)S(1)}, bf16[1,256,256]{2,1,0:T(8,128)(2,1)}, u32[]{:S(2)}) copy-start(bf16[1,256,256]{2,1,0:T(8,128)(2,1)} %param.22) | copy-start | bytes 393220
  19.3 3.9 %copy-start.15 = (s32[1,128]{1,0:T(1,128)S(1)}, s32[1,128]{1,0:T(1,128)}, u32[]{:S(2)}) copy-start(s32[1,128]{1,0:T(1,128)} %param.20) | copy-start | bytes 1540
  19.3 8.2 %collective-permute-start = (bf16[1,1,128,256]{3,1,2,0:T(2,128)(2,1)S(1)}, bf16[1,1,128,256]{3,1,2,0:T(2,128)(2,1)S(1)}, u32[]{:S(2)}, u32[]{:S(2)}) collective-permute-start(bf16[1,1,128,256]{3,1,2,0:T(2,128)(2,1)S(1)} %get-tuple-element.36), channel_id=1, source_target_pairs={{0,4},{4,8},{8,12},{12,0},{1,5},{5,9},{9,13},{13,1},{2,6},{6,10},{... | collective-permute-start | bytes 196616 | tf_op jit(solution)/shard_map/ppermute | solution.py:21
  19.4 8.1 %collective-permute-start.1 = (bf16[1,1,128,256]{3,1,2,0:T(2,128)(2,1)S(1)}, bf16[1,1,128,256]{3,1,2,0:T(2,128)(2,1)S(1)}, u32[]{:S(2)}, u32[]{:S(2)}) collective-permute-start(bf16[1,1,128,256]{3,1,2,0:T(2,128)(2,1)S(1)} %get-tuple-element.37), channel_id=1, source_target_pairs={{4,0},{8,4},{12,8},{0,12},{5,1},{9,5},{13,9},{1,13},{6,2},{10,6},{... | collective-permute-start | bytes 196616 | tf_op jit(solution)/shard_map/ppermute | solution.py:23
  32.7 7.8 %collective-permute-start.8 = (bf16[1,4,21,256]{3,2,1,0:T(8,128)(2,1)S(1)}, bf16[1,4,21,256]{3,2,1,0:T(8,128)(2,1)S(1)}, u32[]{:S(2)}, u32[]{:S(2)}) collective-permute-start(bf16[1,4,21,256]{3,2,1,0:T(8,128)(2,1)S(1)} %get-tuple-element.27), channel_id=1, source_target_pairs={{12,0},{0,4},{4,8},{8,12},{13,1},{1,5},{5,9},{9,13},{14,2},{2,6},{... | collective-permute-start | bytes 129032 | tf_op jit(solution)/shard_map/ppermute | solution.py:37
  33.2 7.3 %collective-permute-start.9 = (bf16[1,4,21,256]{3,2,1,0:T(8,128)(2,1)S(1)}, bf16[1,4,21,256]{3,2,1,0:T(8,128)(2,1)S(1)}, u32[]{:S(2)}, u32[]{:S(2)}) collective-permute-start(bf16[1,4,21,256]{3,2,1,0:T(8,128)(2,1)S(1)} %get-tuple-element.28), channel_id=1, source_target_pairs={{4,0},{8,4},{12,8},{0,12},{5,1},{9,5},{13,9},{1,13},{6,2},{10,6},{... | collective-permute-start | bytes 129032 | tf_op jit(solution)/shard_map/ppermute | solution.py:37
  36.6 5.9 %collective-permute-start.2 = (bf16[1,4,21,256]{3,2,1,0:T(8,128)(2,1)S(1)}, bf16[1,4,21,256]{3,2,1,0:T(8,128)(2,1)S(1)}, u32[]{:S(2)}, u32[]{:S(2)}) collective-permute-start(bf16[1,4,21,256]{3,2,1,0:T(8,128)(2,1)S(1)} %get-tuple-element.33), channel_id=1, source_target_pairs={{12,0},{0,4},{4,8},{8,12},{13,1},{1,5},{5,9},{9,13},{14,2},{2,6},{... | collective-permute-start | bytes 129032 | tf_op jit(solution)/shard_map/ppermute | solution.py:37
  36.7 5.9 %collective-permute-start.3 = (bf16[1,4,21,256]{3,2,1,0:T(8,128)(2,1)S(1)}, bf16[1,4,21,256]{3,2,1,0:T(8,128)(2,1)S(1)}, u32[]{:S(2)}, u32[]{:S(2)}) collective-permute-start(bf16[1,4,21,256]{3,2,1,0:T(8,128)(2,1)S(1)} %get-tuple-element.34), channel_id=1, source_target_pairs={{4,0},{8,4},{12,8},{0,12},{5,1},{9,5},{13,9},{1,13},{6,2},{10,6},{... | collective-permute-start | bytes 129032 | tf_op jit(solution)/shard_map/ppermute | solution.py:37
  54.9 1.7 copy-start.17
  62.3 10.2 %collective-permute-start.6 = (bf16[1,4,21,256]{3,2,1,0:T(8,128)(2,1)S(1)}, bf16[1,4,21,256]{3,2,1,0:T(8,128)(2,1)S(1)}, u32[]{:S(2)}, u32[]{:S(2)}) collective-permute-start(bf16[1,4,21,256]{3,2,1,0:T(8,128)(2,1)S(1)} %get-tuple-element.30), channel_id=1, source_target_pairs={{12,0},{0,4},{4,8},{8,12},{13,1},{1,5},{5,9},{9,13},{14,2},{2,6},{... | collective-permute-start | bytes 129032 | tf_op jit(solution)/shard_map/ppermute | solution.py:37
  62.4 10.2 %collective-permute-start.7 = (bf16[1,4,21,256]{3,2,1,0:T(8,128)(2,1)S(1)}, bf16[1,4,21,256]{3,2,1,0:T(8,128)(2,1)S(1)}, u32[]{:S(2)}, u32[]{:S(2)}) collective-permute-start(bf16[1,4,21,256]{3,2,1,0:T(8,128)(2,1)S(1)} %get-tuple-element.31), channel_id=1, source_target_pairs={{4,0},{8,4},{12,8},{0,12},{5,1},{9,5},{13,9},{1,13},{6,2},{10,6},{... | collective-permute-start | bytes 129032 | tf_op jit(solution)/shard_map/ppermute | solution.py:37
  68.7 5.9 %collective-permute-start.10 = (bf16[1,4,21,256]{3,2,1,0:T(8,128)(2,1)S(1)}, bf16[1,4,21,256]{3,2,1,0:T(8,128)(2,1)S(1)}, u32[]{:S(2)}, u32[]{:S(2)}) collective-permute-start(bf16[1,4,21,256]{3,2,1,0:T(8,128)(2,1)S(1)} %get-tuple-element.24), channel_id=1, source_target_pairs={{12,0},{0,4},{4,8},{8,12},{13,1},{1,5},{5,9},{9,13},{14,2},{2,6},{... | collective-permute-start | bytes 129032 | tf_op jit(solution)/shard_map/ppermute | solution.py:37
  68.7 5.9 %collective-permute-start.11 = (bf16[1,4,21,256]{3,2,1,0:T(8,128)(2,1)S(1)}, bf16[1,4,21,256]{3,2,1,0:T(8,128)(2,1)S(1)}, u32[]{:S(2)}, u32[]{:S(2)}) collective-permute-start(bf16[1,4,21,256]{3,2,1,0:T(8,128)(2,1)S(1)} %get-tuple-element.25), channel_id=1, source_target_pairs={{4,0},{8,4},{12,8},{0,12},{5,1},{9,5},{13,9},{1,13},{6,2},{10,6},{... | collective-permute-start | bytes 129032 | tf_op jit(solution)/shard_map/ppermute | solution.py:37
  80.6 6.1 %collective-permute-start.12 = (bf16[1,1,128,256]{3,2,1,0:T(8,128)(2,1)S(1)}, bf16[1,1,128,256]{3,2,1,0:T(8,128)(2,1)S(1)}, u32[]{:S(2)}, u32[]{:S(2)}) collective-permute-start(bf16[1,1,128,256]{3,2,1,0:T(8,128)(2,1)S(1)} %get-tuple-element.22), channel_id=1, source_target_pairs={{12,0},{0,4},{4,8},{8,12},{13,1},{1,5},{5,9},{9,13},{14,2},{2,6},{... | collective-permute-start | bytes 196616 | tf_op jit(solution)/shard_map/ppermute | solution.py:37
  80.7 6.1 %collective-permute-start.13 = (bf16[1,1,128,256]{3,2,1,0:T(8,128)(2,1)S(1)}, bf16[1,1,128,256]{3,2,1,0:T(8,128)(2,1)S(1)}, u32[]{:S(2)}, u32[]{:S(2)}) collective-permute-start(bf16[1,1,128,256]{3,2,1,0:T(8,128)(2,1)S(1)} %get-tuple-element.23), channel_id=1, source_target_pairs={{4,0},{8,4},{12,8},{0,12},{5,1},{9,5},{13,9},{1,13},{6,2},{10,6},{... | collective-permute-start | bytes 196616 | tf_op jit(solution)/shard_map/ppermute | solution.py:37
  177.0 1.7 copy-start.4
  177.0 2.4 %copy-start.5 = (f32[256,256]{1,0:T(8,128)S(1)}, f32[256,256]{1,0:T(8,128)}, u32[]{:S(2)}) copy-start(f32[256,256]{1,0:T(8,128)} %get-tuple-element.13) | copy-start | bytes 786436
  178.7 1.3 copy-start.6
  179.4 1.3 copy-start.2
  186.2 1.0 copy-start.3
  (9 other events, 7.8 us)
Sparse Core Ops, SparseCore 0:
  80.7 96.2 all-reduce.8
where the time goes:
time: 196 us; the launch traced here: 195 us
  waiting for transfers between devices  95.9 us (49%)
  starting transfers between devices  28.6 us (15%)
  local copies, waits for them, and re-layouts  19.7 us (10%)
  matrix products  18.4 us (9%)
  between operations  18.1 us (9%)
  other arithmetic  15 us (8%)
    psum x1, waiting for transfers between devices, on_device(): lax.psum((message_term, weight_terms[0], weight_terms[1], weight_terms[2]...  89.5 us
    ppermute x12, starting transfers between devices, passed_along(): return lax.ppermute(block, axis, route)  24.7 us
    unnamed x36, local copies, waits for them, and re-layouts  6.42 us
    reduce_sum x1, other arithmetic, on_device(): jnp.sum(jnp.where(targets[..., None] == slot_ids, positions[None, :, None...  4.57 us
    reduce_sum x5, other arithmetic, on_device(): jnp.sum(matrix * matrix)  4.34 us
    ppermute x12, waiting for transfers between devices, passed_along(): return lax.ppermute(block, axis, route)  4.01 us
  transfers between devices with their start and end apart: 15, of which 5 were waited for; matrix products, arithmetic and copies ran while one was open for 4% of the time, Pallas kernels for 0%

commit v1 on v0

v1 whole, which is shorter than its diff:
```python
import math

import jax
import jax.numpy as jnp
from jax import lax
from jax.experimental import pallas as pl
from jax.experimental.pallas import tpu as pltpu
from jax.sharding import PartitionSpec as P

HEADS = 8
BLOCK = 128
NBRS = 4
JET_DEV = 4
LOW = jnp.bfloat16
FULL = jnp.float32
VMEM = pl.BlockSpec(memory_space=pltpu.VMEM)
SMEM = pl.BlockSpec(memory_space=pltpu.SMEM)


def call(body, outs, scalars, arrays, scratch=()):
    return pl.pallas_call(
        body,
        out_shape=[jax.ShapeDtypeStruct(shape, dtype) for shape, dtype in outs],
        in_specs=[SMEM] * len(scalars) + [VMEM] * len(arrays),
        out_specs=[VMEM] * len(outs),
        scratch_shapes=list(scratch),
    )(*scalars, *arrays)


def shifted(block, axis, distance):
    count = lax.axis_size(axis)
    return lax.ppermute(block, axis, [((i - distance) % count, i) for i in range(count)])


def swapped(block, axis, mask):
    return lax.ppermute(block, axis, [(i, i ^ mask) for i in range(lax.axis_size(axis))])


def mm(a, b):
    return lax.dot_general(a, b, (((1,), (0,)), ((), ())), preferred_element_type=FULL)


def mm_nt(a, b):
    return lax.dot_general(a, b, (((1,), (1,)), ((), ())), preferred_element_type=FULL)


def mm_tn(a, b):
    return lax.dot_general(a, b, (((0,), (0,)), ((), ())), preferred_element_type=FULL)


def iota(shape, dim):
    return lax.broadcasted_iota(jnp.int32, shape, dim)


class Plan:
    def __init__(self, sectors, per_device, members_dev, channels):
        self.sectors, self.cells, self.members, self.channels = sectors, per_device, members_dev, channels
        self.blocks = per_device // BLOCK
        self.radius = min(4, (sectors - 1) // 2)
        self.window = 2 * self.radius + 1
        self.cap = max(2, 2 * members_dev // (JET_DEV * self.window))
        self.used = JET_DEV * self.cap
        self.chunk = -(-(self.used + 1) // 16) * 16
        self.slots = -(-self.window * self.cap // 64) * 64
        self.owned = JET_DEV * self.slots


def index_kernel(plan, where_ref, cell_ref, jet_ref, cot_ref, pick_ref, place_ref, *chunk_refs):
    sector = where_ref[0]
    count, members = plan.chunk, plan.members
    jets = jet_ref[...]
    owner = lax.shift_right_logical(jets, 2)
    offset = owner - sector + plan.radius
    offset = jnp.where(offset < 0, offset + plan.sectors, offset)
    offset = jnp.where(offset >= plan.sectors, offset - plan.sectors, offset)
    inner = lax.bitwise_and(jets, 3)
    row = (offset * JET_DEV + inner).astype(FULL)
    rows, cols = iota((members, members), 0), iota((members, members), 1)
    column = jnp.sum(jnp.where(rows == cols, row, 0.0), axis=1, keepdims=True)
    earlier = jnp.where((column == row) & (rows < cols), 1.0, 0.0)
    rank = jnp.sum(earlier, axis=0, keepdims=True)
    target = offset * count + inner * plan.cap + rank.astype(jnp.int32)
    total = plan.window * count
    slot_hot = jnp.where(iota((total, members), 0) == target, 1.0, 0.0).astype(LOW)
    cell_hot = jnp.where(iota((plan.cells, members), 0) == cell_ref[...], 1.0, 0.0).astype(LOW)
    pick = mm_nt(slot_hot, cell_hot).astype(LOW)
    pick_ref[...] = pick
    place_ref[...] = mm_nt(cell_hot, slot_hot).astype(LOW)
    ones = jnp.ones((8, members), LOW)
    wide = iota((plan.channels, members), 0)
    mask_row = iota((count, plan.channels), 0) == plan.used
    chosen = mm(pick, cot_ref[...])
    for w in range(plan.window):
        hot = jnp.where((wide + w * count == target) & (wide < count), 1.0, 0.0).astype(LOW)
        present = mm_nt(ones, hot)[0:1, :]
        part = chosen[w * count : (w + 1) * count, :]
        chunk_refs[w][...] = jnp.where(mask_row, present, part).astype(LOW)


def hidden_kernel(plan, nbr_ref, cell_ref, low_ref, high_ref, weight_ref, pick_ref, gathered_ref, before_ref, hidden_ref, *chunk_refs):
    blocks = plan.blocks
    entries = [low_ref[...].astype(FULL)]
    entries += [cell_ref[b * BLOCK : (b + 1) * BLOCK, :].astype(FULL) for b in range(blocks)]
    entries += [high_ref[...].astype(FULL)]
    for b in range(blocks):
        total = None
        for j, entry in enumerate(entries):
            times = sum((nbr_ref[b, k] == j).astype(FULL) for k in range(NBRS)) * (1.0 / NBRS)
            total = entry * times if total is None else total + entry * times
        gathered_ref[b * BLOCK : (b + 1) * BLOCK, :] = total.astype(LOW)
    before = mm(gathered_ref[...], weight_ref[...])
    before_ref[...] = before
    silu = before * (1.0 / (1.0 + jnp.exp(-before)))
    hidden = (cell_ref[...].astype(FULL) + silu).astype(LOW)
    hidden_ref[...] = hidden
    chosen = mm(pick_ref[...], hidden).astype(LOW)
    for w in range(plan.window):
        chunk_refs[w][...] = chosen[w * plan.chunk : (w + 1) * plan.chunk, :]


def attend_kernel(plan, *refs):
    window, count, slots, owned, channels = plan.window, plan.chunk, plan.slots, plan.owned, plan.channels
    feat_refs, cot_refs = refs[:window], refs[window : 2 * window]
    wq_ref, wk_ref, wv_ref, wo_ref = refs[2 * window : 2 * window + 4]
    back_refs = refs[2 * window + 4 : 3 * window + 4]
    term_ref, parts_ref = refs[3 * window + 4 :]
    head = channels // HEADS
    scale = 1.0 / math.sqrt(head)

    def seat(c, w):
        jet = sum((c >= t * plan.cap).astype(jnp.int32) for t in range(1, JET_DEV))
        return jnp.where(c < plan.used, c + jet * (slots - plan.cap) + w * plan.cap, -1)

    members = upstream = present = None
    base = plan.used // 16 * 16
    for w in range(window):
        hot = jnp.where(iota((owned, count), 0) == seat(iota((owned, count), 1), w), 1.0, 0.0)
        low = hot.astype(LOW)
        m, u = mm(low, feat_refs[w][...]), mm(low, cot_refs[w][...])
        tail = cot_refs[w][base : base + 16, :].astype(FULL)
        row = jnp.sum(jnp.where(iota(tail.shape, 0) == plan.used - base, tail, 0.0), axis=0, keepdims=True)
        p = jnp.sum(hot * row[:, :count], axis=1, keepdims=True)
        members = m if members is None else members + m
        upstream = u if upstream is None else upstream + u
        present = p if present is None else present + p
    members, upstream = members.astype(LOW), upstream.astype(LOW)
    queries = mm(members, wq_ref[...]).astype(LOW)
    keys = mm(members, wk_ref[...]).astype(LOW)
    vals = mm(members, wv_ref[...]).astype(LOW)
    grad_mix = mm_nt(upstream, wo_ref[...]).astype(LOW)
    lane = iota((1, channels), 1)
    head_of = [(lane >= h * head) & (lane < (h + 1) * head) for h in range(HEADS)]
    low_of = [jnp.where(h, 1.0, 0.0).astype(LOW) for h in head_of]

    def spread(block):
        return jnp.concatenate([block * low_of[h] for h in range(HEADS)], axis=0)

    def merged(wide):
        total = None
        for h in range(HEADS):
            part = jnp.where(head_of[h], wide[h * slots : (h + 1) * slots, :], 0.0)
            total = part if total is None else total + part
        return total

    mixture, grad_q, grad_k, grad_v = [], [], [], []
    for j in range(JET_DEV):
        span = slice(j * slots, (j + 1) * slots)
        q, k, v, g = queries[span], keys[span], vals[span], grad_mix[span]
        here = present[span] > 0.5
        q_wide, g_wide = spread(q), spread(g)
        scores = jnp.where(here, mm_nt(k, q_wide) * scale, -1e30)
        powers = jnp.exp(scores - jnp.max(scores, axis=0, keepdims=True))
        chances = powers * (1.0 / jnp.sum(powers, axis=0, keepdims=True))
        chances_low = chances.astype(LOW)
        grad_chances = mm_nt(v, g_wide)
        inner = jnp.sum(chances * grad_chances, axis=0, keepdims=True)
        grad_scores = (chances * (grad_chances - inner) * scale).astype(LOW)
        mixture.append(merged(mm_tn(chances_low, v)).astype(LOW))
        grad_q.append(merged(mm_tn(grad_scores, k)).astype(LOW))
        grad_k.append(mm(grad_scores, q_wide).astype(LOW))
        grad_v.append(mm(chances_low, g_wide).astype(LOW))
    mixture, grad_q, grad_k, grad_v = [jnp.concatenate(x, axis=0) for x in (mixture, grad_q, grad_k, grad_v)]
    attended = mm(mixture, wo_ref[...]).astype(LOW)
    grad_members = mm_nt(grad_q, wq_ref[...]) + mm_nt(grad_k, wk_ref[...]) + mm_nt(grad_v, wv_ref[...])
    grad_members = grad_members.astype(LOW)
    for w in range(window):
        hot = jnp.where(seat(iota((count, owned), 0), w) == iota((count, owned), 1), 1.0, 0.0).astype(LOW)
        back_refs[w][:count, :] = mm(hot, attended).astype(LOW)
        back_refs[w][count:, :] = mm(hot, grad_members).astype(LOW)
    parts_ref[0] = members
    parts_ref[1] = upstream
    parts_ref[2] = mixture
    parts_ref[3] = grad_q
    parts_ref[4] = grad_k
    parts_ref[5] = grad_v
    members_t, mixture_t = members.T, mixture.T
    term_ref[0:channels] = mm(members_t, grad_q)
    term_ref[channels : 2 * channels] = mm(members_t, grad_k)
    term_ref[2 * channels : 3 * channels] = mm(members_t, grad_v)
    term_ref[3 * channels :] = mm(mixture_t, upstream)


def return_kernel(plan, nbr_ref, *refs):
    window, count = plan.window, plan.chunk
    back_refs = refs[:window]
    place_ref, hidden_ref, cot_ref, before_ref, gathered_ref, weight_ref = refs[window : window + 6]
    out_ref, kept_ref, first_ref, last_ref, term_ref, rows_ref = refs[window + 6 :]
    place = place_ref[...]
    for w in range(window):
        rows_ref[0, w * count : (w + 1) * count, :] = back_refs[w][:count, :]
        rows_ref[1, w * count : (w + 1) * count, :] = back_refs[w][count:, :]
    out_ref[...] = (hidden_ref[...].astype(FULL) + mm(place, rows_ref[0])).astype(LOW)
    grad_hidden = cot_ref[...].astype(FULL) + mm(place, rows_ref[1])
    before = before_ref[...]
    sigmoid = 1.0 / (1.0 + jnp.exp(-before))
    slope = sigmoid * (1.0 + before * (1.0 - sigmoid))
    grad_before = (grad_hidden * slope).astype(LOW)
    grad_gathered = mm_nt(grad_before, weight_ref[...]).astype(LOW).astype(FULL)

    def extended(j):
        total = None
        for b in range(plan.blocks):
            times = sum((nbr_ref[b, k] == j).astype(FULL) for k in range(NBRS)) * (1.0 / NBRS)
            part = grad_gathered[b * BLOCK : (b + 1) * BLOCK, :] * times
            total = part if total is None else total + part
        return total.astype(LOW)

    first_ref[...] = extended(0)
    last_ref[...] = extended(plan.blocks + 1)
    for b in range(plan.blocks):
        span = slice(b * BLOCK, (b + 1) * BLOCK)
        kept_ref[span, :] = grad_hidden[span] + extended(b + 1).astype(FULL)
    term_ref[...] = mm_tn(gathered_ref[...], grad_before)


def edges_kernel(plan, kept_ref, low_ref, high_ref, out_ref):
    last = plan.cells - BLOCK
    if last:
        out_ref[:BLOCK, :] = (kept_ref[:BLOCK, :] + low_ref[...].astype(FULL)).astype(LOW)
        if last > BLOCK:
            out_ref[BLOCK:last, :] = kept_ref[BLOCK:last, :].astype(LOW)
        out_ref[last:, :] = (kept_ref[last:, :] + high_ref[...].astype(FULL)).astype(LOW)
    else:
        out_ref[...] = (kept_ref[...] + low_ref[...].astype(FULL) + high_ref[...].astype(FULL)).astype(LOW)


def halve_kernel(kept_ref, came_ref, bit_ref, send_ref, keep_ref, total_ref):
    half = kept_ref.shape[0] // 2
    total_ref[0] = kept_ref[:half, :] + came_ref[:half, :].astype(FULL)
    total_ref[1] = kept_ref[half:, :] + came_ref[half:, :].astype(FULL)
    bit = bit_ref[0]
    keep_ref[...] = total_ref[bit]
    send_ref[...] = total_ref[1 - bit].astype(LOW)


def scale_kernel(channels, total_ref, *out_refs):
    bound = math.sqrt(5.0) * channels
    squares = jnp.zeros((1, 1), FULL)
    for t in range(5):
        part = total_ref[t * channels : (t + 1) * channels, :].astype(FULL)
        squares = squares + jnp.sum(jnp.sum(part * part, axis=0, keepdims=True), axis=1, keepdims=True)
    factor = bound / jnp.maximum(jnp.sqrt(squares), bound)
    for t in range(5):
        out_refs[t][...] = total_ref[t * channels : (t + 1) * channels, :].astype(FULL) * factor


def summed(terms):
    stages = []
    for axis in ("ev", "phi"):
        mask = 1
        while mask < lax.axis_size(axis):
            stages.append((axis, mask))
            mask *= 2
    bits = [(lax.axis_index(axis) & mask) // mask for axis, mask in stages]
    kept = terms
    for (axis, mask), bit in zip(stages, bits):
        half = kept.shape[0] // 2
        away = lax.dynamic_slice_in_dim(kept, (1 - bit) * half, half, 0).astype(LOW)
        kept = lax.dynamic_slice_in_dim(kept, bit * half, half, 0)
        kept = kept + swapped(away, axis, mask).astype(FULL)
    whole = kept.astype(LOW)
    for (axis, mask), bit in zip(reversed(stages), reversed(bits)):
        other = swapped(whole, axis, mask)
        whole = jnp.where(bit == 0, jnp.concatenate([whole, other], 0), jnp.concatenate([other, whole], 0))
    return whole


def on_device(cell_feats, neighbours, member_cell, member_jet, cotangent, message_weight, query_weight, key_weight, value_weight, output_weight):
    events, per_device, channels = cell_feats.shape
    assert events == 1
    members_dev = member_cell.shape[1]
    plan = Plan(lax.axis_size("phi"), per_device, members_dev, channels)
    window, chunk, radius = plan.window, plan.chunk, plan.radius
    place = lax.axis_index("phi").astype(jnp.int32).reshape(1)
    cells, cot, nbrs = cell_feats[0], cotangent[0], neighbours[0]
    low = shifted(cells[per_device - BLOCK :], "phi", 1)
    high = shifted(cells[:BLOCK], "phi", -1)
    total = window * chunk
    pick, put, *cot_chunks = call(
        lambda *refs: index_kernel(plan, *refs),
        [((total, per_device), LOW), ((per_device, total), LOW)] + [((chunk, channels), LOW)] * window,
        [place],
        [member_cell.reshape(1, members_dev), member_jet.reshape(1, members_dev), cot],
    )
    gathered, before, hidden, *chunks = call(
        lambda *refs: hidden_kernel(plan, *refs),
        [((per_device, channels), LOW), ((per_device, channels), FULL), ((per_device, channels), LOW)]
        + [((chunk, channels), LOW)] * window,
        [nbrs],
        [cells, low, high, message_weight, pick],
    )

    def sent(parts, sign):
        return [part if w == radius else shifted(part, "phi", sign * (w - radius)) for w, part in enumerate(parts)]

    feats = sent(chunks, 1)
    cots = sent(cot_chunks, 1)
    *backs, terms, _ = call(
        lambda *refs: attend_kernel(plan, *refs),
        [((2 * chunk, channels), LOW)] * window + [((4 * channels, channels), FULL), ((6, plan.owned, channels), LOW)],
        [],
        [*feats, *cots, query_weight, key_weight, value_weight, output_weight],
    )
    backs = sent(backs, -1)
    out_cells, kept, first, last, message_term = call(
        lambda *refs: return_kernel(plan, *refs),
        [((per_device, channels), LOW), ((per_device, channels), FULL), ((BLOCK, channels), LOW), ((BLOCK, channels), LOW), ((channels, channels), FULL)],
        [nbrs],
        [*backs, put, hidden, cot, before, gathered, message_weight],
        [pltpu.VMEM((2, total, channels), LOW)],
    )
    from_lower = shifted(last, "phi", 1)
    from_upper = shifted(first, "phi", -1)
    (grad_cells,) = call(
        lambda *refs: edges_kernel(plan, *refs), [((per_device, channels), LOW)], [], [kept, from_lower, from_upper]
    )
    whole = summed(jnp.concatenate([message_term, terms], axis=0))
    grads = call(lambda *refs: scale_kernel(channels, *refs), [((channels, channels), FULL)] * 5, [], [whole])
    return (out_cells[None], grad_cells[None], *grads)


def solution(mesh):
    cells = P(("groups", "ev"), "phi", None)
    flat = P(("groups", "ev"), "phi")
    weights = P("groups", None)
    return jax.shard_map(
        on_device,
        mesh=mesh,
        in_specs=(cells, cells, flat, cells, cells, P(), P(), P(), P(), P()),
        out_specs=(cells, cells, weights, weights, weights, weights, weights),
        check_vma=False,
    )
```

time: 196 us -> 87.1 us (0.44)
  waiting for transfers between devices: 95.9 us -> 34.9 us
  matrix products: 18.4 us -> 0 us
  between operations: 18.1 us -> 0.86 us
  Pallas kernels: 0 us -> 16.6 us
  local copies, waits for them, and re-layouts: 19.7 us -> 4.6 us
  other arithmetic: 15 us -> 1.4 us
    psum x1 -> x0, waiting for transfers between devices: 89.5 us -> none  [on_device(): lax.psum((message_term, weight_terms[0], weight_terms[1], weight_terms[2]...]
    ppermute x14 -> x18, waiting for transfers between devices: 6.29 us -> 34.9 us  [the longest x8 22.8 us: swapped(): lax.ppermute(block, axis, [(i, i ^ mask) for i in range(lax.axis_size(axi...]
    pallas_call x0 -> x6, Pallas kernels: none -> 16.6 us  [call(): pl.pallas_call(body, out_shape=[jax.ShapeDtypeStruct(shape, dtype) for sh...]
    dot_general x23 -> x0, matrix products: 15.8 us -> none  [the longest x1 2.88 us: attend_backward(): jnp.einsum('jnqk,jqnd->jknd', grad_scores, queries, preferred_element_typ...]
    reduce_sum x8 -> x0, other arithmetic: 9.1 us -> none  [the longest x1 4.57 us: on_device(): jnp.sum(jnp.where(targets[..., None] == slot_ids, positions[None, :, None...]
    gather x8 -> x0, local copies, waits for them, and re-layouts: 7.98 us -> none  [the longest x2 2.3 us: to_cells(): return jnp.take_along_axis(padded, holder_pick[..., None], axis=1)]
    mul x5 -> x0, other arithmetic: 3.6 us -> none  [the longest x1 0.72 us: on_device(): totals[1] * factor]
    reshape x11 -> x0, local copies, waits for them, and re-layouts: 3.23 us -> none  [the longest x3 1.21 us: project(): result.astype(jnp.bfloat16).reshape(jet_count, slot_count, HEADS, head_size)]
  transfers between devices with their start and end apart: 15 -> 18, of which waited for: 5 -> 12; matrix products, arithmetic and copies ran while one was open for 4% -> 0% of each run, Pallas kernels for 0% -> 7%
where the time goes in v1:
time: 87.1 us; the launch traced here: 86.7 us
  waiting for transfers between devices  34.9 us (40%)
  starting transfers between devices  28.4 us (33%)
  Pallas kernels  16.6 us (19%)
  local copies, waits for them, and re-layouts  4.6 us (5%)
  other arithmetic  1.4 us (2%)
    ppermute x8, waiting for transfers between devices, swapped(): lax.ppermute(block, axis, [(i, i ^ mask) for i in range(lax.axis_size(axi...  22.8 us
    ppermute x10, starting transfers between devices, shifted(): lax.ppermute(block, axis, [((i - distance) % count, i) for i in range(cou...  18.7 us
    pallas_call x6, Pallas kernels, call(): pl.pallas_call(body, out_shape=[jax.ShapeDtypeStruct(shape, dtype) for sh...  16.6 us
    ppermute x10, waiting for transfers between devices, shifted(): lax.ppermute(block, axis, [((i - distance) % count, i) for i in range(cou...  12.1 us
    ppermute x8, starting transfers between devices, swapped(): lax.ppermute(block, axis, [(i, i ^ mask) for i in range(lax.axis_size(axi...  9.68 us
    unnamed x27, local copies, waits for them, and re-layouts  3.54 us
  transfers between devices with their start and end apart: 18, of which 12 were waited for; matrix products, arithmetic and copies ran while one was open for 0% of the time, Pallas kernels for 7%

profile of v1, /device:TPU:0, one launch (start us, length us, event | category | flops | bytes accessed | tf_op | source)
XLA Modules:
  0.0 86.7 jit_solution(17099986296833399081)
XLA Ops:
  1.5 3.1 %collective-permute-start = (bf16[128,256]{1,0:T(8,128)(2,1)S(1)}, bf16[128,256]{1,0:T(8,128)(2,1)S(1)}, u32[]{:S(2)}, u32[]{:S(2)}) collective-permute-start(bf16[128,256]{1,0:T(8,128)(2,1)S(1)} %get-tuple-element.58), channel_id=1, source_target_pairs={{12,0},{0,4},{4,8},{8,12},{13,1},{1,5},{5,9},{9,13},{14,2},{2,6},{... | collective-permute-start | bytes 196616 | tf_op jit(solution)/shard_map/ppermute | solution.py:32
  4.6 2.1 %collective-permute-start.1 = (bf16[128,256]{1,0:T(8,128)(2,1)S(1)}, bf16[128,256]{1,0:T(8,128)(2,1)S(1)}, u32[]{:S(2)}, u32[]{:S(2)}) collective-permute-start(bf16[128,256]{1,0:T(8,128)(2,1)S(1)} %get-tuple-element.57), channel_id=1, source_target_pairs={{4,0},{8,4},{12,8},{0,12},{5,1},{9,5},{13,9},{1,13},{6,2},{10,6},{... | collective-permute-start | bytes 196616 | tf_op jit(solution)/shard_map/ppermute | solution.py:32
  6.7 2.0 %shard_map.153 = (bf16[288,256]{1,0:T(8,128)(2,1)}, bf16[256,288]{1,0:T(8,128)(2,1)}, bf16[96,256]{1,0:T(8,128)(2,1)}, bf16[96,256]{1,0:T(8,128)(2,1)}, bf16[96,256]{1,0:T(8,128)(2,1)}) custom-call(s32[1]{0:T(128)} %bitcast.4.refs_0_, s32[1,128]{1,0:T(1,128)} %refs_1_.1, s32[1,128]{1,0:T(1,128)} %bitcast.17, bf16[256,256]{1,0:T(8,128)(2,1)} %bitcast.11), custom_call_target="tpu_custom_call" | custom-call | tf_op jit(solution)/shard_map/pallas_call | solution.py:21
  8.7 2.0 %collective-permute-start.4 = (bf16[96,256]{1,0:T(8,128)(2,1)}, bf16[96,256]{1,0:T(8,128)(2,1)S(1)}, u32[]{:S(2)}, u32[]{:S(2)}) collective-permute-start(bf16[96,256]{1,0:T(8,128)(2,1)} %get-tuple-element.36), channel_id=1, source_target_pairs={{4,0},{8,4},{12,8},{0,12},{5,1},{9,5},{13,9},{1,13},{6,2},{10,6},{... | collective-permute-start | bytes 147464 | tf_op jit(solution)/shard_map/ppermute | solution.py:32
  11.4 2.2 %shard_map.154 = (bf16[256,256]{1,0:T(8,128)(2,1)}, f32[256,256]{1,0:T(8,128)}, bf16[256,256]{1,0:T(8,128)(2,1)}, bf16[96,256]{1,0:T(8,128)(2,1)}, bf16[96,256]{1,0:T(8,128)(2,1)}, /*index=5*/bf16[96,256]{1,0:T(8,128)(2,1)}) custom-call(s32[2,4]{1,0:T(2,128)} %bitcast.15, bf16[256,256]{1,0:T(8,128)(2,1)} %bitcast.13, bf16[128,256]{1,0:T(8,128)(2,1)} %copy-done.3, ...), custom_call_target="tpu_custom_call" | custom-call | tf_op jit(solution)/shard_map/pallas_call | solution.py:21
  13.6 3.8 %collective-permute-start.2 = (bf16[96,256]{1,0:T(8,128)(2,1)}, bf16[96,256]{1,0:T(8,128)(2,1)S(1)}, u32[]{:S(2)}, u32[]{:S(2)}) collective-permute-start(bf16[96,256]{1,0:T(8,128)(2,1)} %get-tuple-element.33), channel_id=1, source_target_pairs={{4,0},{8,4},{12,8},{0,12},{5,1},{9,5},{13,9},{1,13},{6,2},{10,6},{... | collective-permute-start | bytes 147464 | tf_op jit(solution)/shard_map/ppermute | solution.py:32
  17.4 2.0 %collective-permute-done.2.refs_0_ = bf16[96,256]{1,0:T(8,128)(2,1)S(1)} collective-permute-done((bf16[96,256]{1,0:T(8,128)(2,1)}, bf16[96,256]{1,0:T(8,128)(2,1)S(1)}, u32[]{:S(2)}, u32[]{:S(2)}) %collective-permute-start.2) | collective-permute-done | bytes 49184 | tf_op jit(solution)/shard_map/ppermute | solution.py:32
  19.4 4.0 %collective-permute-done.3.refs_2_ = bf16[96,256]{1,0:T(8,128)(2,1)S(1)} collective-permute-done((bf16[96,256]{1,0:T(8,128)(2,1)}, bf16[96,256]{1,0:T(8,128)(2,1)S(1)}, u32[]{:S(2)}, u32[]{:S(2)}) %collective-permute-start.3) | collective-permute-done | bytes 49184 | tf_op jit(solution)/shard_map/ppermute | solution.py:32
  24.1 5.7 %shard_map.155 = (bf16[192,256]{1,0:T(8,128)(2,1)}, bf16[192,256]{1,0:T(8,128)(2,1)}, bf16[192,256]{1,0:T(8,128)(2,1)}, f32[1024,256]{1,0:T(8,128)}, bf16[6,256,256]{2,1,0:T(8,128)(2,1)}) custom-call(bf16[96,256]{1,0:T(8,128)(2,1)} %copy-done.9, bf16[96,256]{1,0:T(8,128)(2,1)} %get-tuple-element.34.refs_1_, bf16[96,256]{1,0:T(8,128)(2,1)} %copy-done.10, ...), custom_call_target="tpu_custom_call" | custom-call | tf_op jit(solution)/shard_map/pallas_call | solution.py:21
  29.8 3.8 %collective-permute-start.7 = (bf16[192,256]{1,0:T(8,128)(2,1)}, bf16[192,256]{1,0:T(8,128)(2,1)S(1)}, u32[]{:S(2)}, u32[]{:S(2)}) collective-permute-start(bf16[192,256]{1,0:T(8,128)(2,1)} %get-tuple-element.41), channel_id=1, source_target_pairs={{4,0},{8,4},{12,8},{0,12},{5,1},{9,5},{13,9},{1,13},{6,2},{10,6},{... | collective-permute-start | bytes 294920 | tf_op jit(solution)/shard_map/ppermute | solution.py:32
  33.6 2.8 %collective-permute-done.6.refs_1_ = bf16[192,256]{1,0:T(8,128)(2,1)S(1)} collective-permute-done((bf16[192,256]{1,0:T(8,128)(2,1)}, bf16[192,256]{1,0:T(8,128)(2,1)S(1)}, u32[]{:S(2)}, u32[]{:S(2)}) %collective-permute-start.6) | collective-permute-done | bytes 98336 | tf_op jit(solution)/shard_map/ppermute | solution.py:32
  37.1 2.7 %shard_map.156 = (bf16[256,256]{1,0:T(8,128)(2,1)}, f32[256,256]{1,0:T(8,128)}, bf16[128,256]{1,0:T(8,128)(2,1)}, bf16[128,256]{1,0:T(8,128)(2,1)}, f32[256,256]{1,0:T(8,128)}) custom-call(s32[2,4]{1,0:T(2,128)} %bitcast.16, bf16[192,256]{1,0:T(8,128)(2,1)} %copy-done.1, bf16[192,256]{1,0:T(8,128)(2,1)} %get-tuple-element.40.refs_2_, ...), custom_call_target="tpu_custom_call" | custom-call | tf_op jit(solution)/shard_map/pallas_call | solution.py:21
  44.2 4.7 %collective-permute-done.11 = bf16[320,256]{1,0:T(8,128)(2,1)S(1)} collective-permute-done((bf16[320,256]{1,0:T(8,128)(2,1)S(1)}, bf16[320,256]{1,0:T(8,128)(2,1)S(1)}, u32[]{:S(2)}, u32[]{:S(2)}) %collective-permute-start.11) | collective-permute-done | bytes 163872 | tf_op jit(solution)/shard_map/ppermute | solution.py:36
  49.2 4.4 %collective-permute-done.12 = bf16[160,256]{1,0:T(8,128)(2,1)S(1)} collective-permute-done((bf16[160,256]{1,0:T(8,128)(2,1)S(1)}, bf16[160,256]{1,0:T(8,128)(2,1)S(1)}, u32[]{:S(2)}, u32[]{:S(2)}) %collective-permute-start.12) | collective-permute-done | bytes 81952 | tf_op jit(solution)/shard_map/ppermute | solution.py:36
  53.6 2.4 %collective-permute-start.13 = (bf16[80,256]{1,0:T(8,128)(2,1)S(1)}, bf16[80,256]{1,0:T(8,128)(2,1)S(1)}, u32[]{:S(2)}, u32[]{:S(2)}) collective-permute-start(bf16[80,256]{1,0:T(8,128)(2,1)S(1)} %dynamic-slice_convert_fusion.3), channel_id=1, source_target_pairs={{0,8},{4,12},{8,0},{12,4},{1,9},{5,13},{9,1},{13,5},{2,10},{6,14},... | collective-permute-start | bytes 122888 | tf_op jit(solution)/shard_map/ppermute | solution.py:36
  56.0 2.6 %collective-permute-done.13 = bf16[80,256]{1,0:T(8,128)(2,1)S(1)} collective-permute-done((bf16[80,256]{1,0:T(8,128)(2,1)S(1)}, bf16[80,256]{1,0:T(8,128)(2,1)S(1)}, u32[]{:S(2)}, u32[]{:S(2)}) %collective-permute-start.13) | collective-permute-done | bytes 40992 | tf_op jit(solution)/shard_map/ppermute | solution.py:36
  58.6 2.4 %collective-permute-start.14 = (bf16[80,256]{1,0:T(8,128)(2,1)S(1)}, bf16[80,256]{1,0:T(8,128)(2,1)S(1)}, u32[]{:S(2)}, u32[]{:S(2)}) collective-permute-start(bf16[80,256]{1,0:T(8,128)(2,1)S(1)} %add_convert_fusion), channel_id=1, source_target_pairs={{0,8},{4,12},{8,0},{12,4},{1,9},{5,13},{9,1},{13,5},{2,10},{6,14},... | collective-permute-start | bytes 122888 | tf_op jit(solution)/shard_map/ppermute | solution.py:36
  61.0 2.7 %collective-permute-done.14 = bf16[80,256]{1,0:T(8,128)(2,1)S(1)} collective-permute-done((bf16[80,256]{1,0:T(8,128)(2,1)S(1)}, bf16[80,256]{1,0:T(8,128)(2,1)S(1)}, u32[]{:S(2)}, u32[]{:S(2)}) %collective-permute-start.14) | collective-permute-done | bytes 40992 | tf_op jit(solution)/shard_map/ppermute | solution.py:36
  65.2 3.0 %collective-permute-done.15 = bf16[160,256]{1,0:T(8,128)(2,1)S(1)} collective-permute-done((bf16[160,256]{1,0:T(8,128)(2,1)S(1)}, bf16[160,256]{1,0:T(8,128)(2,1)S(1)}, u32[]{:S(2)}, u32[]{:S(2)}) %collective-permute-start.15) | collective-permute-done | bytes 81952 | tf_op jit(solution)/shard_map/ppermute | solution.py:36
  69.8 3.8 %collective-permute-done.16 = bf16[320,256]{1,0:T(8,128)(2,1)S(1)} collective-permute-done((bf16[320,256]{1,0:T(8,128)(2,1)S(1)}, bf16[320,256]{1,0:T(8,128)(2,1)S(1)}, u32[]{:S(2)}, u32[]{:S(2)}) %collective-permute-start.16) | collective-permute-done | bytes 163872 | tf_op jit(solution)/shard_map/ppermute | solution.py:36
  75.4 2.4 %collective-permute-start.9 = (bf16[128,256]{1,0:T(8,128)(2,1)S(1)}, bf16[128,256]{1,0:T(8,128)(2,1)S(1)}, u32[]{:S(2)}, u32[]{:S(2)}) collective-permute-start(bf16[128,256]{1,0:T(8,128)(2,1)S(1)} %copy-done.11), channel_id=1, source_target_pairs={{4,0},{8,4},{12,8},{0,12},{5,1},{9,5},{13,9},{1,13},{6,2},{10,6},{... | collective-permute-start | bytes 196616 | tf_op jit(solution)/shard_map/ppermute | solution.py:32
  77.8 2.8 %collective-permute-done.8.refs_1_ = bf16[128,256]{1,0:T(8,128)(2,1)S(1)} collective-permute-done((bf16[128,256]{1,0:T(8,128)(2,1)S(1)}, bf16[128,256]{1,0:T(8,128)(2,1)S(1)}, u32[]{:S(2)}, u32[]{:S(2)}) %collective-permute-start.8) | collective-permute-done | bytes 65568 | tf_op jit(solution)/shard_map/ppermute | solution.py:32
  81.7 1.7 %shard_map.157 = bf16[256,256]{1,0:T(8,128)(2,1)} custom-call(f32[256,256]{1,0:T(8,128)} %get-tuple-element.47.refs_0_, bf16[128,256]{1,0:T(8,128)(2,1)} %copy-done.5, bf16[128,256]{1,0:T(8,128)(2,1)} %copy-done.6), custom_call_target="tpu_custom_call" | custom-call | tf_op jit(solution)/shard_map/pallas_call | solution.py:21
  84.4 2.3 %shard_map.158 = (f32[256,256]{1,0:T(8,128)}, f32[256,256]{1,0:T(8,128)}, f32[256,256]{1,0:T(8,128)}, f32[256,256]{1,0:T(8,128)}, f32[256,256]{1,0:T(8,128)}) custom-call(bf16[1280,256]{1,0:T(8,128)(2,1)} %maximum_select_fusion.refs_0_), custom_call_target="tpu_custom_call" | custom-call | tf_op jit(solution)/shard_map/pallas_call | solution.py:21
  (59 shorter events, 14.6 us)
Async XLA Ops:
  1.5 9.2 %collective-permute-start = (bf16[128,256]{1,0:T(8,128)(2,1)S(1)}, bf16[128,256]{1,0:T(8,128)(2,1)S(1)}, u32[]{:S(2)}, u32[]{:S(2)}) collective-permute-start(bf16[128,256]{1,0:T(8,128)(2,1)S(1)} %get-tuple-element.58), channel_id=1, source_target_pairs={{12,0},{0,4},{4,8},{8,12},{13,1},{1,5},{5,9},{9,13},{14,2},{2,6},{... | collective-permute-start | bytes 196616 | tf_op jit(solution)/shard_map/ppermute | solution.py:32
  4.6 6.2 %collective-permute-start.1 = (bf16[128,256]{1,0:T(8,128)(2,1)S(1)}, bf16[128,256]{1,0:T(8,128)(2,1)S(1)}, u32[]{:S(2)}, u32[]{:S(2)}) collective-permute-start(bf16[128,256]{1,0:T(8,128)(2,1)S(1)} %get-tuple-element.57), channel_id=1, source_target_pairs={{4,0},{8,4},{12,8},{0,12},{5,1},{9,5},{13,9},{1,13},{6,2},{10,6},{... | collective-permute-start | bytes 196616 | tf_op jit(solution)/shard_map/ppermute | solution.py:32
  8.7 8.6 %collective-permute-start.4 = (bf16[96,256]{1,0:T(8,128)(2,1)}, bf16[96,256]{1,0:T(8,128)(2,1)S(1)}, u32[]{:S(2)}, u32[]{:S(2)}) collective-permute-start(bf16[96,256]{1,0:T(8,128)(2,1)} %get-tuple-element.36), channel_id=1, source_target_pairs={{4,0},{8,4},{12,8},{0,12},{5,1},{9,5},{13,9},{1,13},{6,2},{10,6},{... | collective-permute-start | bytes 147464 | tf_op jit(solution)/shard_map/ppermute | solution.py:32
  10.7 6.7 %collective-permute-start.5 = (bf16[96,256]{1,0:T(8,128)(2,1)}, bf16[96,256]{1,0:T(8,128)(2,1)S(1)}, u32[]{:S(2)}, u32[]{:S(2)}) collective-permute-start(bf16[96,256]{1,0:T(8,128)(2,1)} %get-tuple-element.38), channel_id=1, source_target_pairs={{12,0},{0,4},{4,8},{8,12},{13,1},{1,5},{5,9},{9,13},{14,2},{2,6},{... | collective-permute-start | bytes 147464 | tf_op jit(solution)/shard_map/ppermute | solution.py:32
  13.6 5.8 %collective-permute-start.2 = (bf16[96,256]{1,0:T(8,128)(2,1)}, bf16[96,256]{1,0:T(8,128)(2,1)S(1)}, u32[]{:S(2)}, u32[]{:S(2)}) collective-permute-start(bf16[96,256]{1,0:T(8,128)(2,1)} %get-tuple-element.33), channel_id=1, source_target_pairs={{4,0},{8,4},{12,8},{0,12},{5,1},{9,5},{13,9},{1,13},{6,2},{10,6},{... | collective-permute-start | bytes 147464 | tf_op jit(solution)/shard_map/ppermute | solution.py:32
  17.3 6.1 %collective-permute-start.3 = (bf16[96,256]{1,0:T(8,128)(2,1)}, bf16[96,256]{1,0:T(8,128)(2,1)S(1)}, u32[]{:S(2)}, u32[]{:S(2)}) collective-permute-start(bf16[96,256]{1,0:T(8,128)(2,1)} %get-tuple-element.35), channel_id=1, source_target_pairs={{12,0},{0,4},{4,8},{8,12},{13,1},{1,5},{5,9},{9,13},{14,2},{2,6},{... | collective-permute-start | bytes 147464 | tf_op jit(solution)/shard_map/ppermute | solution.py:32
  17.3 6.1 %copy-start.7 = (bf16[96,256]{1,0:T(8,128)(2,1)}, bf16[96,256]{1,0:T(8,128)(2,1)S(1)}, u32[]{:S(2)}) copy-start(bf16[96,256]{1,0:T(8,128)(2,1)S(1)} %collective-permute-done.4.refs_3_) | copy-start | bytes 147460
  17.4 6.1 %copy-start.8 = (bf16[96,256]{1,0:T(8,128)(2,1)}, bf16[96,256]{1,0:T(8,128)(2,1)S(1)}, u32[]{:S(2)}) copy-start(bf16[96,256]{1,0:T(8,128)(2,1)S(1)} %collective-permute-done.5.refs_5_) | copy-start | bytes 147460
  19.4 4.0 %copy-start.9 = (bf16[96,256]{1,0:T(8,128)(2,1)}, bf16[96,256]{1,0:T(8,128)(2,1)S(1)}, u32[]{:S(2)}) copy-start(bf16[96,256]{1,0:T(8,128)(2,1)S(1)} %collective-permute-done.2.refs_0_) | copy-start | bytes 147460
  29.8 10.9 %copy-start = (f32[1024,256]{1,0:T(8,128)S(1)}, f32[1024,256]{1,0:T(8,128)}, u32[]{:S(2)}) copy-start(f32[1024,256]{1,0:T(8,128)} %get-tuple-element.51) | copy-start | bytes 3145732
  29.8 6.6 %collective-permute-start.6 = (bf16[192,256]{1,0:T(8,128)(2,1)}, bf16[192,256]{1,0:T(8,128)(2,1)S(1)}, u32[]{:S(2)}, u32[]{:S(2)}) collective-permute-start(bf16[192,256]{1,0:T(8,128)(2,1)} %get-tuple-element.39), channel_id=1, source_target_pairs={{12,0},{0,4},{4,8},{8,12},{13,1},{1,5},{5,9},{9,13},{14,2},{2,6},{... | collective-permute-start | bytes 294920 | tf_op jit(solution)/shard_map/ppermute | solution.py:32
  29.8 6.6 %collective-permute-start.7 = (bf16[192,256]{1,0:T(8,128)(2,1)}, bf16[192,256]{1,0:T(8,128)(2,1)S(1)}, u32[]{:S(2)}, u32[]{:S(2)}) collective-permute-start(bf16[192,256]{1,0:T(8,128)(2,1)} %get-tuple-element.41), channel_id=1, source_target_pairs={{4,0},{8,4},{12,8},{0,12},{5,1},{9,5},{13,9},{1,13},{6,2},{10,6},{... | collective-permute-start | bytes 294920 | tf_op jit(solution)/shard_map/ppermute | solution.py:32
  40.9 1.7 %collective-permute-start.10 = (bf16[640,256]{1,0:T(8,128)(2,1)S(1)}, bf16[640,256]{1,0:T(8,128)(2,1)S(1)}, u32[]{:S(2)}, u32[]{:S(2)}) collective-permute-start(bf16[640,256]{1,0:T(8,128)(2,1)S(1)} %dynamic-slice_convert_fusion), channel_id=1, source_target_pairs={{0,1},{1,0},{2,3},{3,2},{4,5},{5,4},{6,7},{7,6},{8,9},{9,8},{10,11... | collective-permute-start | bytes 983048 | tf_op jit(solution)/shard_map/ppermute | solution.py:36
  42.7 6.3 %collective-permute-start.11 = (bf16[320,256]{1,0:T(8,128)(2,1)S(1)}, bf16[320,256]{1,0:T(8,128)(2,1)S(1)}, u32[]{:S(2)}, u32[]{:S(2)}) collective-permute-start(bf16[320,256]{1,0:T(8,128)(2,1)S(1)} %dynamic-slice_convert_fusion.1), channel_id=1, source_target_pairs={{0,2},{1,3},{2,0},{3,1},{4,6},{5,7},{6,4},{7,5},{8,10},{9,11},{10,... | collective-permute-start | bytes 491528 | tf_op jit(solution)/shard_map/ppermute | solution.py:36
  44.2 29.6 %copy-start.12 = (bf16[128,256]{1,0:T(8,128)(2,1)S(1)}, bf16[128,256]{1,0:T(8,128)(2,1)}, u32[]{:S(2)}) copy-start(bf16[128,256]{1,0:T(8,128)(2,1)} %get-tuple-element.48) | copy-start | bytes 196612
  44.2 31.1 %copy-start.11 = (bf16[128,256]{1,0:T(8,128)(2,1)S(1)}, bf16[128,256]{1,0:T(8,128)(2,1)}, u32[]{:S(2)}) copy-start(bf16[128,256]{1,0:T(8,128)(2,1)} %get-tuple-element.49) | copy-start | bytes 196612
  49.1 4.5 %collective-permute-start.12 = (bf16[160,256]{1,0:T(8,128)(2,1)S(1)}, bf16[160,256]{1,0:T(8,128)(2,1)S(1)}, u32[]{:S(2)}, u32[]{:S(2)}) collective-permute-start(bf16[160,256]{1,0:T(8,128)(2,1)S(1)} %dynamic-slice_convert_fusion.2), channel_id=1, source_target_pairs={{0,4},{4,0},{8,12},{12,8},{1,5},{5,1},{9,13},{13,9},{2,6},{6,2},{1... | collective-permute-start | bytes 245768 | tf_op jit(solution)/shard_map/ppermute | solution.py:36
  53.6 5.0 %collective-permute-start.13 = (bf16[80,256]{1,0:T(8,128)(2,1)S(1)}, bf16[80,256]{1,0:T(8,128)(2,1)S(1)}, u32[]{:S(2)}, u32[]{:S(2)}) collective-permute-start(bf16[80,256]{1,0:T(8,128)(2,1)S(1)} %dynamic-slice_convert_fusion.3), channel_id=1, source_target_pairs={{0,8},{4,12},{8,0},{12,4},{1,9},{5,13},{9,1},{13,5},{2,10},{6,14},... | collective-permute-start | bytes 122888 | tf_op jit(solution)/shard_map/ppermute | solution.py:36
  58.6 5.1 %collective-permute-start.14 = (bf16[80,256]{1,0:T(8,128)(2,1)S(1)}, bf16[80,256]{1,0:T(8,128)(2,1)S(1)}, u32[]{:S(2)}, u32[]{:S(2)}) collective-permute-start(bf16[80,256]{1,0:T(8,128)(2,1)S(1)} %add_convert_fusion), channel_id=1, source_target_pairs={{0,8},{4,12},{8,0},{12,4},{1,9},{5,13},{9,1},{13,5},{2,10},{6,14},... | collective-permute-start | bytes 122888 | tf_op jit(solution)/shard_map/ppermute | solution.py:36
  63.7 4.5 %collective-permute-start.15 = (bf16[160,256]{1,0:T(8,128)(2,1)S(1)}, bf16[160,256]{1,0:T(8,128)(2,1)S(1)}, u32[]{:S(2)}, u32[]{:S(2)}) collective-permute-start(bf16[160,256]{1,0:T(8,128)(2,1)S(1)} %maximum_select_fusion.3), channel_id=1, source_target_pairs={{0,4},{4,0},{8,12},{12,8},{1,5},{5,1},{9,13},{13,9},{2,6},{6,2},{1... | collective-permute-start | bytes 245768 | tf_op jit(solution)/shard_map/ppermute | solution.py:36
  68.2 5.4 %collective-permute-start.16 = (bf16[320,256]{1,0:T(8,128)(2,1)S(1)}, bf16[320,256]{1,0:T(8,128)(2,1)S(1)}, u32[]{:S(2)}, u32[]{:S(2)}) collective-permute-start(bf16[320,256]{1,0:T(8,128)(2,1)S(1)} %maximum_select_fusion.2), channel_id=1, source_target_pairs={{0,2},{1,3},{2,0},{3,1},{4,6},{5,7},{6,4},{7,5},{8,10},{9,11},{10,... | collective-permute-start | bytes 491528 | tf_op jit(solution)/shard_map/ppermute | solution.py:36
  73.7 9.6 %collective-permute-start.17 = (bf16[640,256]{1,0:T(8,128)(2,1)S(1)}, bf16[640,256]{1,0:T(8,128)(2,1)S(1)}, u32[]{:S(2)}, u32[]{:S(2)}) collective-permute-start(bf16[640,256]{1,0:T(8,128)(2,1)S(1)} %maximum_select_fusion.1), channel_id=1, source_target_pairs={{0,1},{1,0},{2,3},{3,2},{4,5},{5,4},{6,7},{7,6},{8,9},{9,8},{10,11... | collective-permute-start | bytes 983048 | tf_op jit(solution)/shard_map/ppermute | solution.py:36
  73.8 6.7 %collective-permute-start.8 = (bf16[128,256]{1,0:T(8,128)(2,1)S(1)}, bf16[128,256]{1,0:T(8,128)(2,1)S(1)}, u32[]{:S(2)}, u32[]{:S(2)}) collective-permute-start(bf16[128,256]{1,0:T(8,128)(2,1)S(1)} %copy-done.12), channel_id=1, source_target_pairs={{12,0},{0,4},{4,8},{8,12},{13,1},{1,5},{5,9},{9,13},{14,2},{2,6},{... | collective-permute-start | bytes 196616 | tf_op jit(solution)/shard_map/ppermute | solution.py:32
  75.4 5.7 %collective-permute-start.9 = (bf16[128,256]{1,0:T(8,128)(2,1)S(1)}, bf16[128,256]{1,0:T(8,128)(2,1)S(1)}, u32[]{:S(2)}, u32[]{:S(2)}) collective-permute-start(bf16[128,256]{1,0:T(8,128)(2,1)S(1)} %copy-done.11), channel_id=1, source_target_pairs={{4,0},{8,4},{12,8},{0,12},{5,1},{9,5},{13,9},{1,13},{6,2},{10,6},{... | collective-permute-start | bytes 196616 | tf_op jit(solution)/shard_map/ppermute | solution.py:32
  (7 other events, 4.5 us)

commit v2 on v1

--- a/solution.py
+++ b/solution.py
@@ -17,14 +17,15 @@
 SMEM = pl.BlockSpec(memory_space=pltpu.SMEM)
 
 
-def call(body, outs, scalars, arrays, scratch=()):
+def call(body, outs, scalars, arrays, scratch=(), final=False):
+    kind = jax.ShapeDtypeStruct if final else pltpu.VMEM
     return pl.pallas_call(
         body,
-        out_shape=[jax.ShapeDtypeStruct(shape, dtype) for shape, dtype in outs],
+        out_shape=[kind(shape, dtype) for shape, dtype in outs],
         in_specs=[SMEM] * len(scalars) + [VMEM] * len(arrays),
         out_specs=[VMEM] * len(outs),
         scratch_shapes=list(scratch),
-    )(*scalars, *arrays)
+    )(*scalars, *[pltpu.with_memory_space_constraint(x, pltpu.VMEM) for x in arrays])
 
 
 def shifted(block, axis, distance):
@@ -123,7 +124,7 @@
     feat_refs, cot_refs = refs[:window], refs[window : 2 * window]
     wq_ref, wk_ref, wv_ref, wo_ref = refs[2 * window : 2 * window + 4]
     back_refs = refs[2 * window + 4 : 3 * window + 4]
-    term_ref, parts_ref = refs[3 * window + 4 :]
+    (parts_ref,) = refs[3 * window + 4 :]
     head = channels // HEADS
     scale = 1.0 / math.sqrt(head)
 
@@ -193,18 +194,23 @@
     parts_ref[3] = grad_q
     parts_ref[4] = grad_k
     parts_ref[5] = grad_v
-    members_t, mixture_t = members.T, mixture.T
-    term_ref[0:channels] = mm(members_t, grad_q)
-    term_ref[channels : 2 * channels] = mm(members_t, grad_k)
-    term_ref[2 * channels : 3 * channels] = mm(members_t, grad_v)
-    term_ref[3 * channels :] = mm(mixture_t, upstream)
-
-
-def return_kernel(plan, nbr_ref, *refs):
+
+
+def term_kernel(channels, bit_ref, parts_ref, send_ref, keep_ref):
+    bit = bit_ref[0]
+    for half, ref in ((1 - bit, send_ref), (bit, keep_ref)):
+        for t in range(2):
+            term = 2 * half + t
+            left = parts_ref[jnp.where(term == 3, 2, 0)]
+            right = parts_ref[jnp.where(term == 3, 1, 3 + term)]
+            ref[t * channels : (t + 1) * channels, :] = mm_tn(left, right).astype(ref.dtype)
+
+
+def return_kernel(plan, nbr_ref, bit_ref, *refs):
     window, count = plan.window, plan.chunk
     back_refs = refs[:window]
     place_ref, hidden_ref, cot_ref, before_ref, gathered_ref, weight_ref = refs[window : window + 6]
-    out_ref, kept_ref, first_ref, last_ref, term_ref, rows_ref = refs[window + 6 :]
+    out_ref, kept_ref, first_ref, last_ref, send_ref, keep_ref, rows_ref, term_ref = refs[window + 6 :]
     place = place_ref[...]
     for w in range(window):
         rows_ref[0, w * count : (w + 1) * count, :] = back_refs[w][:count, :]
@@ -230,7 +236,10 @@
     for b in range(plan.blocks):
         span = slice(b * BLOCK, (b + 1) * BLOCK)
         kept_ref[span, :] = grad_hidden[span] + extended(b + 1).astype(FULL)
-    term_ref[...] = mm_tn(gathered_ref[...], grad_before)
+    half = plan.channels // 2
+    term_ref[...] = mm_tn(gathered_ref[...], grad_before).reshape(2, half, plan.channels)
+    send_ref[...] = term_ref[1 - bit_ref[0]].astype(LOW)
+    keep_ref[...] = term_ref[bit_ref[0]]
 
 
 def edges_kernel(plan, kept_ref, low_ref, high_ref, out_ref):
@@ -244,24 +253,67 @@
         out_ref[...] = (kept_ref[...] + low_ref[...].astype(FULL) + high_ref[...].astype(FULL)).astype(LOW)
 
 
-def halve_kernel(kept_ref, came_ref, bit_ref, send_ref, keep_ref, total_ref):
+def rows_of(ref, at, count):
+    return ref[pl.ds(pl.multiple_of(at * count, count), count), :]
+
+
+def halve_kernel(bit_ref, kept_ref, came_ref, send_ref, keep_ref):
     half = kept_ref.shape[0] // 2
-    total_ref[0] = kept_ref[:half, :] + came_ref[:half, :].astype(FULL)
-    total_ref[1] = kept_ref[half:, :] + came_ref[half:, :].astype(FULL)
     bit = bit_ref[0]
-    keep_ref[...] = total_ref[bit]
-    send_ref[...] = total_ref[1 - bit].astype(LOW)
-
-
-def scale_kernel(channels, total_ref, *out_refs):
+    keep_ref[...] = rows_of(kept_ref, bit, half) + rows_of(came_ref, bit, half).astype(FULL)
+    send_ref[...] = (rows_of(kept_ref, 1 - bit, half) + rows_of(came_ref, 1 - bit, half).astype(FULL)).astype(LOW)
+
+
+def quarter_kernel(place_ref, kept_ref, came_ref, keep_ref, *send_refs):
+    size = kept_ref.shape[0] // 4
+    for mask in range(4):
+        at = lax.bitwise_xor(place_ref[0], mask)
+        part = rows_of(kept_ref, at, size) + rows_of(came_ref, at, size).astype(FULL)
+        if mask:
+            send_refs[mask - 1][...] = part.astype(LOW)
+        else:
+            keep_ref[...] = part
+
+
+def add_kernel(*refs):
+    total = refs[0][...].astype(FULL)
+    for ref in refs[1:-1]:
+        total = total + ref[...].astype(FULL)
+    refs[-1][...] = total.astype(LOW)
+
+
+def join_kernel(place_ref, *refs):
+    out_ref = refs[-1]
+    size = refs[0].shape[0]
+    for mask, ref in enumerate(refs[:-1]):
+        at = lax.bitwise_xor(place_ref[0], mask)
+        out_ref[pl.ds(pl.multiple_of(at * size, size), size), :] = ref[...]
+
+
+def joined_kernel(bit_ref, own_ref, came_ref, term_a_ref, term_b_ref, out_ref):
+    size = own_ref.shape[0]
+    bit = bit_ref[0]
+    out_ref[pl.ds(pl.multiple_of(bit * size, size), size), :] = own_ref[...]
+    out_ref[pl.ds(pl.multiple_of((1 - bit) * size, size), size), :] = came_ref[...]
+    out_ref[2 * size :, :] = (term_a_ref[...].astype(FULL) + term_b_ref[...].astype(FULL)).astype(LOW)
+
+
+def total_of(squares_of):
+    return jnp.sum(jnp.sum(squares_of * squares_of, axis=0, keepdims=True), axis=1, keepdims=True)
+
+
+def scale_kernel(channels, bit_ref, own_ref, came_ref, *refs):
+    out_refs, both_ref = refs[:5], refs[5]
     bound = math.sqrt(5.0) * channels
-    squares = jnp.zeros((1, 1), FULL)
-    for t in range(5):
-        part = total_ref[t * channels : (t + 1) * channels, :].astype(FULL)
-        squares = squares + jnp.sum(jnp.sum(part * part, axis=0, keepdims=True), axis=1, keepdims=True)
+    squares = total_of(own_ref[...].astype(FULL)) + total_of(came_ref[...].astype(FULL))
     factor = bound / jnp.maximum(jnp.sqrt(squares), bound)
-    for t in range(5):
-        out_refs[t][...] = total_ref[t * channels : (t + 1) * channels, :].astype(FULL) * factor
+    both_ref[bit_ref[0]] = own_ref[...]
+    both_ref[1 - bit_ref[0]] = came_ref[...]
+    half = channels // 2
+    for h in range(2):
+        for t in range(2):
+            out_refs[1 + 2 * h + t][...] = both_ref[h, t * channels : (t + 1) * channels, :].astype(FULL) * factor
+        out_refs[0][h * half : (h + 1) * half, :] = both_ref[h, 2 * channels :, :].astype(FULL) * factor
 
 
 def summed(terms):
@@ -315,27 +367,68 @@
 
     feats = sent(chunks, 1)
     cots = sent(cot_chunks, 1)
-    *backs, terms, _ = call(
+    *backs, parts = call(
         lambda *refs: attend_kernel(plan, *refs),
-        [((2 * chunk, channels), LOW)] * window + [((4 * channels, channels), FULL), ((6, plan.owned, channels), LOW)],
+        [((2 * chunk, channels), LOW)] * window + [((6, plan.owned, channels), LOW)],
         [],
         [*feats, *cots, query_weight, key_weight, value_weight, output_weight],
     )
     backs = sent(backs, -1)
-    out_cells, kept, first, last, message_term = call(
+    core, across = [((lax.axis_index("ev") >> b) & 1).astype(jnp.int32).reshape(1) for b in range(2)]
+    a_send, a_keep = call(
+        lambda *refs: term_kernel(channels, *refs),
+        [((2 * channels, channels), LOW), ((2 * channels, channels), FULL)],
+        [core],
+        [parts],
+    )
+    a_came = swapped(a_send, "ev", 1)
+    a_send, a_keep = call(halve_kernel, [((channels, channels), LOW), ((channels, channels), FULL)], [across], [a_keep, a_came])
+    a_came = swapped(a_send, "ev", 2)
+    half, piece = channels // 2, channels // 4
+    out_cells, kept, first, last, m_send, m_keep = call(
         lambda *refs: return_kernel(plan, *refs),
-        [((per_device, channels), LOW), ((per_device, channels), FULL), ((BLOCK, channels), LOW), ((BLOCK, channels), LOW), ((channels, channels), FULL)],
-        [nbrs],
+        [
+            ((per_device, channels), LOW),
+            ((per_device, channels), FULL),
+            ((BLOCK, channels), LOW),
+            ((BLOCK, channels), LOW),
+            ((half, channels), LOW),
+            ((half, channels), FULL),
+        ],
+        [nbrs, core],
         [*backs, put, hidden, cot, before, gathered, message_weight],
-        [pltpu.VMEM((2, total, channels), LOW)],
-    )
+        [pltpu.VMEM((2, total, channels), LOW), pltpu.VMEM((2, half, channels), FULL)],
+    )
+    m_came = swapped(m_send, "ev", 1)
     from_lower = shifted(last, "phi", 1)
     from_upper = shifted(first, "phi", -1)
+    a_keep, *a_sends = call(
+        quarter_kernel, [((piece, channels), FULL)] + [((piece, channels), LOW)] * 3, [place], [a_keep, a_came]
+    )
+    (m_own,) = call(add_kernel, [((half, channels), LOW)], [], [m_keep, m_came])
+    m_came = swapped(m_own, "ev", 2)
+    a_cames = [swapped(part, "phi", mask + 1) for mask, part in enumerate(a_sends)]
+    (m_own,) = call(add_kernel, [((half, channels), LOW)], [], [m_own, m_came])
+    m_came = swapped(m_own, "phi", 1)
+    (a_own,) = call(add_kernel, [((piece, channels), LOW)], [], [a_keep, *a_cames])
+    a_cames = [swapped(a_own, "phi", mask) for mask in (1, 2, 3)]
+    (m_own,) = call(add_kernel, [((half, channels), LOW)], [], [m_own, m_came])
+    m_came = swapped(m_own, "phi", 2)
+    (a_own,) = call(join_kernel, [((channels, channels), LOW)], [place], [a_own, *a_cames])
+    a_came = swapped(a_own, "ev", 2)
+    (own,) = call(joined_kernel, [((2 * channels + half, channels), LOW)], [across], [a_own, a_came, m_own, m_came])
+    came = swapped(own, "ev", 1)
+    grads = call(
+        lambda *refs: scale_kernel(channels, *refs),
+        [((channels, channels), FULL)] * 5,
+        [core],
+        [own, came],
+        [pltpu.VMEM((2, 2 * channels + half, channels), LOW)],
+        final=True,
+    )
     (grad_cells,) = call(
-        lambda *refs: edges_kernel(plan, *refs), [((per_device, channels), LOW)], [], [kept, from_lower, from_upper]
-    )
-    whole = summed(jnp.concatenate([message_term, terms], axis=0))
-    grads = call(lambda *refs: scale_kernel(channels, *refs), [((channels, channels), FULL)] * 5, [], [whole])
+        lambda *refs: edges_kernel(plan, *refs), [((per_device, channels), LOW)], [], [kept, from_lower, from_upper], final=True
+    )
     return (out_cells[None], grad_cells[None], *grads)
 
 

time: 87.1 us -> 69.6 us (0.80)
  waiting for transfers between devices: 34.9 us -> 24.7 us
  Pallas kernels: 16.6 us -> 8.42 us
  starting transfers between devices: 28.4 us -> 33.1 us
  local copies, waits for them, and re-layouts: 4.6 us -> 2.3 us
  other arithmetic: 1.4 us -> 0 us
    ppermute x8 -> x14, waiting for transfers between devices: 22.8 us -> 12.9 us  [swapped(): lax.ppermute(block, axis, [(i, i ^ mask) for i in range(lax.axis_size(axi...]
    pallas_call x6 -> x15, Pallas kernels: 16.6 us -> 8.42 us  [call(): pl.pallas_call(body, out_shape=[kind(shape, dtype) for shape, dtype in ou...]
    ppermute x8 -> x14, starting transfers between devices: 9.68 us -> 14.3 us  [swapped(): lax.ppermute(block, axis, [(i, i ^ mask) for i in range(lax.axis_size(axi...]
    unnamed x27 -> x23, local copies, waits for them, and re-layouts: 3.54 us -> 1.34 us
    select_n x4 -> x0, other arithmetic: 1.28 us -> none  [summed(): jnp.where(bit == 0, jnp.concatenate([whole, other], 0), jnp.concatenate([...]
  transfers between devices with their start and end apart: 18 -> 24, of which waited for: 12 -> 13; matrix products, arithmetic and copies ran while one was open for 0% -> 1% of each run, Pallas kernels for 7% -> 5%
where the time goes in v2:
time: 69.6 us; the launch traced here: 69.4 us
  starting transfers between devices  33.1 us (48%)
  waiting for transfers between devices  24.7 us (35%)
  Pallas kernels  8.42 us (12%)
  local copies, waits for them, and re-layouts  2.3 us (3%)
  between operations  0.88 us (1%)
    ppermute x10, starting transfers between devices, shifted(): lax.ppermute(block, axis, [((i - distance) % count, i) for i in range(cou...  18.9 us
    ppermute x14, starting transfers between devices, swapped(): lax.ppermute(block, axis, [(i, i ^ mask) for i in range(lax.axis_size(axi...  14.3 us
    ppermute x14, waiting for transfers between devices, swapped(): lax.ppermute(block, axis, [(i, i ^ mask) for i in range(lax.axis_size(axi...  12.9 us
    ppermute x10, waiting for transfers between devices, shifted(): lax.ppermute(block, axis, [((i - distance) % count, i) for i in range(cou...  11.8 us
    pallas_call x15, Pallas kernels, call(): pl.pallas_call(body, out_shape=[kind(shape, dtype) for shape, dtype in ou...  8.42 us
  transfers between devices with their start and end apart: 24, of which 13 were waited for; matrix products, arithmetic and copies ran while one was open for 1% of the time, Pallas kernels for 5%

profile of v2, /device:TPU:0, one launch (start us, length us, event | category | flops | bytes accessed | tf_op | source)
XLA Modules:
  0.0 69.4 jit_solution(10685934199857517664)
XLA Ops:
  0.7 1.0 %slice_bitcast_fusion = (bf16[128,256]{1,0:T(8,128)(2,1)S(1)}, bf16[128,256]{1,0:T(8,128)(2,1)S(1)}) fusion(bf16[1,256,256]{2,1,0:T(8,128)(2,1)} %param.10), kind=kLoop, calls=%fused_computation | loop fusion | bytes 262144 | tf_op jit(solution)/shard_map/slice | solution.py:349
  1.7 5.1 %collective-permute-start.1 = (bf16[128,256]{1,0:T(8,128)(2,1)S(1)}, bf16[128,256]{1,0:T(8,128)(2,1)S(1)}, u32[]{:S(2)}, u32[]{:S(2)}) collective-permute-start(bf16[128,256]{1,0:T(8,128)(2,1)S(1)} %get-tuple-element.75), channel_id=1, source_target_pairs={{4,0},{8,4},{12,8},{0,12},{5,1},{9,5},{13,9},{1,13},{6,2},{10,6},{... | collective-permute-start | bytes 196616 | tf_op jit(solution)/shard_map/ppermute | solution.py:33
  7.2 3.9 %collective-permute-start.4 = (bf16[96,256]{1,0:T(8,128)(2,1)S(1)}, bf16[96,256]{1,0:T(8,128)(2,1)S(1)}, u32[]{:S(2)}, u32[]{:S(2)}) collective-permute-start(bf16[96,256]{1,0:T(8,128)(2,1)S(1)} %get-tuple-element.45), channel_id=1, source_target_pairs={{4,0},{8,4},{12,8},{0,12},{5,1},{9,5},{13,9},{1,13},{6,2},{10,6},{... | collective-permute-start | bytes 147464 | tf_op jit(solution)/shard_map/ppermute | solution.py:33
  11.1 1.7 %collective-permute-done.refs_2_ = bf16[128,256]{1,0:T(8,128)(2,1)S(1)} collective-permute-done((bf16[128,256]{1,0:T(8,128)(2,1)S(1)}, bf16[128,256]{1,0:T(8,128)(2,1)S(1)}, u32[]{:S(2)}, u32[]{:S(2)}) %collective-permute-start) | collective-permute-done | bytes 65568 | tf_op jit(solution)/shard_map/ppermute | solution.py:33
  12.9 1.3 %shard_map.154 = (bf16[256,256]{1,0:T(8,128)(2,1)S(1)}, f32[256,256]{1,0:T(8,128)S(1)}, bf16[256,256]{1,0:T(8,128)(2,1)S(1)}, bf16[96,256]{1,0:T(8,128)(2,1)S(1)...) custom-call(s32[2,4]{1,0:T(2,128)} %bitcast.19, bf16[256,256]{1,0:T(8,128)(2,1)S(1)} %bitcast.14, ...), custom_call_target="tpu_custom_call" | custom-call | tf_op jit(solution)/shard_map/pallas_call | solution.py:22
  14.1 2.2 %collective-permute-start.2 = (bf16[96,256]{1,0:T(8,128)(2,1)S(1)}, bf16[96,256]{1,0:T(8,128)(2,1)S(1)}, u32[]{:S(2)}, u32[]{:S(2)}) collective-permute-start(bf16[96,256]{1,0:T(8,128)(2,1)S(1)} %get-tuple-element.42), channel_id=1, source_target_pairs={{4,0},{8,4},{12,8},{0,12},{5,1},{9,5},{13,9},{1,13},{6,2},{10,6},{... | collective-permute-start | bytes 147464 | tf_op jit(solution)/shard_map/ppermute | solution.py:33
  17.1 1.2 %collective-permute-done.2.refs_0_ = bf16[96,256]{1,0:T(8,128)(2,1)S(1)} collective-permute-done((bf16[96,256]{1,0:T(8,128)(2,1)S(1)}, bf16[96,256]{1,0:T(8,128)(2,1)S(1)}, u32[]{:S(2)}, u32[]{:S(2)}) %collective-permute-start.2) | collective-permute-done | bytes 49184 | tf_op jit(solution)/shard_map/ppermute | solution.py:33
  18.3 3.9 %collective-permute-done.3.refs_2_ = bf16[96,256]{1,0:T(8,128)(2,1)S(1)} collective-permute-done((bf16[96,256]{1,0:T(8,128)(2,1)S(1)}, bf16[96,256]{1,0:T(8,128)(2,1)S(1)}, u32[]{:S(2)}, u32[]{:S(2)}) %collective-permute-start.3) | collective-permute-done | bytes 49184 | tf_op jit(solution)/shard_map/ppermute | solution.py:33
  22.2 3.1 %shard_map.155 = (bf16[192,256]{1,0:T(8,128)(2,1)S(1)}, bf16[192,256]{1,0:T(8,128)(2,1)S(1)}, bf16[192,256]{1,0:T(8,128)(2,1)S(1)}, bf16[6,256,256]{2,1,0:T(8,128)(2,1)S(1)}) custom-call(bf16[96,256]{1,0:T(8,128)(2,1)S(1)} %collective-permute-done.2.refs_0_, bf16[96,256]{1,0:T(8,128)(2,1)S(1)} %get-tuple-element.43.refs_1_, ...), custom_call_target="tpu_custom_call" | custom-call | tf_op jit(solution)/shard_map/pallas_call | solution.py:22
  26.5 3.8 %collective-permute-start.7 = (bf16[192,256]{1,0:T(8,128)(2,1)S(1)}, bf16[192,256]{1,0:T(8,128)(2,1)S(1)}, u32[]{:S(2)}, u32[]{:S(2)}) collective-permute-start(bf16[192,256]{1,0:T(8,128)(2,1)S(1)} %get-tuple-element.50), channel_id=1, source_target_pairs={{4,0},{8,4},{12,8},{0,12},{5,1},{9,5},{13,9},{1,13},{6,2},{10,6},{... | collective-permute-start | bytes 294920 | tf_op jit(solution)/shard_map/ppermute | solution.py:33
  30.3 1.6 %collective-permute-start.11 = (bf16[256,256]{1,0:T(8,128)(2,1)S(1)}, bf16[256,256]{1,0:T(8,128)(2,1)S(1)}, u32[]{:S(2)}, u32[]{:S(2)}) collective-permute-start(bf16[256,256]{1,0:T(8,128)(2,1)S(1)} %get-tuple-element.63), channel_id=1, source_target_pairs={{0,2},{1,3},{2,0},{3,1},{4,6},{5,7},{6,4},{7,5},{8,10},{9,11},{10,... | collective-permute-start | bytes 393224 | tf_op jit(solution)/shard_map/ppermute | solution.py:37
  31.9 1.9 %collective-permute-done.6.refs_2_ = bf16[192,256]{1,0:T(8,128)(2,1)S(1)} collective-permute-done((bf16[192,256]{1,0:T(8,128)(2,1)S(1)}, bf16[192,256]{1,0:T(8,128)(2,1)S(1)}, u32[]{:S(2)}, u32[]{:S(2)}) %collective-permute-start.6) | collective-permute-done | bytes 98336 | tf_op jit(solution)/shard_map/ppermute | solution.py:33
  33.8 1.2 %shard_map.156 = (bf16[256,256]{1,0:T(8,128)(2,1)S(1)}, f32[256,256]{1,0:T(8,128)S(1)}, bf16[128,256]{1,0:T(8,128)(2,1)S(1)}, bf16[128,256]{1,0:T(8,128)(2,1)S(1...) custom-call(s32[2,4]{1,0:T(2,128)} %bitcast.20, s32[1]{0:T(128)} %bitcast.1.refs_1_.refs_0_, ...), custom_call_target="tpu_custom_call" | custom-call | tf_op jit(solution)/shard_map/pallas_call | solution.py:22
  35.1 1.2 %collective-permute-done.19.refs_1_ = bf16[128,256]{1,0:T(8,128)(2,1)S(1)} collective-permute-done((bf16[128,256]{1,0:T(8,128)(2,1)S(1)}, bf16[128,256]{1,0:T(8,128)(2,1)S(1)}, u32[]{:S(2)}, u32[]{:S(2)}) %collective-permute-start.19) | collective-permute-done | bytes 65568 | tf_op jit(solution)/shard_map/ppermute | solution.py:37
  36.5 3.6 %collective-permute-start.13 = (bf16[64,256]{1,0:T(8,128)(2,1)S(1)}, bf16[64,256]{1,0:T(8,128)(2,1)S(1)}, u32[]{:S(2)}, u32[]{:S(2)}) collective-permute-start(bf16[64,256]{1,0:T(8,128)(2,1)S(1)} %get-tuple-element.66), channel_id=1, source_target_pairs={{0,8},{4,12},{8,0},{12,4},{1,9},{5,13},{9,1},{13,5},{2,10},{6,14},... | collective-permute-start | bytes 98312 | tf_op jit(solution)/shard_map/ppermute | solution.py:37
  40.9 1.5 %collective-permute-start.20 = (bf16[128,256]{1,0:T(8,128)(2,1)S(1)}, bf16[128,256]{1,0:T(8,128)(2,1)S(1)}, u32[]{:S(2)}, u32[]{:S(2)}) collective-permute-start(bf16[128,256]{1,0:T(8,128)(2,1)S(1)} %shard_map.163.refs_0_), channel_id=1, source_target_pairs={{0,2},{1,3},{2,0},{3,1},{4,6},{5,7},{6,4},{7,5},{8,10},{9,11},{10,... | collective-permute-start | bytes 196616 | tf_op jit(solution)/shard_map/ppermute | solution.py:37
  42.4 3.5 %collective-permute-done.14.refs_3_ = bf16[64,256]{1,0:T(8,128)(2,1)S(1)} collective-permute-done((bf16[64,256]{1,0:T(8,128)(2,1)S(1)}, bf16[64,256]{1,0:T(8,128)(2,1)S(1)}, u32[]{:S(2)}, u32[]{:S(2)}) %collective-permute-start.14) | collective-permute-done | bytes 32800 | tf_op jit(solution)/shard_map/ppermute | solution.py:37
  46.7 3.7 %collective-permute-start.15 = (bf16[64,256]{1,0:T(8,128)(2,1)S(1)}, bf16[64,256]{1,0:T(8,128)(2,1)S(1)}, u32[]{:S(2)}, u32[]{:S(2)}) collective-permute-start(bf16[64,256]{1,0:T(8,128)(2,1)S(1)} %shard_map.161.refs_0_), channel_id=1, source_target_pairs={{0,4},{4,0},{8,12},{12,8},{1,5},{5,1},{9,13},{13,9},{2,6},{6,2},{1... | collective-permute-start | bytes 98312 | tf_op jit(solution)/shard_map/ppermute | solution.py:37
  50.5 1.4 %collective-permute-done.17.refs_3_ = bf16[64,256]{1,0:T(8,128)(2,1)S(1)} collective-permute-done((bf16[64,256]{1,0:T(8,128)(2,1)S(1)}, bf16[64,256]{1,0:T(8,128)(2,1)S(1)}, u32[]{:S(2)}, u32[]{:S(2)}) %collective-permute-start.17) | collective-permute-done | bytes 32800 | tf_op jit(solution)/shard_map/ppermute | solution.py:37
  52.4 1.6 %collective-permute-start.18 = (bf16[256,256]{1,0:T(8,128)(2,1)S(1)}, bf16[256,256]{1,0:T(8,128)(2,1)S(1)}, u32[]{:S(2)}, u32[]{:S(2)}) collective-permute-start(bf16[256,256]{1,0:T(8,128)(2,1)S(1)} %shard_map.162.own_ref), channel_id=1, source_target_pairs={{0,2},{1,3},{2,0},{3,1},{4,6},{5,7},{6,4},{7,5},{8,10},{9,11},{10,... | collective-permute-start | bytes 393224 | tf_op jit(solution)/shard_map/ppermute | solution.py:37
  55.2 5.5 %collective-permute-done.22.term_b_ref = bf16[128,256]{1,0:T(8,128)(2,1)S(1)} collective-permute-done((bf16[128,256]{1,0:T(8,128)(2,1)S(1)}, bf16[128,256]{1,0:T(8,128)(2,1)S(1)}, u32[]{:S(2)}, u32[]{:S(2)}) %collective-permute-start.22) | collective-permute-done | bytes 65568 | tf_op jit(solution)/shard_map/ppermute | solution.py:37
  61.4 3.3 %collective-permute-start.9 = (bf16[128,256]{1,0:T(8,128)(2,1)S(1)}, bf16[128,256]{1,0:T(8,128)(2,1)S(1)}, u32[]{:S(2)}, u32[]{:S(2)}) collective-permute-start(bf16[128,256]{1,0:T(8,128)(2,1)S(1)} %get-tuple-element.58), channel_id=1, source_target_pairs={{4,0},{8,4},{12,8},{0,12},{5,1},{9,5},{13,9},{1,13},{6,2},{10,6},{... | collective-permute-start | bytes 196616 | tf_op jit(solution)/shard_map/ppermute | solution.py:33
  65.3 2.2 %collective-permute-done.8.refs_1_ = bf16[128,256]{1,0:T(8,128)(2,1)S(1)} collective-permute-done((bf16[128,256]{1,0:T(8,128)(2,1)S(1)}, bf16[128,256]{1,0:T(8,128)(2,1)S(1)}, u32[]{:S(2)}, u32[]{:S(2)}) %collective-permute-start.8) | collective-permute-done | bytes 65568 | tf_op jit(solution)/shard_map/ppermute | solution.py:33
  68.2 1.2 %shard_map.167 = (f32[256,256]{1,0:T(8,128)}, f32[256,256]{1,0:T(8,128)}, f32[256,256]{1,0:T(8,128)}, f32[256,256]{1,0:T(8,128)}, f32[256,256]{1,0:T(8,128)}) custom-call(s32[1]{0:T(128)} %bitcast.1.refs_1_.refs_0_, bf16[640,256]{1,0:T(8,128)(2,1)S(1)} %shard_map.166.refs_1_, bf16[640,256]{1,0:T(8,128)(2,1)S(1)} %collective-permute-done.23.refs_2_), custom_call_target="tpu_custom_call" | custom-call | tf_op jit(solution)/shard_map/pallas_call | solution.py:22
  (63 shorter events, 8.0 us)
Async XLA Ops:
  1.7 9.4 %collective-permute-start.1 = (bf16[128,256]{1,0:T(8,128)(2,1)S(1)}, bf16[128,256]{1,0:T(8,128)(2,1)S(1)}, u32[]{:S(2)}, u32[]{:S(2)}) collective-permute-start(bf16[128,256]{1,0:T(8,128)(2,1)S(1)} %get-tuple-element.75), channel_id=1, source_target_pairs={{4,0},{8,4},{12,8},{0,12},{5,1},{9,5},{13,9},{1,13},{6,2},{10,6},{... | collective-permute-start | bytes 196616 | tf_op jit(solution)/shard_map/ppermute | solution.py:33
  6.8 6.1 %collective-permute-start = (bf16[128,256]{1,0:T(8,128)(2,1)S(1)}, bf16[128,256]{1,0:T(8,128)(2,1)S(1)}, u32[]{:S(2)}, u32[]{:S(2)}) collective-permute-start(bf16[128,256]{1,0:T(8,128)(2,1)S(1)} %get-tuple-element.76), channel_id=1, source_target_pairs={{12,0},{0,4},{4,8},{8,12},{13,1},{1,5},{5,9},{9,13},{14,2},{2,6},{... | collective-permute-start | bytes 196616 | tf_op jit(solution)/shard_map/ppermute | solution.py:33
  7.2 9.1 %collective-permute-start.4 = (bf16[96,256]{1,0:T(8,128)(2,1)S(1)}, bf16[96,256]{1,0:T(8,128)(2,1)S(1)}, u32[]{:S(2)}, u32[]{:S(2)}) collective-permute-start(bf16[96,256]{1,0:T(8,128)(2,1)S(1)} %get-tuple-element.45), channel_id=1, source_target_pairs={{4,0},{8,4},{12,8},{0,12},{5,1},{9,5},{13,9},{1,13},{6,2},{10,6},{... | collective-permute-start | bytes 147464 | tf_op jit(solution)/shard_map/ppermute | solution.py:33
  11.1 6.0 %collective-permute-start.5 = (bf16[96,256]{1,0:T(8,128)(2,1)S(1)}, bf16[96,256]{1,0:T(8,128)(2,1)S(1)}, u32[]{:S(2)}, u32[]{:S(2)}) collective-permute-start(bf16[96,256]{1,0:T(8,128)(2,1)S(1)} %get-tuple-element.47), channel_id=1, source_target_pairs={{12,0},{0,4},{4,8},{8,12},{13,1},{1,5},{5,9},{9,13},{14,2},{2,6},{... | collective-permute-start | bytes 147464 | tf_op jit(solution)/shard_map/ppermute | solution.py:33
  14.1 4.1 %collective-permute-start.2 = (bf16[96,256]{1,0:T(8,128)(2,1)S(1)}, bf16[96,256]{1,0:T(8,128)(2,1)S(1)}, u32[]{:S(2)}, u32[]{:S(2)}) collective-permute-start(bf16[96,256]{1,0:T(8,128)(2,1)S(1)} %get-tuple-element.42), channel_id=1, source_target_pairs={{4,0},{8,4},{12,8},{0,12},{5,1},{9,5},{13,9},{1,13},{6,2},{10,6},{... | collective-permute-start | bytes 147464 | tf_op jit(solution)/shard_map/ppermute | solution.py:33
  16.3 5.9 %collective-permute-start.3 = (bf16[96,256]{1,0:T(8,128)(2,1)S(1)}, bf16[96,256]{1,0:T(8,128)(2,1)S(1)}, u32[]{:S(2)}, u32[]{:S(2)}) collective-permute-start(bf16[96,256]{1,0:T(8,128)(2,1)S(1)} %get-tuple-element.44), channel_id=1, source_target_pairs={{12,0},{0,4},{4,8},{8,12},{13,1},{1,5},{5,9},{9,13},{14,2},{2,6},{... | collective-permute-start | bytes 147464 | tf_op jit(solution)/shard_map/ppermute | solution.py:33
  26.3 4.0 %collective-permute-start.10 = (bf16[512,256]{1,0:T(8,128)(2,1)S(1)}, bf16[512,256]{1,0:T(8,128)(2,1)S(1)}, u32[]{:S(2)}, u32[]{:S(2)}) collective-permute-start(bf16[512,256]{1,0:T(8,128)(2,1)S(1)} %get-tuple-element.61), channel_id=1, source_target_pairs={{0,1},{1,0},{2,3},{3,2},{4,5},{5,4},{6,7},{7,6},{8,9},{9,8},{10,11... | collective-permute-start | bytes 786440 | tf_op jit(solution)/shard_map/ppermute | solution.py:37
  26.4 7.4 %collective-permute-start.6 = (bf16[192,256]{1,0:T(8,128)(2,1)S(1)}, bf16[192,256]{1,0:T(8,128)(2,1)S(1)}, u32[]{:S(2)}, u32[]{:S(2)}) collective-permute-start(bf16[192,256]{1,0:T(8,128)(2,1)S(1)} %get-tuple-element.48), channel_id=1, source_target_pairs={{12,0},{0,4},{4,8},{8,12},{13,1},{1,5},{5,9},{9,13},{14,2},{2,6},{... | collective-permute-start | bytes 294920 | tf_op jit(solution)/shard_map/ppermute | solution.py:33
  26.5 7.4 %collective-permute-start.7 = (bf16[192,256]{1,0:T(8,128)(2,1)S(1)}, bf16[192,256]{1,0:T(8,128)(2,1)S(1)}, u32[]{:S(2)}, u32[]{:S(2)}) collective-permute-start(bf16[192,256]{1,0:T(8,128)(2,1)S(1)} %get-tuple-element.50), channel_id=1, source_target_pairs={{4,0},{8,4},{12,8},{0,12},{5,1},{9,5},{13,9},{1,13},{6,2},{10,6},{... | collective-permute-start | bytes 294920 | tf_op jit(solution)/shard_map/ppermute | solution.py:33
  30.3 6.1 %collective-permute-start.11 = (bf16[256,256]{1,0:T(8,128)(2,1)S(1)}, bf16[256,256]{1,0:T(8,128)(2,1)S(1)}, u32[]{:S(2)}, u32[]{:S(2)}) collective-permute-start(bf16[256,256]{1,0:T(8,128)(2,1)S(1)} %get-tuple-element.63), channel_id=1, source_target_pairs={{0,2},{1,3},{2,0},{3,1},{4,6},{5,7},{6,4},{7,5},{8,10},{9,11},{10,... | collective-permute-start | bytes 393224 | tf_op jit(solution)/shard_map/ppermute | solution.py:37
  35.0 1.3 %collective-permute-start.19 = (bf16[128,256]{1,0:T(8,128)(2,1)S(1)}, bf16[128,256]{1,0:T(8,128)(2,1)S(1)}, u32[]{:S(2)}, u32[]{:S(2)}) collective-permute-start(bf16[128,256]{1,0:T(8,128)(2,1)S(1)} %get-tuple-element.69), channel_id=1, source_target_pairs={{0,1},{1,0},{2,3},{3,2},{4,5},{5,4},{6,7},{7,6},{8,9},{9,8},{10,11... | collective-permute-start | bytes 196616 | tf_op jit(solution)/shard_map/ppermute | solution.py:37
  36.4 6.0 %collective-permute-start.12 = (bf16[64,256]{1,0:T(8,128)(2,1)S(1)}, bf16[64,256]{1,0:T(8,128)(2,1)S(1)}, u32[]{:S(2)}, u32[]{:S(2)}) collective-permute-start(bf16[64,256]{1,0:T(8,128)(2,1)S(1)} %get-tuple-element.65), channel_id=1, source_target_pairs={{0,4},{4,0},{8,12},{12,8},{1,5},{5,1},{9,13},{13,9},{2,6},{6,2},{1... | collective-permute-start | bytes 98312 | tf_op jit(solution)/shard_map/ppermute | solution.py:37
  36.5 5.9 %collective-permute-start.13 = (bf16[64,256]{1,0:T(8,128)(2,1)S(1)}, bf16[64,256]{1,0:T(8,128)(2,1)S(1)}, u32[]{:S(2)}, u32[]{:S(2)}) collective-permute-start(bf16[64,256]{1,0:T(8,128)(2,1)S(1)} %get-tuple-element.66), channel_id=1, source_target_pairs={{0,8},{4,12},{8,0},{12,4},{1,9},{5,13},{9,1},{13,5},{2,10},{6,14},... | collective-permute-start | bytes 98312 | tf_op jit(solution)/shard_map/ppermute | solution.py:37
  40.1 5.7 %collective-permute-start.14 = (bf16[64,256]{1,0:T(8,128)(2,1)S(1)}, bf16[64,256]{1,0:T(8,128)(2,1)S(1)}, u32[]{:S(2)}, u32[]{:S(2)}) collective-permute-start(bf16[64,256]{1,0:T(8,128)(2,1)S(1)} %get-tuple-element.67), channel_id=1, source_target_pairs={{0,12},{4,8},{8,4},{12,0},{1,13},{5,9},{9,5},{13,1},{2,14},{6,10},... | collective-permute-start | bytes 98312 | tf_op jit(solution)/shard_map/ppermute | solution.py:37
  40.9 9.5 %collective-permute-start.20 = (bf16[128,256]{1,0:T(8,128)(2,1)S(1)}, bf16[128,256]{1,0:T(8,128)(2,1)S(1)}, u32[]{:S(2)}, u32[]{:S(2)}) collective-permute-start(bf16[128,256]{1,0:T(8,128)(2,1)S(1)} %shard_map.163.refs_0_), channel_id=1, source_target_pairs={{0,2},{1,3},{2,0},{3,1},{4,6},{5,7},{6,4},{7,5},{8,10},{9,11},{10,... | collective-permute-start | bytes 196616 | tf_op jit(solution)/shard_map/ppermute | solution.py:37
  45.9 6.0 %collective-permute-start.17 = (bf16[64,256]{1,0:T(8,128)(2,1)S(1)}, bf16[64,256]{1,0:T(8,128)(2,1)S(1)}, u32[]{:S(2)}, u32[]{:S(2)}) collective-permute-start(bf16[64,256]{1,0:T(8,128)(2,1)S(1)} %shard_map.161.refs_0_), channel_id=1, source_target_pairs={{0,12},{4,8},{8,4},{12,0},{1,13},{5,9},{9,5},{13,1},{2,14},{6,10},... | collective-permute-start | bytes 98312 | tf_op jit(solution)/shard_map/ppermute | solution.py:37
  46.7 5.5 %collective-permute-start.16 = (bf16[64,256]{1,0:T(8,128)(2,1)S(1)}, bf16[64,256]{1,0:T(8,128)(2,1)S(1)}, u32[]{:S(2)}, u32[]{:S(2)}) collective-permute-start(bf16[64,256]{1,0:T(8,128)(2,1)S(1)} %shard_map.161.refs_0_), channel_id=1, source_target_pairs={{0,8},{4,12},{8,0},{12,4},{1,9},{5,13},{9,1},{13,5},{2,10},{6,14},... | collective-permute-start | bytes 98312 | tf_op jit(solution)/shard_map/ppermute | solution.py:37
  46.7 5.7 %collective-permute-start.15 = (bf16[64,256]{1,0:T(8,128)(2,1)S(1)}, bf16[64,256]{1,0:T(8,128)(2,1)S(1)}, u32[]{:S(2)}, u32[]{:S(2)}) collective-permute-start(bf16[64,256]{1,0:T(8,128)(2,1)S(1)} %shard_map.161.refs_0_), channel_id=1, source_target_pairs={{0,4},{4,0},{8,12},{12,8},{1,5},{5,1},{9,13},{13,9},{2,6},{6,2},{1... | collective-permute-start | bytes 98312 | tf_op jit(solution)/shard_map/ppermute | solution.py:37
  50.4 4.3 %collective-permute-start.21 = (bf16[128,256]{1,0:T(8,128)(2,1)S(1)}, bf16[128,256]{1,0:T(8,128)(2,1)S(1)}, u32[]{:S(2)}, u32[]{:S(2)}) collective-permute-start(bf16[128,256]{1,0:T(8,128)(2,1)S(1)} %shard_map.164.refs_0_), channel_id=1, source_target_pairs={{0,4},{4,0},{8,12},{12,8},{1,5},{5,1},{9,13},{13,9},{2,6},{6,2},{1... | collective-permute-start | bytes 196616 | tf_op jit(solution)/shard_map/ppermute | solution.py:37
  52.4 8.3 %collective-permute-start.18 = (bf16[256,256]{1,0:T(8,128)(2,1)S(1)}, bf16[256,256]{1,0:T(8,128)(2,1)S(1)}, u32[]{:S(2)}, u32[]{:S(2)}) collective-permute-start(bf16[256,256]{1,0:T(8,128)(2,1)S(1)} %shard_map.162.own_ref), channel_id=1, source_target_pairs={{0,2},{1,3},{2,0},{3,1},{4,6},{5,7},{6,4},{7,5},{8,10},{9,11},{10,... | collective-permute-start | bytes 393224 | tf_op jit(solution)/shard_map/ppermute | solution.py:37
  54.7 5.9 %collective-permute-start.22 = (bf16[128,256]{1,0:T(8,128)(2,1)S(1)}, bf16[128,256]{1,0:T(8,128)(2,1)S(1)}, u32[]{:S(2)}, u32[]{:S(2)}) collective-permute-start(bf16[128,256]{1,0:T(8,128)(2,1)S(1)} %shard_map.165.term_a_ref), channel_id=1, source_target_pairs={{0,8},{4,12},{8,0},{12,4},{1,9},{5,13},{9,1},{13,5},{2,10},{6,14},... | collective-permute-start | bytes 196616 | tf_op jit(solution)/shard_map/ppermute | solution.py:37
  60.7 7.5 %collective-permute-start.23 = (bf16[640,256]{1,0:T(8,128)(2,1)S(1)}, bf16[640,256]{1,0:T(8,128)(2,1)S(1)}, u32[]{:S(2)}, u32[]{:S(2)}) collective-permute-start(bf16[640,256]{1,0:T(8,128)(2,1)S(1)} %shard_map.166.refs_1_), channel_id=1, source_target_pairs={{0,1},{1,0},{2,3},{3,2},{4,5},{5,4},{6,7},{7,6},{8,9},{9,8},{10,11... | collective-permute-start | bytes 983048 | tf_op jit(solution)/shard_map/ppermute | solution.py:37
  60.8 6.7 %collective-permute-start.8 = (bf16[128,256]{1,0:T(8,128)(2,1)S(1)}, bf16[128,256]{1,0:T(8,128)(2,1)S(1)}, u32[]{:S(2)}, u32[]{:S(2)}) collective-permute-start(bf16[128,256]{1,0:T(8,128)(2,1)S(1)} %get-tuple-element.57), channel_id=1, source_target_pairs={{12,0},{0,4},{4,8},{8,12},{13,1},{1,5},{5,9},{9,13},{14,2},{2,6},{... | collective-permute-start | bytes 196616 | tf_op jit(solution)/shard_map/ppermute | solution.py:33
  61.4 6.2 %collective-permute-start.9 = (bf16[128,256]{1,0:T(8,128)(2,1)S(1)}, bf16[128,256]{1,0:T(8,128)(2,1)S(1)}, u32[]{:S(2)}, u32[]{:S(2)}) collective-permute-start(bf16[128,256]{1,0:T(8,128)(2,1)S(1)} %get-tuple-element.58), channel_id=1, source_target_pairs={{4,0},{8,4},{12,8},{0,12},{5,1},{9,5},{13,9},{1,13},{6,2},{10,6},{... | collective-permute-start | bytes 196616 | tf_op jit(solution)/shard_map/ppermute | solution.py:33
  (11 other events, 83.3 us)

commit v3 on v2

--- a/solution.py
+++ b/solution.py
@@ -17,7 +17,7 @@
 SMEM = pl.BlockSpec(memory_space=pltpu.SMEM)
 
 
-def call(body, outs, scalars, arrays, scratch=(), final=False):
+def call(body, outs, scalars, arrays, scratch=(), final=False, micros=0.1):
     kind = jax.ShapeDtypeStruct if final else pltpu.VMEM
     return pl.pallas_call(
         body,
@@ -25,6 +25,8 @@
         in_specs=[SMEM] * len(scalars) + [VMEM] * len(arrays),
         out_specs=[VMEM] * len(outs),
         scratch_shapes=list(scratch),
+        compiler_params=pltpu.CompilerParams(vmem_limit_bytes=16 << 20),
+        cost_estimate=pl.CostEstimate(flops=int(micros * 1e9), transcendentals=0, bytes_accessed=0),
     )(*scalars, *[pltpu.with_memory_space_constraint(x, pltpu.VMEM) for x in arrays])
 
 
@@ -64,16 +66,28 @@
         self.chunk = -(-(self.used + 1) // 16) * 16
         self.slots = -(-self.window * self.cap // 64) * 64
         self.owned = JET_DEV * self.slots
+        assert sectors % 2 == 0
+        self.hops = sorted((o ^ 1 for o in range(-self.radius, self.radius + 1)), key=abs)
+
+    def routed(self, parts, back=False):
+        n = self.sectors
+        moved = []
+        for part, hop in zip(parts, self.hops):
+            route = [(p, (p + (hop if p % 2 == 0 else -hop)) % n) for p in range(n)]
+            if back:
+                route = [(there, here) for here, there in route]
+            moved.append(lax.ppermute(part, "phi", route) if hop else part)
+        return moved
 
 
 def index_kernel(plan, where_ref, cell_ref, jet_ref, cot_ref, pick_ref, place_ref, *chunk_refs):
     sector = where_ref[0]
     count, members = plan.chunk, plan.members
     jets = jet_ref[...]
-    owner = lax.shift_right_logical(jets, 2)
-    offset = owner - sector + plan.radius
-    offset = jnp.where(offset < 0, offset + plan.sectors, offset)
-    offset = jnp.where(offset >= plan.sectors, offset - plan.sectors, offset)
+    hop = lax.bitwise_xor(lax.shift_right_logical(jets, 2), 1) - sector
+    hop = jnp.where(lax.bitwise_and(sector, 1) == 0, hop, -hop)
+    hop = jnp.where(hop < 0, hop + plan.sectors, hop)
+    offset = sum(jnp.where(hop == known % plan.sectors, k, 0) for k, known in enumerate(plan.hops))
     inner = lax.bitwise_and(jets, 3)
     row = (offset * JET_DEV + inner).astype(FULL)
     rows, cols = iota((members, members), 0), iota((members, members), 1)
@@ -98,8 +112,10 @@
         chunk_refs[w][...] = jnp.where(mask_row, present, part).astype(LOW)
 
 
-def hidden_kernel(plan, nbr_ref, cell_ref, low_ref, high_ref, weight_ref, pick_ref, gathered_ref, before_ref, hidden_ref, *chunk_refs):
+def hidden_kernel(plan, nbr_ref, cell_ref, low_ref, high_ref, weight_ref, pick_ref, *refs):
     blocks = plan.blocks
+    cot_refs, chunk_refs = refs[: plan.window], refs[plan.window + 3 :]
+    gathered_ref, before_ref, hidden_ref = refs[plan.window : plan.window + 3]
     entries = [low_ref[...].astype(FULL)]
     entries += [cell_ref[b * BLOCK : (b + 1) * BLOCK, :].astype(FULL) for b in range(blocks)]
     entries += [high_ref[...].astype(FULL)]
@@ -116,15 +132,16 @@
     hidden_ref[...] = hidden
     chosen = mm(pick_ref[...], hidden).astype(LOW)
     for w in range(plan.window):
-        chunk_refs[w][...] = chosen[w * plan.chunk : (w + 1) * plan.chunk, :]
+        chunk_refs[w][: plan.chunk, :] = chosen[w * plan.chunk : (w + 1) * plan.chunk, :]
+        chunk_refs[w][plan.chunk :, :] = cot_refs[w][...]
 
 
 def attend_kernel(plan, *refs):
     window, count, slots, owned, channels = plan.window, plan.chunk, plan.slots, plan.owned, plan.channels
-    feat_refs, cot_refs = refs[:window], refs[window : 2 * window]
-    wq_ref, wk_ref, wv_ref, wo_ref = refs[2 * window : 2 * window + 4]
-    back_refs = refs[2 * window + 4 : 3 * window + 4]
-    (parts_ref,) = refs[3 * window + 4 :]
+    chunk_refs = refs[:window]
+    wq_ref, wk_ref, wv_ref, wo_ref = refs[window : window + 4]
+    back_refs = refs[window + 4 : 2 * window + 4]
+    (parts_ref,) = refs[2 * window + 4 :]
     head = channels // HEADS
     scale = 1.0 / math.sqrt(head)
 
@@ -137,8 +154,8 @@
     for w in range(window):
         hot = jnp.where(iota((owned, count), 0) == seat(iota((owned, count), 1), w), 1.0, 0.0)
         low = hot.astype(LOW)
-        m, u = mm(low, feat_refs[w][...]), mm(low, cot_refs[w][...])
-        tail = cot_refs[w][base : base + 16, :].astype(FULL)
+        m, u = mm(low, chunk_refs[w][:count, :]), mm(low, chunk_refs[w][count:, :])
+        tail = chunk_refs[w][count + base : count + base + 16, :].astype(FULL)
         row = jnp.sum(jnp.where(iota(tail.shape, 0) == plan.used - base, tail, 0.0), axis=0, keepdims=True)
         p = jnp.sum(hot * row[:, :count], axis=1, keepdims=True)
         members = m if members is None else members + m
@@ -264,30 +281,11 @@
     send_ref[...] = (rows_of(kept_ref, 1 - bit, half) + rows_of(came_ref, 1 - bit, half).astype(FULL)).astype(LOW)
 
 
-def quarter_kernel(place_ref, kept_ref, came_ref, keep_ref, *send_refs):
-    size = kept_ref.shape[0] // 4
-    for mask in range(4):
-        at = lax.bitwise_xor(place_ref[0], mask)
-        part = rows_of(kept_ref, at, size) + rows_of(came_ref, at, size).astype(FULL)
-        if mask:
-            send_refs[mask - 1][...] = part.astype(LOW)
-        else:
-            keep_ref[...] = part
-
-
 def add_kernel(*refs):
     total = refs[0][...].astype(FULL)
     for ref in refs[1:-1]:
         total = total + ref[...].astype(FULL)
     refs[-1][...] = total.astype(LOW)
-
-
-def join_kernel(place_ref, *refs):
-    out_ref = refs[-1]
-    size = refs[0].shape[0]
-    for mask, ref in enumerate(refs[:-1]):
-        at = lax.bitwise_xor(place_ref[0], mask)
-        out_ref[pl.ds(pl.multiple_of(at * size, size), size), :] = ref[...]
 
 
 def joined_kernel(bit_ref, own_ref, came_ref, term_a_ref, term_b_ref, out_ref):
@@ -316,33 +314,12 @@
         out_refs[0][h * half : (h + 1) * half, :] = both_ref[h, 2 * channels :, :].astype(FULL) * factor
 
 
-def summed(terms):
-    stages = []
-    for axis in ("ev", "phi"):
-        mask = 1
-        while mask < lax.axis_size(axis):
-            stages.append((axis, mask))
-            mask *= 2
-    bits = [(lax.axis_index(axis) & mask) // mask for axis, mask in stages]
-    kept = terms
-    for (axis, mask), bit in zip(stages, bits):
-        half = kept.shape[0] // 2
-        away = lax.dynamic_slice_in_dim(kept, (1 - bit) * half, half, 0).astype(LOW)
-        kept = lax.dynamic_slice_in_dim(kept, bit * half, half, 0)
-        kept = kept + swapped(away, axis, mask).astype(FULL)
-    whole = kept.astype(LOW)
-    for (axis, mask), bit in zip(reversed(stages), reversed(bits)):
-        other = swapped(whole, axis, mask)
-        whole = jnp.where(bit == 0, jnp.concatenate([whole, other], 0), jnp.concatenate([other, whole], 0))
-    return whole
-
-
 def on_device(cell_feats, neighbours, member_cell, member_jet, cotangent, message_weight, query_weight, key_weight, value_weight, output_weight):
     events, per_device, channels = cell_feats.shape
     assert events == 1
     members_dev = member_cell.shape[1]
     plan = Plan(lax.axis_size("phi"), per_device, members_dev, channels)
-    window, chunk, radius = plan.window, plan.chunk, plan.radius
+    window, chunk = plan.window, plan.chunk
     place = lax.axis_index("phi").astype(jnp.int32).reshape(1)
     cells, cot, nbrs = cell_feats[0], cotangent[0], neighbours[0]
     low = shifted(cells[per_device - BLOCK :], "phi", 1)
@@ -353,27 +330,26 @@
         [((total, per_device), LOW), ((per_device, total), LOW)] + [((chunk, channels), LOW)] * window,
         [place],
         [member_cell.reshape(1, members_dev), member_jet.reshape(1, members_dev), cot],
+        micros=0.5,
     )
     gathered, before, hidden, *chunks = call(
         lambda *refs: hidden_kernel(plan, *refs),
         [((per_device, channels), LOW), ((per_device, channels), FULL), ((per_device, channels), LOW)]
-        + [((chunk, channels), LOW)] * window,
+        + [((2 * chunk, channels), LOW)] * window,
         [nbrs],
-        [cells, low, high, message_weight, pick],
-    )
-
-    def sent(parts, sign):
-        return [part if w == radius else shifted(part, "phi", sign * (w - radius)) for w, part in enumerate(parts)]
-
-    feats = sent(chunks, 1)
-    cots = sent(cot_chunks, 1)
+        [cells, low, high, message_weight, pick, *cot_chunks],
+        micros=1.0,
+    )
+
+    chunks = plan.routed(chunks)
     *backs, parts = call(
         lambda *refs: attend_kernel(plan, *refs),
         [((2 * chunk, channels), LOW)] * window + [((6, plan.owned, channels), LOW)],
         [],
-        [*feats, *cots, query_weight, key_weight, value_weight, output_weight],
-    )
-    backs = sent(backs, -1)
+        [*chunks, query_weight, key_weight, value_weight, output_weight],
+        micros=3.0,
+    )
+    backs = plan.routed(backs, back=True)
     core, across = [((lax.axis_index("ev") >> b) & 1).astype(jnp.int32).reshape(1) for b in range(2)]
     a_send, a_keep = call(
         lambda *refs: term_kernel(channels, *refs),
@@ -384,7 +360,7 @@
     a_came = swapped(a_send, "ev", 1)
     a_send, a_keep = call(halve_kernel, [((channels, channels), LOW), ((channels, channels), FULL)], [across], [a_keep, a_came])
     a_came = swapped(a_send, "ev", 2)
-    half, piece = channels // 2, channels // 4
+    half = channels // 2
     out_cells, kept, first, last, m_send, m_keep = call(
         lambda *refs: return_kernel(plan, *refs),
         [
@@ -398,24 +374,29 @@
         [nbrs, core],
         [*backs, put, hidden, cot, before, gathered, message_weight],
         [pltpu.VMEM((2, total, channels), LOW), pltpu.VMEM((2, half, channels), FULL)],
-    )
+        micros=4.0,
+    )
+    def added(rows, *parts):
+        return call(add_kernel, [((rows, channels), LOW)], [], list(parts))[0]
+
     m_came = swapped(m_send, "ev", 1)
+    a_own = added(channels, a_keep, a_came)
     from_lower = shifted(last, "phi", 1)
     from_upper = shifted(first, "phi", -1)
-    a_keep, *a_sends = call(
-        quarter_kernel, [((piece, channels), FULL)] + [((piece, channels), LOW)] * 3, [place], [a_keep, a_came]
-    )
-    (m_own,) = call(add_kernel, [((half, channels), LOW)], [], [m_keep, m_came])
+    m_own = added(half, m_keep, m_came)
     m_came = swapped(m_own, "ev", 2)
-    a_cames = [swapped(part, "phi", mask + 1) for mask, part in enumerate(a_sends)]
-    (m_own,) = call(add_kernel, [((half, channels), LOW)], [], [m_own, m_came])
-    m_came = swapped(m_own, "phi", 1)
-    (a_own,) = call(add_kernel, [((piece, channels), LOW)], [], [a_keep, *a_cames])
-    a_cames = [swapped(a_own, "phi", mask) for mask in (1, 2, 3)]
-    (m_own,) = call(add_kernel, [((half, channels), LOW)], [], [m_own, m_came])
-    m_came = swapped(m_own, "phi", 2)
-    (a_own,) = call(join_kernel, [((channels, channels), LOW)], [place], [a_own, *a_cames])
+    mask = 1
+    while mask < plan.sectors:
+        a_came = swapped(a_own, "phi", mask)
+        m_own = added(half, m_own, m_came)
+        m_came = swapped(m_own, "phi", mask)
+        a_own = added(channels, a_own, a_came)
+        mask *= 2
     a_came = swapped(a_own, "ev", 2)
+    (grad_cells,) = call(
+        lambda *refs: edges_kernel(plan, *refs), [((per_device, channels), LOW)], [], [kept, from_lower, from_upper]
+    )
+    m_came, grad_cells = lax.optimization_barrier((m_came, grad_cells))
     (own,) = call(joined_kernel, [((2 * channels + half, channels), LOW)], [across], [a_own, a_came, m_own, m_came])
     came = swapped(own, "ev", 1)
     grads = call(
@@ -425,9 +406,6 @@
         [own, came],
         [pltpu.VMEM((2, 2 * channels + half, channels), LOW)],
         final=True,
-    )
-    (grad_cells,) = call(
-        lambda *refs: edges_kernel(plan, *refs), [((per_device, channels), LOW)], [], [kept, from_lower, from_upper], final=True
     )
     return (out_cells[None], grad_cells[None], *grads)
 

time: 69.6 us -> 59.2 us (0.85)
  starting transfers between devices: 33.1 us -> 20.1 us
  waiting for transfers between devices: 24.7 us -> 27.2 us
  local copies, waits for them, and re-layouts: 2.3 us -> 3.6 us
  Pallas kernels: 8.42 us -> 7.43 us
    ppermute x10 -> x4, starting transfers between devices: 18.9 us -> 8.93 us  [shifted(): lax.ppermute(block, axis, [((i - distance) % count, i) for i in range(cou...]
    ppermute x0 -> x4, waiting for transfers between devices: none -> 7.91 us  [routed(): moved.append(lax.ppermute(part, 'phi', route) if hop else part)]
    ppermute x14 -> x10, starting transfers between devices: 14.3 us -> 7.31 us  [swapped(): lax.ppermute(block, axis, [(i, i ^ mask) for i in range(lax.axis_size(axi...]
    ppermute x10 -> x4, waiting for transfers between devices: 11.8 us -> 7.12 us  [shifted(): lax.ppermute(block, axis, [((i - distance) % count, i) for i in range(cou...]
    ppermute x0 -> x4, starting transfers between devices: none -> 3.82 us  [routed(): moved.append(lax.ppermute(part, 'phi', route) if hop else part)]
    unnamed x23 -> x22, local copies, waits for them, and re-layouts: 1.34 us -> 2.68 us
    pallas_call x15, Pallas kernels: 8.42 us -> 7.43 us  [call(): pl.pallas_call(body, out_shape=[kind(shape, dtype) for shape, dtype in ou...]
    ppermute x14 -> x10, waiting for transfers between devices: 12.9 us -> 12.2 us  [swapped(): lax.ppermute(block, axis, [(i, i ^ mask) for i in range(lax.axis_size(axi...]
  transfers between devices with their start and end apart: 24 -> 18, of which waited for: 13 -> 14; matrix products, arithmetic and copies ran while one was open for 1% -> 2% of each run, Pallas kernels for 5% -> 3%
where the time goes in v3:
time: 59.2 us; the launch traced here: 59.1 us
  waiting for transfers between devices  27.2 us (46%)
  starting transfers between devices  20.1 us (34%)
  Pallas kernels  7.43 us (13%)
  local copies, waits for them, and re-layouts  3.6 us (6%)
  between operations  0.79 us (1%)
    ppermute x10, waiting for transfers between devices, swapped(): lax.ppermute(block, axis, [(i, i ^ mask) for i in range(lax.axis_size(axi...  12.2 us
    ppermute x4, starting transfers between devices, shifted(): lax.ppermute(block, axis, [((i - distance) % count, i) for i in range(cou...  8.93 us
    ppermute x4, waiting for transfers between devices, routed(): moved.append(lax.ppermute(part, 'phi', route) if hop else part)  7.91 us
    pallas_call x15, Pallas kernels, call(): pl.pallas_call(body, out_shape=[kind(shape, dtype) for shape, dtype in ou...  7.43 us
    ppermute x10, starting transfers between devices, swapped(): lax.ppermute(block, axis, [(i, i ^ mask) for i in range(lax.axis_size(axi...  7.31 us
    ppermute x4, waiting for transfers between devices, shifted(): lax.ppermute(block, axis, [((i - distance) % count, i) for i in range(cou...  7.12 us
    ppermute x4, starting transfers between devices, routed(): moved.append(lax.ppermute(part, 'phi', route) if hop else part)  3.82 us
    unnamed x22, local copies, waits for them, and re-layouts  2.68 us
  transfers between devices with their start and end apart: 18, of which 14 were waited for; matrix products, arithmetic and copies ran while one was open for 2% of the time, Pallas kernels for 3%

profile of v3, /device:TPU:0, one launch (start us, length us, event | category | flops | bytes accessed | tf_op | source)
XLA Modules:
  0.0 59.1 jit_solution(9295540080230781289)
XLA Ops:
  0.6 0.9 %slice_bitcast_fusion = (bf16[128,256]{1,0:T(8,128)(2,1)S(1)}, bf16[128,256]{1,0:T(8,128)(2,1)S(1)}) fusion(bf16[1,256,256]{2,1,0:T(8,128)(2,1)} %param.10), kind=kLoop, calls=%fused_computation | loop fusion | bytes 262144 | tf_op jit(solution)/shard_map/slice | solution.py:326
  1.6 5.1 %collective-permute-start.1 = (bf16[128,256]{1,0:T(8,128)(2,1)S(1)}, bf16[128,256]{1,0:T(8,128)(2,1)S(1)}, u32[]{:S(2)}, u32[]{:S(2)}) collective-permute-start(bf16[128,256]{1,0:T(8,128)(2,1)S(1)} %get-tuple-element.71), channel_id=1, source_target_pairs={{4,0},{8,4},{12,8},{0,12},{5,1},{9,5},{13,9},{1,13},{6,2},{10,6},{... | collective-permute-start | bytes 196616 | tf_op jit(solution)/shard_map/ppermute | solution.py:35
  7.8 0.9 %collective-permute-done.1.refs_3_ = bf16[128,256]{1,0:T(8,128)(2,1)S(1)} collective-permute-done((bf16[128,256]{1,0:T(8,128)(2,1)S(1)}, bf16[128,256]{1,0:T(8,128)(2,1)S(1)}, u32[]{:S(2)}, u32[]{:S(2)}) %collective-permute-start.1) | collective-permute-done | bytes 65568 | tf_op jit(solution)/shard_map/ppermute | solution.py:35
  8.7 4.0 %collective-permute-done.refs_2_ = bf16[128,256]{1,0:T(8,128)(2,1)S(1)} collective-permute-done((bf16[128,256]{1,0:T(8,128)(2,1)S(1)}, bf16[128,256]{1,0:T(8,128)(2,1)S(1)}, u32[]{:S(2)}, u32[]{:S(2)}) %collective-permute-start) | collective-permute-done | bytes 65568 | tf_op jit(solution)/shard_map/ppermute | solution.py:35
  13.4 1.0 %shard_map.154 = (bf16[256,256]{1,0:T(8,128)(2,1)S(1)}, f32[256,256]{1,0:T(8,128)S(1)}, bf16[256,256]{1,0:T(8,128)(2,1)S(1)}, bf16[192,256]{1,0:T(8,128)(2,1)S(1...) custom-call(s32[2,4]{1,0:T(2,128)S(1)} %bitcast.18, bf16[256,256]{1,0:T(8,128)(2,1)S(1)} %bitcast.15, ...), custom_call_target="tpu_custom_call" | custom-call | flops 1000000000 | tf_op jit(solution)/shard_map/pallas_call | solution.py:22
  15.3 3.8 %collective-permute-done.2.refs_1_ = bf16[192,256]{1,0:T(8,128)(2,1)S(1)} collective-permute-done((bf16[192,256]{1,0:T(8,128)(2,1)S(1)}, bf16[192,256]{1,0:T(8,128)(2,1)S(1)}, u32[]{:S(2)}, u32[]{:S(2)}) %collective-permute-start.2) | collective-permute-done | bytes 98336 | tf_op jit(solution)/shard_map/ppermute | solution.py:79
  19.1 1.0 %collective-permute-done.3.refs_2_ = bf16[192,256]{1,0:T(8,128)(2,1)S(1)} collective-permute-done((bf16[192,256]{1,0:T(8,128)(2,1)S(1)}, bf16[192,256]{1,0:T(8,128)(2,1)S(1)}, u32[]{:S(2)}, u32[]{:S(2)}) %collective-permute-start.3) | collective-permute-done | bytes 98336 | tf_op jit(solution)/shard_map/ppermute | solution.py:79
  20.2 3.1 %shard_map.155 = (bf16[192,256]{1,0:T(8,128)(2,1)S(1)}, bf16[192,256]{1,0:T(8,128)(2,1)S(1)}, bf16[192,256]{1,0:T(8,128)(2,1)S(1)}, bf16[6,256,256]{2,1,0:T(8,128)(2,1)S(1)}) custom-call(bf16[192,256]{1,0:T(8,128)(2,1)S(1)} %get-tuple-element.43.refs_0_, bf16[192,256]{1,0:T(8,128)(2,1)S(1)} %collective-permute-done.2.refs_1_, ...), custom_call_target="tpu_custom_call" | custom-call | flops 3000000000 | tf_op jit(solution)/shard_map/pallas_call | solution.py:22
  23.7 1.5 %collective-permute-done.12.came_ref = bf16[512,256]{1,0:T(8,128)(2,1)S(1)} collective-permute-done((bf16[512,256]{1,0:T(8,128)(2,1)S(1)}, bf16[512,256]{1,0:T(8,128)(2,1)S(1)}, u32[]{:S(2)}, u32[]{:S(2)}) %collective-permute-start.12) | collective-permute-done | bytes 262176 | tf_op jit(solution)/shard_map/ppermute | solution.py:39
  25.3 1.6 %collective-permute-start.13 = (bf16[256,256]{1,0:T(8,128)(2,1)S(1)}, bf16[256,256]{1,0:T(8,128)(2,1)S(1)}, u32[]{:S(2)}, u32[]{:S(2)}) collective-permute-start(bf16[256,256]{1,0:T(8,128)(2,1)S(1)} %get-tuple-element.64), channel_id=1, source_target_pairs={{0,2},{1,3},{2,0},{3,1},{4,6},{5,7},{6,4},{7,5},{8,10},{9,11},{10,... | collective-permute-start | bytes 393224 | tf_op jit(solution)/shard_map/ppermute | solution.py:39
  26.9 1.9 %collective-permute-start.4 = (bf16[192,256]{1,0:T(8,128)(2,1)S(1)}, bf16[192,256]{1,0:T(8,128)(2,1)S(1)}, u32[]{:S(2)}, u32[]{:S(2)}) collective-permute-start(bf16[192,256]{1,0:T(8,128)(2,1)S(1)} %get-tuple-element.47), channel_id=1, source_target_pairs={{4,0},{0,4},{12,8},{8,12},{5,1},{1,5},{13,9},{9,13},{6,2},{2,6},{1... | collective-permute-start | bytes 294920 | tf_op jit(solution)/shard_map/ppermute | solution.py:79
  28.7 1.1 %collective-permute-start.5 = (bf16[192,256]{1,0:T(8,128)(2,1)S(1)}, bf16[192,256]{1,0:T(8,128)(2,1)S(1)}, u32[]{:S(2)}, u32[]{:S(2)}) collective-permute-start(bf16[192,256]{1,0:T(8,128)(2,1)S(1)} %get-tuple-element.48), channel_id=1, source_target_pairs={{8,0},{12,4},{0,8},{4,12},{9,1},{13,5},{1,9},{5,13},{10,2},{14,6},... | collective-permute-start | bytes 294920 | tf_op jit(solution)/shard_map/ppermute | solution.py:79
  29.8 1.1 %collective-permute-done.13.refs_1_ = bf16[256,256]{1,0:T(8,128)(2,1)S(1)} collective-permute-done((bf16[256,256]{1,0:T(8,128)(2,1)S(1)}, bf16[256,256]{1,0:T(8,128)(2,1)S(1)}, u32[]{:S(2)}, u32[]{:S(2)}) %collective-permute-start.13) | collective-permute-done | bytes 131104 | tf_op jit(solution)/shard_map/ppermute | solution.py:39
  30.9 1.9 %collective-permute-start.14 = (bf16[256,256]{1,0:T(8,128)(2,1)S(1)}, bf16[256,256]{1,0:T(8,128)(2,1)S(1)}, u32[]{:S(2)}, u32[]{:S(2)}) collective-permute-start(bf16[256,256]{1,0:T(8,128)(2,1)S(1)} %shard_map.163.refs_0_), channel_id=1, source_target_pairs={{0,4},{4,0},{8,12},{12,8},{1,5},{5,1},{9,13},{13,9},{2,6},{6,2},{1... | collective-permute-start | bytes 393224 | tf_op jit(solution)/shard_map/ppermute | solution.py:39
  32.9 3.1 %collective-permute-done.5.refs_4_ = bf16[192,256]{1,0:T(8,128)(2,1)S(1)} collective-permute-done((bf16[192,256]{1,0:T(8,128)(2,1)S(1)}, bf16[192,256]{1,0:T(8,128)(2,1)S(1)}, u32[]{:S(2)}, u32[]{:S(2)}) %collective-permute-start.5) | collective-permute-done | bytes 98336 | tf_op jit(solution)/shard_map/ppermute | solution.py:79
  36.0 1.1 %shard_map.156 = (bf16[256,256]{1,0:T(8,128)(2,1)S(1)}, f32[256,256]{1,0:T(8,128)S(1)}, bf16[128,256]{1,0:T(8,128)(2,1)S(1)}, bf16[128,256]{1,0:T(8,128)(2,1)S(1...) custom-call(s32[2,4]{1,0:T(2,128)S(1)} %bitcast.19, s32[1]{0:T(128)} %bitcast.1.refs_1_.refs_0_, ...), custom_call_target="tpu_custom_call" | custom-call | flops 4000000000 | tf_op jit(solution)/shard_map/pallas_call | solution.py:22
  39.2 3.5 %collective-permute-done.7.refs_1_ = bf16[128,256]{1,0:T(8,128)(2,1)S(1)} collective-permute-done((bf16[128,256]{1,0:T(8,128)(2,1)S(1)}, bf16[128,256]{1,0:T(8,128)(2,1)S(1)}, u32[]{:S(2)}, u32[]{:S(2)}) %collective-permute-start.7) | collective-permute-done | bytes 65568 | tf_op jit(solution)/shard_map/ppermute | solution.py:39
  42.7 1.1 %collective-permute-start.8 = (bf16[128,256]{1,0:T(8,128)(2,1)S(1)}, bf16[128,256]{1,0:T(8,128)(2,1)S(1)}, u32[]{:S(2)}, u32[]{:S(2)}) collective-permute-start(bf16[128,256]{1,0:T(8,128)(2,1)S(1)} %shard_map.158.refs_0_), channel_id=1, source_target_pairs={{0,4},{4,0},{8,12},{12,8},{1,5},{5,1},{9,13},{13,9},{2,6},{6,2},{1... | collective-permute-start | bytes 196616 | tf_op jit(solution)/shard_map/ppermute | solution.py:39
  43.8 2.1 %collective-permute-done.15.refs_1_ = bf16[256,256]{1,0:T(8,128)(2,1)S(1)} collective-permute-done((bf16[256,256]{1,0:T(8,128)(2,1)S(1)}, bf16[256,256]{1,0:T(8,128)(2,1)S(1)}, u32[]{:S(2)}, u32[]{:S(2)}) %collective-permute-start.15) | collective-permute-done | bytes 131104 | tf_op jit(solution)/shard_map/ppermute | solution.py:39
  46.0 1.0 %collective-permute-start.16 = (bf16[256,256]{1,0:T(8,128)(2,1)S(1)}, bf16[256,256]{1,0:T(8,128)(2,1)S(1)}, u32[]{:S(2)}, u32[]{:S(2)}) collective-permute-start(bf16[256,256]{1,0:T(8,128)(2,1)S(1)} %shard_map.165.own_ref), channel_id=1, source_target_pairs={{0,2},{1,3},{2,0},{3,1},{4,6},{5,7},{6,4},{7,5},{8,10},{9,11},{10,... | collective-permute-start | bytes 393224 | tf_op jit(solution)/shard_map/ppermute | solution.py:39
  47.0 3.8 %collective-permute-start.11 = (bf16[128,256]{1,0:T(8,128)(2,1)S(1)}, bf16[128,256]{1,0:T(8,128)(2,1)S(1)}, u32[]{:S(2)}, u32[]{:S(2)}) collective-permute-start(bf16[128,256]{1,0:T(8,128)(2,1)S(1)} %get-tuple-element.58), channel_id=1, source_target_pairs={{4,0},{8,4},{12,8},{0,12},{5,1},{9,5},{13,9},{1,13},{6,2},{10,6},{... | collective-permute-start | bytes 196616 | tf_op jit(solution)/shard_map/ppermute | solution.py:35
  51.0 2.2 %collective-permute-done.10.refs_1_ = bf16[128,256]{1,0:T(8,128)(2,1)S(1)} collective-permute-done((bf16[128,256]{1,0:T(8,128)(2,1)S(1)}, bf16[128,256]{1,0:T(8,128)(2,1)S(1)}, u32[]{:S(2)}, u32[]{:S(2)}) %collective-permute-start.10) | collective-permute-done | bytes 65568 | tf_op jit(solution)/shard_map/ppermute | solution.py:35
  53.2 2.9 %collective-permute-done.9.term_b_ref = bf16[128,256]{1,0:T(8,128)(2,1)S(1)} collective-permute-done((bf16[128,256]{1,0:T(8,128)(2,1)S(1)}, bf16[128,256]{1,0:T(8,128)(2,1)S(1)}, u32[]{:S(2)}, u32[]{:S(2)}) %collective-permute-start.9) | collective-permute-done | bytes 65568 | tf_op jit(solution)/shard_map/ppermute | solution.py:39
  57.8 1.2 %shard_map.167 = (f32[256,256]{1,0:T(8,128)}, f32[256,256]{1,0:T(8,128)}, f32[256,256]{1,0:T(8,128)}, f32[256,256]{1,0:T(8,128)}, f32[256,256]{1,0:T(8,128)}) custom-call(s32[1]{0:T(128)} %bitcast.1.refs_1_.refs_0_, bf16[640,256]{1,0:T(8,128)(2,1)S(1)} %shard_map.166.refs_1_, bf16[640,256]{1,0:T(8,128)(2,1)S(1)} %collective-permute-done.17.refs_2_), custom_call_target="tpu_custom_call" | custom-call | flops 100000000 | tf_op jit(solution)/shard_map/pallas_call | solution.py:22
  (50 shorter events, 7.2 us)
Async XLA Ops:
  0.6 6.0 %copy-start.6 = (bf16[1,256,256]{2,1,0:T(8,128)(2,1)S(1)}, bf16[1,256,256]{2,1,0:T(8,128)(2,1)}, u32[]{:S(2)}) copy-start(bf16[1,256,256]{2,1,0:T(8,128)(2,1)} %param.14) | copy-start | bytes 393220
  1.6 7.2 %collective-permute-start.1 = (bf16[128,256]{1,0:T(8,128)(2,1)S(1)}, bf16[128,256]{1,0:T(8,128)(2,1)S(1)}, u32[]{:S(2)}, u32[]{:S(2)}) collective-permute-start(bf16[128,256]{1,0:T(8,128)(2,1)S(1)} %get-tuple-element.71), channel_id=1, source_target_pairs={{4,0},{8,4},{12,8},{0,12},{5,1},{9,5},{13,9},{1,13},{6,2},{10,6},{... | collective-permute-start | bytes 196616 | tf_op jit(solution)/shard_map/ppermute | solution.py:35
  6.7 6.1 %collective-permute-start = (bf16[128,256]{1,0:T(8,128)(2,1)S(1)}, bf16[128,256]{1,0:T(8,128)(2,1)S(1)}, u32[]{:S(2)}, u32[]{:S(2)}) collective-permute-start(bf16[128,256]{1,0:T(8,128)(2,1)S(1)} %get-tuple-element.72), channel_id=1, source_target_pairs={{12,0},{0,4},{4,8},{8,12},{13,1},{1,5},{5,9},{9,13},{14,2},{2,6},{... | collective-permute-start | bytes 196616 | tf_op jit(solution)/shard_map/ppermute | solution.py:35
  7.3 5.4 %copy-start.5 = (bf16[256,256]{1,0:T(8,128)(2,1)S(1)}, bf16[256,256]{1,0:T(8,128)(2,1)}, u32[]{:S(2)}) copy-start(bf16[256,256]{1,0:T(8,128)(2,1)} %refs_10_.1) | copy-start | bytes 393220
  13.4 6.8 %copy-start.1 = (bf16[256,256]{1,0:T(8,128)(2,1)S(1)}, bf16[256,256]{1,0:T(8,128)(2,1)}, u32[]{:S(2)}) copy-start(bf16[256,256]{1,0:T(8,128)(2,1)} %refs_3_.1) | copy-start | bytes 393220
  13.4 6.8 %copy-start.2 = (bf16[256,256]{1,0:T(8,128)(2,1)S(1)}, bf16[256,256]{1,0:T(8,128)(2,1)}, u32[]{:S(2)}) copy-start(bf16[256,256]{1,0:T(8,128)(2,1)} %refs_4_.3) | copy-start | bytes 393220
  13.4 6.8 %copy-start.3 = (bf16[256,256]{1,0:T(8,128)(2,1)S(1)}, bf16[256,256]{1,0:T(8,128)(2,1)}, u32[]{:S(2)}) copy-start(bf16[256,256]{1,0:T(8,128)(2,1)} %refs_5_.1) | copy-start | bytes 393220
  13.4 6.8 %copy-start.4 = (bf16[256,256]{1,0:T(8,128)(2,1)S(1)}, bf16[256,256]{1,0:T(8,128)(2,1)}, u32[]{:S(2)}) copy-start(bf16[256,256]{1,0:T(8,128)(2,1)} %refs_6_.1) | copy-start | bytes 393220
  14.4 4.7 %collective-permute-start.2 = (bf16[192,256]{1,0:T(8,128)(2,1)S(1)}, bf16[192,256]{1,0:T(8,128)(2,1)S(1)}, u32[]{:S(2)}, u32[]{:S(2)}) collective-permute-start(bf16[192,256]{1,0:T(8,128)(2,1)S(1)} %get-tuple-element.44), channel_id=1, source_target_pairs={{0,4},{4,0},{8,12},{12,8},{1,5},{5,1},{9,13},{13,9},{2,6},{6,2},{1... | collective-permute-start | bytes 294920 | tf_op jit(solution)/shard_map/ppermute | solution.py:79
  14.5 5.7 %collective-permute-start.3 = (bf16[192,256]{1,0:T(8,128)(2,1)S(1)}, bf16[192,256]{1,0:T(8,128)(2,1)S(1)}, u32[]{:S(2)}, u32[]{:S(2)}) collective-permute-start(bf16[192,256]{1,0:T(8,128)(2,1)S(1)} %get-tuple-element.45), channel_id=1, source_target_pairs={{0,8},{4,12},{8,0},{12,4},{1,9},{5,13},{9,1},{13,5},{2,10},{6,14},... | collective-permute-start | bytes 294920 | tf_op jit(solution)/shard_map/ppermute | solution.py:79
  23.7 1.6 %collective-permute-start.12 = (bf16[512,256]{1,0:T(8,128)(2,1)S(1)}, bf16[512,256]{1,0:T(8,128)(2,1)S(1)}, u32[]{:S(2)}, u32[]{:S(2)}) collective-permute-start(bf16[512,256]{1,0:T(8,128)(2,1)S(1)} %get-tuple-element.62), channel_id=1, source_target_pairs={{0,1},{1,0},{2,3},{3,2},{4,5},{5,4},{6,7},{7,6},{8,9},{9,8},{10,11... | collective-permute-start | bytes 786440 | tf_op jit(solution)/shard_map/ppermute | solution.py:39
  25.3 5.6 %collective-permute-start.13 = (bf16[256,256]{1,0:T(8,128)(2,1)S(1)}, bf16[256,256]{1,0:T(8,128)(2,1)S(1)}, u32[]{:S(2)}, u32[]{:S(2)}) collective-permute-start(bf16[256,256]{1,0:T(8,128)(2,1)S(1)} %get-tuple-element.64), channel_id=1, source_target_pairs={{0,2},{1,3},{2,0},{3,1},{4,6},{5,7},{6,4},{7,5},{8,10},{9,11},{10,... | collective-permute-start | bytes 393224 | tf_op jit(solution)/shard_map/ppermute | solution.py:39
  26.9 6.0 %collective-permute-start.4 = (bf16[192,256]{1,0:T(8,128)(2,1)S(1)}, bf16[192,256]{1,0:T(8,128)(2,1)S(1)}, u32[]{:S(2)}, u32[]{:S(2)}) collective-permute-start(bf16[192,256]{1,0:T(8,128)(2,1)S(1)} %get-tuple-element.47), channel_id=1, source_target_pairs={{4,0},{0,4},{12,8},{8,12},{5,1},{1,5},{13,9},{9,13},{6,2},{2,6},{1... | collective-permute-start | bytes 294920 | tf_op jit(solution)/shard_map/ppermute | solution.py:79
  28.7 7.2 %collective-permute-start.5 = (bf16[192,256]{1,0:T(8,128)(2,1)S(1)}, bf16[192,256]{1,0:T(8,128)(2,1)S(1)}, u32[]{:S(2)}, u32[]{:S(2)}) collective-permute-start(bf16[192,256]{1,0:T(8,128)(2,1)S(1)} %get-tuple-element.48), channel_id=1, source_target_pairs={{8,0},{12,4},{0,8},{4,12},{9,1},{13,5},{1,9},{5,13},{10,2},{14,6},... | collective-permute-start | bytes 294920 | tf_op jit(solution)/shard_map/ppermute | solution.py:79
  30.9 6.5 %collective-permute-start.14 = (bf16[256,256]{1,0:T(8,128)(2,1)S(1)}, bf16[256,256]{1,0:T(8,128)(2,1)S(1)}, u32[]{:S(2)}, u32[]{:S(2)}) collective-permute-start(bf16[256,256]{1,0:T(8,128)(2,1)S(1)} %shard_map.163.refs_0_), channel_id=1, source_target_pairs={{0,4},{4,0},{8,12},{12,8},{1,5},{5,1},{9,13},{13,9},{2,6},{6,2},{1... | collective-permute-start | bytes 393224 | tf_op jit(solution)/shard_map/ppermute | solution.py:39
  37.0 1.3 %collective-permute-start.6 = (bf16[128,256]{1,0:T(8,128)(2,1)S(1)}, bf16[128,256]{1,0:T(8,128)(2,1)S(1)}, u32[]{:S(2)}, u32[]{:S(2)}) collective-permute-start(bf16[128,256]{1,0:T(8,128)(2,1)S(1)} %get-tuple-element.55), channel_id=1, source_target_pairs={{0,1},{1,0},{2,3},{3,2},{4,5},{5,4},{6,7},{7,6},{8,9},{9,8},{10,11... | collective-permute-start | bytes 196616 | tf_op jit(solution)/shard_map/ppermute | solution.py:39
  37.5 8.5 %collective-permute-start.15 = (bf16[256,256]{1,0:T(8,128)(2,1)S(1)}, bf16[256,256]{1,0:T(8,128)(2,1)S(1)}, u32[]{:S(2)}, u32[]{:S(2)}) collective-permute-start(bf16[256,256]{1,0:T(8,128)(2,1)S(1)} %shard_map.164.refs_0_), channel_id=1, source_target_pairs={{0,8},{4,12},{8,0},{12,4},{1,9},{5,13},{9,1},{13,5},{2,10},{6,14},... | collective-permute-start | bytes 393224 | tf_op jit(solution)/shard_map/ppermute | solution.py:39
  38.4 4.3 %collective-permute-start.7 = (bf16[128,256]{1,0:T(8,128)(2,1)S(1)}, bf16[128,256]{1,0:T(8,128)(2,1)S(1)}, u32[]{:S(2)}, u32[]{:S(2)}) collective-permute-start(bf16[128,256]{1,0:T(8,128)(2,1)S(1)} %shard_map.157.refs_0_), channel_id=1, source_target_pairs={{0,2},{1,3},{2,0},{3,1},{4,6},{5,7},{6,4},{7,5},{8,10},{9,11},{10,... | collective-permute-start | bytes 196616 | tf_op jit(solution)/shard_map/ppermute | solution.py:39
  42.7 8.1 %collective-permute-start.8 = (bf16[128,256]{1,0:T(8,128)(2,1)S(1)}, bf16[128,256]{1,0:T(8,128)(2,1)S(1)}, u32[]{:S(2)}, u32[]{:S(2)}) collective-permute-start(bf16[128,256]{1,0:T(8,128)(2,1)S(1)} %shard_map.158.refs_0_), channel_id=1, source_target_pairs={{0,4},{4,0},{8,12},{12,8},{1,5},{5,1},{9,13},{13,9},{2,6},{6,2},{1... | collective-permute-start | bytes 196616 | tf_op jit(solution)/shard_map/ppermute | solution.py:39
  46.0 10.1 %collective-permute-start.16 = (bf16[256,256]{1,0:T(8,128)(2,1)S(1)}, bf16[256,256]{1,0:T(8,128)(2,1)S(1)}, u32[]{:S(2)}, u32[]{:S(2)}) collective-permute-start(bf16[256,256]{1,0:T(8,128)(2,1)S(1)} %shard_map.165.own_ref), channel_id=1, source_target_pairs={{0,2},{1,3},{2,0},{3,1},{4,6},{5,7},{6,4},{7,5},{8,10},{9,11},{10,... | collective-permute-start | bytes 393224 | tf_op jit(solution)/shard_map/ppermute | solution.py:39
  47.0 6.1 %collective-permute-start.10 = (bf16[128,256]{1,0:T(8,128)(2,1)S(1)}, bf16[128,256]{1,0:T(8,128)(2,1)S(1)}, u32[]{:S(2)}, u32[]{:S(2)}) collective-permute-start(bf16[128,256]{1,0:T(8,128)(2,1)S(1)} %get-tuple-element.57), channel_id=1, source_target_pairs={{12,0},{0,4},{4,8},{8,12},{13,1},{1,5},{5,9},{9,13},{14,2},{2,6},{... | collective-permute-start | bytes 196616 | tf_op jit(solution)/shard_map/ppermute | solution.py:35
  47.0 6.1 %collective-permute-start.11 = (bf16[128,256]{1,0:T(8,128)(2,1)S(1)}, bf16[128,256]{1,0:T(8,128)(2,1)S(1)}, u32[]{:S(2)}, u32[]{:S(2)}) collective-permute-start(bf16[128,256]{1,0:T(8,128)(2,1)S(1)} %get-tuple-element.58), channel_id=1, source_target_pairs={{4,0},{8,4},{12,8},{0,12},{5,1},{9,5},{13,9},{1,13},{6,2},{10,6},{... | collective-permute-start | bytes 196616 | tf_op jit(solution)/shard_map/ppermute | solution.py:35
  50.9 5.2 %collective-permute-start.9 = (bf16[128,256]{1,0:T(8,128)(2,1)S(1)}, bf16[128,256]{1,0:T(8,128)(2,1)S(1)}, u32[]{:S(2)}, u32[]{:S(2)}) collective-permute-start(bf16[128,256]{1,0:T(8,128)(2,1)S(1)} %shard_map.159.term_a_ref), channel_id=1, source_target_pairs={{0,8},{4,12},{8,0},{12,4},{1,9},{5,13},{9,1},{13,5},{2,10},{6,14},... | collective-permute-start | bytes 196616 | tf_op jit(solution)/shard_map/ppermute | solution.py:39
  56.2 1.7 %collective-permute-start.17 = (bf16[640,256]{1,0:T(8,128)(2,1)S(1)}, bf16[640,256]{1,0:T(8,128)(2,1)S(1)}, u32[]{:S(2)}, u32[]{:S(2)}) collective-permute-start(bf16[640,256]{1,0:T(8,128)(2,1)S(1)} %shard_map.166.refs_1_), channel_id=1, source_target_pairs={{0,1},{1,0},{2,3},{3,2},{4,5},{5,4},{6,7},{7,6},{8,9},{9,8},{10,11... | collective-permute-start | bytes 983048 | tf_op jit(solution)/shard_map/ppermute | solution.py:39
  (4 other events, 7.4 us)

commit v4 on v3

--- a/solution.py
+++ b/solution.py
@@ -69,6 +69,10 @@
         assert sectors % 2 == 0
         self.hops = sorted((o ^ 1 for o in range(-self.radius, self.radius + 1)), key=abs)
 
+    def seat(self, c, w):
+        jet = sum((c >= t * self.cap).astype(jnp.int32) for t in range(1, JET_DEV))
+        return jnp.where(c < self.used, c + jet * (self.slots - self.cap) + w * self.cap, -1)
+
     def routed(self, parts, back=False):
         n = self.sectors
         moved = []
@@ -80,8 +84,16 @@
         return moved
 
 
-def index_kernel(plan, where_ref, cell_ref, jet_ref, cot_ref, pick_ref, place_ref, *chunk_refs):
+def index_kernel(plan, where_ref, nbr_ref, cell_ref, jet_ref, cot_ref, pick_ref, place_ref, times_ref, *chunk_refs):
     sector = where_ref[0]
+    entries = plan.blocks + 2
+    line = iota(times_ref.shape, 0)
+    times = jnp.zeros(times_ref.shape, FULL)
+    for b in range(plan.blocks):
+        for j in range(entries):
+            share = sum((nbr_ref[b, k] == j).astype(FULL) for k in range(NBRS)) * (1.0 / NBRS)
+            times = jnp.where(line == b * entries + j, share, times)
+    times_ref[...] = times
     count, members = plan.chunk, plan.members
     jets = jet_ref[...]
     hop = lax.bitwise_xor(lax.shift_right_logical(jets, 2), 1) - sector
@@ -112,7 +124,7 @@
         chunk_refs[w][...] = jnp.where(mask_row, present, part).astype(LOW)
 
 
-def hidden_kernel(plan, nbr_ref, cell_ref, low_ref, high_ref, weight_ref, pick_ref, *refs):
+def hidden_kernel(plan, times_ref, cell_ref, low_ref, high_ref, weight_ref, pick_ref, *refs):
     blocks = plan.blocks
     cot_refs, chunk_refs = refs[: plan.window], refs[plan.window + 3 :]
     gathered_ref, before_ref, hidden_ref = refs[plan.window : plan.window + 3]
@@ -122,8 +134,9 @@
     for b in range(blocks):
         total = None
         for j, entry in enumerate(entries):
-            times = sum((nbr_ref[b, k] == j).astype(FULL) for k in range(NBRS)) * (1.0 / NBRS)
-            total = entry * times if total is None else total + entry * times
+            line = b * len(entries) + j
+            part = entry * times_ref[line : line + 1, :]
+            total = part if total is None else total + part
         gathered_ref[b * BLOCK : (b + 1) * BLOCK, :] = total.astype(LOW)
     before = mm(gathered_ref[...], weight_ref[...])
     before_ref[...] = before
@@ -139,20 +152,14 @@
 def attend_kernel(plan, *refs):
     window, count, slots, owned, channels = plan.window, plan.chunk, plan.slots, plan.owned, plan.channels
     chunk_refs = refs[:window]
-    wq_ref, wk_ref, wv_ref, wo_ref = refs[window : window + 4]
-    back_refs = refs[window + 4 : 2 * window + 4]
-    (parts_ref,) = refs[2 * window + 4 :]
+    wq_ref, wk_ref, wv_ref, wo_ref, parts_ref = refs[window:]
     head = channels // HEADS
     scale = 1.0 / math.sqrt(head)
-
-    def seat(c, w):
-        jet = sum((c >= t * plan.cap).astype(jnp.int32) for t in range(1, JET_DEV))
-        return jnp.where(c < plan.used, c + jet * (slots - plan.cap) + w * plan.cap, -1)
 
     members = upstream = present = None
     base = plan.used // 16 * 16
     for w in range(window):
-        hot = jnp.where(iota((owned, count), 0) == seat(iota((owned, count), 1), w), 1.0, 0.0)
+        hot = jnp.where(iota((owned, count), 0) == plan.seat(iota((owned, count), 1), w), 1.0, 0.0)
         low = hot.astype(LOW)
         m, u = mm(low, chunk_refs[w][:count, :]), mm(low, chunk_refs[w][count:, :])
         tail = chunk_refs[w][count + base : count + base + 16, :].astype(FULL)
@@ -198,19 +205,23 @@
         grad_k.append(mm(grad_scores, q_wide).astype(LOW))
         grad_v.append(mm(chances_low, g_wide).astype(LOW))
     mixture, grad_q, grad_k, grad_v = [jnp.concatenate(x, axis=0) for x in (mixture, grad_q, grad_k, grad_v)]
-    attended = mm(mixture, wo_ref[...]).astype(LOW)
-    grad_members = mm_nt(grad_q, wq_ref[...]) + mm_nt(grad_k, wk_ref[...]) + mm_nt(grad_v, wv_ref[...])
-    grad_members = grad_members.astype(LOW)
-    for w in range(window):
-        hot = jnp.where(seat(iota((count, owned), 0), w) == iota((count, owned), 1), 1.0, 0.0).astype(LOW)
-        back_refs[w][:count, :] = mm(hot, attended).astype(LOW)
-        back_refs[w][count:, :] = mm(hot, grad_members).astype(LOW)
     parts_ref[0] = members
     parts_ref[1] = upstream
     parts_ref[2] = mixture
     parts_ref[3] = grad_q
     parts_ref[4] = grad_k
     parts_ref[5] = grad_v
+
+
+def back_kernel(plan, parts_ref, wq_ref, wk_ref, wv_ref, wo_ref, *back_refs):
+    count, owned = plan.chunk, plan.owned
+    attended = mm(parts_ref[2], wo_ref[...]).astype(LOW)
+    grad_members = mm_nt(parts_ref[3], wq_ref[...]) + mm_nt(parts_ref[4], wk_ref[...]) + mm_nt(parts_ref[5], wv_ref[...])
+    grad_members = grad_members.astype(LOW)
+    for w in range(plan.window):
+        hot = jnp.where(plan.seat(iota((count, owned), 0), w) == iota((count, owned), 1), 1.0, 0.0).astype(LOW)
+        back_refs[w][:count, :] = mm(hot, attended).astype(LOW)
+        back_refs[w][count:, :] = mm(hot, grad_members).astype(LOW)
 
 
 def term_kernel(channels, bit_ref, parts_ref, send_ref, keep_ref):
@@ -223,7 +234,7 @@
             ref[t * channels : (t + 1) * channels, :] = mm_tn(left, right).astype(ref.dtype)
 
 
-def return_kernel(plan, nbr_ref, bit_ref, *refs):
+def return_kernel(plan, bit_ref, times_ref, *refs):
     window, count = plan.window, plan.chunk
     back_refs = refs[:window]
     place_ref, hidden_ref, cot_ref, before_ref, gathered_ref, weight_ref = refs[window : window + 6]
@@ -243,8 +254,8 @@
     def extended(j):
         total = None
         for b in range(plan.blocks):
-            times = sum((nbr_ref[b, k] == j).astype(FULL) for k in range(NBRS)) * (1.0 / NBRS)
-            part = grad_gathered[b * BLOCK : (b + 1) * BLOCK, :] * times
+            line = b * (plan.blocks + 2) + j
+            part = grad_gathered[b * BLOCK : (b + 1) * BLOCK, :] * times_ref[line : line + 1, :]
             total = part if total is None else total + part
         return total.astype(LOW)
 
@@ -325,10 +336,12 @@
     low = shifted(cells[per_device - BLOCK :], "phi", 1)
     high = shifted(cells[:BLOCK], "phi", -1)
     total = window * chunk
-    pick, put, *cot_chunks = call(
+    lines = -(-plan.blocks * (plan.blocks + 2) // 8) * 8
+    pick, put, times, *cot_chunks = call(
         lambda *refs: index_kernel(plan, *refs),
-        [((total, per_device), LOW), ((per_device, total), LOW)] + [((chunk, channels), LOW)] * window,
-        [place],
+        [((total, per_device), LOW), ((per_device, total), LOW), ((lines, channels), FULL)]
+        + [((chunk, channels), LOW)] * window,
+        [place, nbrs],
         [member_cell.reshape(1, members_dev), member_jet.reshape(1, members_dev), cot],
         micros=0.5,
     )
@@ -336,18 +349,22 @@
         lambda *refs: hidden_kernel(plan, *refs),
         [((per_device, channels), LOW), ((per_device, channels), FULL), ((per_device, channels), LOW)]
         + [((2 * chunk, channels), LOW)] * window,
-        [nbrs],
-        [cells, low, high, message_weight, pick, *cot_chunks],
+        [],
+        [times, cells, low, high, message_weight, pick, *cot_chunks],
         micros=1.0,
     )
 
     chunks = plan.routed(chunks)
-    *backs, parts = call(
-        lambda *refs: attend_kernel(plan, *refs),
-        [((2 * chunk, channels), LOW)] * window + [((6, plan.owned, channels), LOW)],
+    weights = [query_weight, key_weight, value_weight, output_weight]
+    (parts,) = call(
+        lambda *refs: attend_kernel(plan, *refs), [((6, plan.owned, channels), LOW)], [], [*chunks, *weights], micros=2.5
+    )
+    backs = call(
+        lambda *refs: back_kernel(plan, *refs),
+        [((2 * chunk, channels), LOW)] * window,
         [],
-        [*chunks, query_weight, key_weight, value_weight, output_weight],
-        micros=3.0,
+        [parts, *weights],
+        micros=0.7,
     )
     backs = plan.routed(backs, back=True)
     core, across = [((lax.axis_index("ev") >> b) & 1).astype(jnp.int32).reshape(1) for b in range(2)]
@@ -371,8 +388,8 @@
             ((half, channels), LOW),
             ((half, channels), FULL),
         ],
-        [nbrs, core],
-        [*backs, put, hidden, cot, before, gathered, message_weight],
+        [core],
+        [times, *backs, put, hidden, cot, before, gathered, message_weight],
         [pltpu.VMEM((2, total, channels), LOW), pltpu.VMEM((2, half, channels), FULL)],
         micros=4.0,
     )
@@ -389,6 +406,8 @@
     while mask < plan.sectors:
         a_came = swapped(a_own, "phi", mask)
         m_own = added(half, m_own, m_came)
+        if 2 * mask == plan.sectors:
+            m_own = lax.optimization_barrier((m_own, from_lower, from_upper))[0]
         m_came = swapped(m_own, "phi", mask)
         a_own = added(channels, a_own, a_came)
         mask *= 2

time: 59.2 us -> 56.4 us (0.953)
  waiting for transfers between devices: 27.2 us -> 23.4 us
  starting transfers between devices: 20.1 us -> 22.1 us
  local copies, waits for them, and re-layouts: 3.6 us -> 2.95 us
    ppermute x4, waiting for transfers between devices: 7.12 us -> 2.86 us  [shifted(): lax.ppermute(block, axis, [((i - distance) % count, i) for i in range(cou...]
    ppermute x4, starting transfers between devices: 3.82 us -> 5.83 us  [routed(): moved.append(lax.ppermute(part, 'phi', route) if hop else part)]
    unnamed x22, local copies, waits for them, and re-layouts: 2.68 us -> 2.03 us
    pallas_call x15 -> x16, Pallas kernels: 7.43 us -> 7 us  [call(): pl.pallas_call(body, out_shape=[kind(shape, dtype) for shape, dtype in ou...]
  transfers between devices with their start and end apart: 18 -> 18, of which waited for: 14 -> 13; matrix products, arithmetic and copies ran while one was open for 2% -> 2% of each run, Pallas kernels for 3% -> 4%
where the time goes in v4:
time: 56.4 us; the launch traced here: 56.3 us
  waiting for transfers between devices  23.4 us (41%)
  starting transfers between devices  22.1 us (39%)
  Pallas kernels  7 us (12%)
  local copies, waits for them, and re-layouts  2.95 us (5%)
  between operations  0.81 us (1%)
    ppermute x10, waiting for transfers between devices, swapped(): lax.ppermute(block, axis, [(i, i ^ mask) for i in range(lax.axis_size(axi...  12.7 us
    ppermute x4, starting transfers between devices, shifted(): lax.ppermute(block, axis, [((i - distance) % count, i) for i in range(cou...  8.99 us
    ppermute x4, waiting for transfers between devices, routed(): moved.append(lax.ppermute(part, 'phi', route) if hop else part)  7.82 us
    ppermute x10, starting transfers between devices, swapped(): lax.ppermute(block, axis, [(i, i ^ mask) for i in range(lax.axis_size(axi...  7.31 us
    pallas_call x16, Pallas kernels, call(): pl.pallas_call(body, out_shape=[kind(shape, dtype) for shape, dtype in ou...  7 us
    ppermute x4, starting transfers between devices, routed(): moved.append(lax.ppermute(part, 'phi', route) if hop else part)  5.83 us
    ppermute x4, waiting for transfers between devices, shifted(): lax.ppermute(block, axis, [((i - distance) % count, i) for i in range(cou...  2.86 us
    unnamed x22, local copies, waits for them, and re-layouts  2.03 us
  transfers between devices with their start and end apart: 18, of which 13 were waited for; matrix products, arithmetic and copies ran while one was open for 2% of the time, Pallas kernels for 4%

profile of v4, /device:TPU:0, one launch (start us, length us, event | category | flops | bytes accessed | tf_op | source)
XLA Modules:
  0.0 56.3 jit_solution(6801082247168102970)
XLA Ops:
  0.6 0.9 %slice_bitcast_fusion = (bf16[128,256]{1,0:T(8,128)(2,1)S(1)}, bf16[128,256]{1,0:T(8,128)(2,1)S(1)}) fusion(bf16[1,256,256]{2,1,0:T(8,128)(2,1)} %param.10), kind=kLoop, calls=%fused_computation | loop fusion | bytes 262144 | tf_op jit(solution)/shard_map/slice | solution.py:337
  1.6 3.1 %collective-permute-start = (bf16[128,256]{1,0:T(8,128)(2,1)S(1)}, bf16[128,256]{1,0:T(8,128)(2,1)S(1)}, u32[]{:S(2)}, u32[]{:S(2)}) collective-permute-start(bf16[128,256]{1,0:T(8,128)(2,1)S(1)} %get-tuple-element.74), channel_id=1, source_target_pairs={{12,0},{0,4},{4,8},{8,12},{13,1},{1,5},{5,9},{9,13},{14,2},{2,6},{... | collective-permute-start | bytes 196616 | tf_op jit(solution)/shard_map/ppermute | solution.py:35
  4.6 2.1 %collective-permute-start.1 = (bf16[128,256]{1,0:T(8,128)(2,1)S(1)}, bf16[128,256]{1,0:T(8,128)(2,1)S(1)}, u32[]{:S(2)}, u32[]{:S(2)}) collective-permute-start(bf16[128,256]{1,0:T(8,128)(2,1)S(1)} %get-tuple-element.73), channel_id=1, source_target_pairs={{4,0},{8,4},{12,8},{0,12},{5,1},{9,5},{13,9},{1,13},{6,2},{10,6},{... | collective-permute-start | bytes 196616 | tf_op jit(solution)/shard_map/ppermute | solution.py:35
  7.4 1.0 %shard_map.153 = (bf16[288,256]{1,0:T(8,128)(2,1)S(1)}, bf16[256,288]{1,0:T(8,128)(2,1)S(1)}, f32[8,256]{1,0:T(8,128)S(1)}, bf16[96,256]{1,0:T(8,128)(2,1)S(1)},...) custom-call(s32[1]{0:T(128)} %bitcast.1.refs_0_, s32[2,4]{1,0:T(2,128)S(1)} %bitcast.18, ...), custom_call_target="tpu_custom_call" | custom-call | flops 500000000 | tf_op jit(solution)/shard_map/pallas_call | solution.py:22
  10.1 1.2 %collective-permute-start.2 = (bf16[192,256]{1,0:T(8,128)(2,1)S(1)}, bf16[192,256]{1,0:T(8,128)(2,1)S(1)}, u32[]{:S(2)}, u32[]{:S(2)}) collective-permute-start(bf16[192,256]{1,0:T(8,128)(2,1)S(1)} %get-tuple-element.46), channel_id=1, source_target_pairs={{0,4},{4,0},{8,12},{12,8},{1,5},{5,1},{9,13},{13,9},{2,6},{6,2},{1... | collective-permute-start | bytes 294920 | tf_op jit(solution)/shard_map/ppermute | solution.py:83
  11.3 2.6 %collective-permute-start.3 = (bf16[192,256]{1,0:T(8,128)(2,1)S(1)}, bf16[192,256]{1,0:T(8,128)(2,1)S(1)}, u32[]{:S(2)}, u32[]{:S(2)}) collective-permute-start(bf16[192,256]{1,0:T(8,128)(2,1)S(1)} %get-tuple-element.47), channel_id=1, source_target_pairs={{0,8},{4,12},{8,0},{12,4},{1,9},{5,13},{9,1},{13,5},{2,10},{6,14},... | collective-permute-start | bytes 294920 | tf_op jit(solution)/shard_map/ppermute | solution.py:83
  13.9 0.9 %collective-permute-done.2.refs_1_ = bf16[192,256]{1,0:T(8,128)(2,1)S(1)} collective-permute-done((bf16[192,256]{1,0:T(8,128)(2,1)S(1)}, bf16[192,256]{1,0:T(8,128)(2,1)S(1)}, u32[]{:S(2)}, u32[]{:S(2)}) %collective-permute-start.2) | collective-permute-done | bytes 98336 | tf_op jit(solution)/shard_map/ppermute | solution.py:83
  14.9 3.3 %collective-permute-done.3.refs_2_ = bf16[192,256]{1,0:T(8,128)(2,1)S(1)} collective-permute-done((bf16[192,256]{1,0:T(8,128)(2,1)S(1)}, bf16[192,256]{1,0:T(8,128)(2,1)S(1)}, u32[]{:S(2)}, u32[]{:S(2)}) %collective-permute-start.3) | collective-permute-done | bytes 98336 | tf_op jit(solution)/shard_map/ppermute | solution.py:83
  18.2 2.6 %shard_map.155.refs_0_.refs_1_ = bf16[6,256,256]{2,1,0:T(8,128)(2,1)S(1)} custom-call(bf16[192,256]{1,0:T(8,128)(2,1)S(1)} %get-tuple-element.45.refs_0_, bf16[192,256]{1,0:T(8,128)(2,1)S(1)} %collective-permute-done.2.refs_1_, bf16[192,256]{1,0:T(8,128)(2,1)S(1)} %collective-permute-done.3.refs_2_, bf16[256,256]{1,0:T(8,128)(2,1)S(1)} %copy-done.1, ...), custom_call_target="tpu_custom_call" | custom-call | flops 2500000000 | tf_op jit(solution)/shard_map/pallas_call | solution.py:22
  21.2 1.5 %collective-permute-done.12.came_ref = bf16[512,256]{1,0:T(8,128)(2,1)S(1)} collective-permute-done((bf16[512,256]{1,0:T(8,128)(2,1)S(1)}, bf16[512,256]{1,0:T(8,128)(2,1)S(1)}, u32[]{:S(2)}, u32[]{:S(2)}) %collective-permute-start.12) | collective-permute-done | bytes 262176 | tf_op jit(solution)/shard_map/ppermute | solution.py:39
  22.8 1.5 %collective-permute-start.13 = (bf16[256,256]{1,0:T(8,128)(2,1)S(1)}, bf16[256,256]{1,0:T(8,128)(2,1)S(1)}, u32[]{:S(2)}, u32[]{:S(2)}) collective-permute-start(bf16[256,256]{1,0:T(8,128)(2,1)S(1)} %get-tuple-element.66), channel_id=1, source_target_pairs={{0,2},{1,3},{2,0},{3,1},{4,6},{5,7},{6,4},{7,5},{8,10},{9,11},{10,... | collective-permute-start | bytes 393224 | tf_op jit(solution)/shard_map/ppermute | solution.py:39
  25.0 1.9 %collective-permute-start.5 = (bf16[192,256]{1,0:T(8,128)(2,1)S(1)}, bf16[192,256]{1,0:T(8,128)(2,1)S(1)}, u32[]{:S(2)}, u32[]{:S(2)}) collective-permute-start(bf16[192,256]{1,0:T(8,128)(2,1)S(1)} %get-tuple-element.50), channel_id=1, source_target_pairs={{8,0},{12,4},{0,8},{4,12},{9,1},{13,5},{1,9},{5,13},{10,2},{14,6},... | collective-permute-start | bytes 294920 | tf_op jit(solution)/shard_map/ppermute | solution.py:83
  26.9 1.4 %collective-permute-done.13.refs_1_ = bf16[256,256]{1,0:T(8,128)(2,1)S(1)} collective-permute-done((bf16[256,256]{1,0:T(8,128)(2,1)S(1)}, bf16[256,256]{1,0:T(8,128)(2,1)S(1)}, u32[]{:S(2)}, u32[]{:S(2)}) %collective-permute-start.13) | collective-permute-done | bytes 131104 | tf_op jit(solution)/shard_map/ppermute | solution.py:39
  28.7 3.6 %collective-permute-done.4.refs_3_ = bf16[192,256]{1,0:T(8,128)(2,1)S(1)} collective-permute-done((bf16[192,256]{1,0:T(8,128)(2,1)S(1)}, bf16[192,256]{1,0:T(8,128)(2,1)S(1)}, u32[]{:S(2)}, u32[]{:S(2)}) %collective-permute-start.4) | collective-permute-done | bytes 98336 | tf_op jit(solution)/shard_map/ppermute | solution.py:83
  32.8 1.6 %collective-permute-done.14.refs_1_ = bf16[256,256]{1,0:T(8,128)(2,1)S(1)} collective-permute-done((bf16[256,256]{1,0:T(8,128)(2,1)S(1)}, bf16[256,256]{1,0:T(8,128)(2,1)S(1)}, u32[]{:S(2)}, u32[]{:S(2)}) %collective-permute-start.14) | collective-permute-done | bytes 131104 | tf_op jit(solution)/shard_map/ppermute | solution.py:39
  34.5 1.7 %collective-permute-start.15 = (bf16[256,256]{1,0:T(8,128)(2,1)S(1)}, bf16[256,256]{1,0:T(8,128)(2,1)S(1)}, u32[]{:S(2)}, u32[]{:S(2)}) collective-permute-start(bf16[256,256]{1,0:T(8,128)(2,1)S(1)} %shard_map.165.refs_0_), channel_id=1, source_target_pairs={{0,8},{4,12},{8,0},{12,4},{1,9},{5,13},{9,1},{13,5},{2,10},{6,14},... | collective-permute-start | bytes 393224 | tf_op jit(solution)/shard_map/ppermute | solution.py:39
  36.6 3.9 %collective-permute-done.7.refs_1_ = bf16[128,256]{1,0:T(8,128)(2,1)S(1)} collective-permute-done((bf16[128,256]{1,0:T(8,128)(2,1)S(1)}, bf16[128,256]{1,0:T(8,128)(2,1)S(1)}, u32[]{:S(2)}, u32[]{:S(2)}) %collective-permute-start.7) | collective-permute-done | bytes 65568 | tf_op jit(solution)/shard_map/ppermute | solution.py:39
  40.5 1.5 %collective-permute-start.8 = (bf16[128,256]{1,0:T(8,128)(2,1)S(1)}, bf16[128,256]{1,0:T(8,128)(2,1)S(1)}, u32[]{:S(2)}, u32[]{:S(2)}) collective-permute-start(bf16[128,256]{1,0:T(8,128)(2,1)S(1)} %shard_map.159.refs_0_), channel_id=1, source_target_pairs={{0,4},{4,0},{8,12},{12,8},{1,5},{5,1},{9,13},{13,9},{2,6},{6,2},{1... | collective-permute-start | bytes 196616 | tf_op jit(solution)/shard_map/ppermute | solution.py:39
  42.6 3.2 %collective-permute-start.10 = (bf16[128,256]{1,0:T(8,128)(2,1)S(1)}, bf16[128,256]{1,0:T(8,128)(2,1)S(1)}, u32[]{:S(2)}, u32[]{:S(2)}) collective-permute-start(bf16[128,256]{1,0:T(8,128)(2,1)S(1)} %get-tuple-element.59), channel_id=1, source_target_pairs={{4,0},{8,4},{12,8},{0,12},{5,1},{9,5},{13,9},{1,13},{6,2},{10,6},{... | collective-permute-start | bytes 196616 | tf_op jit(solution)/shard_map/ppermute | solution.py:35
  46.5 1.6 %collective-permute-done.9.refs_1_ = bf16[128,256]{1,0:T(8,128)(2,1)S(1)} collective-permute-done((bf16[128,256]{1,0:T(8,128)(2,1)S(1)}, bf16[128,256]{1,0:T(8,128)(2,1)S(1)}, u32[]{:S(2)}, u32[]{:S(2)}) %collective-permute-start.9) | collective-permute-done | bytes 65568 | tf_op jit(solution)/shard_map/ppermute | solution.py:35
  48.1 1.2 %collective-permute-start.11 = (bf16[128,256]{1,0:T(8,128)(2,1)S(1)}, bf16[128,256]{1,0:T(8,128)(2,1)S(1)}, u32[]{:S(2)}, u32[]{:S(2)}) collective-permute-start(bf16[128,256]{1,0:T(8,128)(2,1)S(1)} %shard_map.160.term_a_ref), channel_id=1, source_target_pairs={{0,8},{4,12},{8,0},{12,4},{1,9},{5,13},{9,1},{13,5},{2,10},{6,14},... | collective-permute-start | bytes 196616 | tf_op jit(solution)/shard_map/ppermute | solution.py:39
  49.4 3.9 %collective-permute-done.11.term_b_ref = bf16[128,256]{1,0:T(8,128)(2,1)S(1)} collective-permute-done((bf16[128,256]{1,0:T(8,128)(2,1)S(1)}, bf16[128,256]{1,0:T(8,128)(2,1)S(1)}, u32[]{:S(2)}, u32[]{:S(2)}) %collective-permute-start.11) | collective-permute-done | bytes 65568 | tf_op jit(solution)/shard_map/ppermute | solution.py:39
  53.4 0.7 %copy.17 = bf16[1,256,256]{2,1,0:T(8,128)(2,1)} copy(bf16[1,256,256]{2,1,0:T(8,128)(2,1)S(1)} %bitcast.14) | data formatting | bytes 262144
  55.0 1.2 %shard_map.168 = (f32[256,256]{1,0:T(8,128)}, f32[256,256]{1,0:T(8,128)}, f32[256,256]{1,0:T(8,128)}, f32[256,256]{1,0:T(8,128)}, f32[256,256]{1,0:T(8,128)}) custom-call(s32[1]{0:T(128)} %bitcast.refs_0_, bf16[640,256]{1,0:T(8,128)(2,1)S(1)} %shard_map.167.refs_1_, bf16[640,256]{1,0:T(8,128)(2,1)S(1)} %collective-permute-done.17.refs_2_), custom_call_target="tpu_custom_call" | custom-call | flops 100000000 | tf_op jit(solution)/shard_map/pallas_call | solution.py:22
  (51 shorter events, 7.3 us)
Async XLA Ops:
  0.6 6.1 %copy-start.5 = (bf16[1,256,256]{2,1,0:T(8,128)(2,1)S(1)}, bf16[1,256,256]{2,1,0:T(8,128)(2,1)}, u32[]{:S(2)}) copy-start(bf16[1,256,256]{2,1,0:T(8,128)(2,1)} %param.14) | copy-start | bytes 393220
  1.6 7.5 %collective-permute-start = (bf16[128,256]{1,0:T(8,128)(2,1)S(1)}, bf16[128,256]{1,0:T(8,128)(2,1)S(1)}, u32[]{:S(2)}, u32[]{:S(2)}) collective-permute-start(bf16[128,256]{1,0:T(8,128)(2,1)S(1)} %get-tuple-element.74), channel_id=1, source_target_pairs={{12,0},{0,4},{4,8},{8,12},{13,1},{1,5},{5,9},{9,13},{14,2},{2,6},{... | collective-permute-start | bytes 196616 | tf_op jit(solution)/shard_map/ppermute | solution.py:35
  4.6 5.0 %collective-permute-start.1 = (bf16[128,256]{1,0:T(8,128)(2,1)S(1)}, bf16[128,256]{1,0:T(8,128)(2,1)S(1)}, u32[]{:S(2)}, u32[]{:S(2)}) collective-permute-start(bf16[128,256]{1,0:T(8,128)(2,1)S(1)} %get-tuple-element.73), channel_id=1, source_target_pairs={{4,0},{8,4},{12,8},{0,12},{5,1},{9,5},{13,9},{1,13},{6,2},{10,6},{... | collective-permute-start | bytes 196616 | tf_op jit(solution)/shard_map/ppermute | solution.py:35
  7.4 2.2 %copy-start.6 = (bf16[256,256]{1,0:T(8,128)(2,1)S(1)}, bf16[256,256]{1,0:T(8,128)(2,1)}, u32[]{:S(2)}) copy-start(bf16[256,256]{1,0:T(8,128)(2,1)} %refs_10_.1) | copy-start | bytes 393220
  9.6 8.5 %copy-start.1 = (bf16[256,256]{1,0:T(8,128)(2,1)S(1)}, bf16[256,256]{1,0:T(8,128)(2,1)}, u32[]{:S(2)}) copy-start(bf16[256,256]{1,0:T(8,128)(2,1)} %refs_1_.1) | copy-start | bytes 393220
  9.6 8.5 %copy-start.2 = (bf16[256,256]{1,0:T(8,128)(2,1)S(1)}, bf16[256,256]{1,0:T(8,128)(2,1)}, u32[]{:S(2)}) copy-start(bf16[256,256]{1,0:T(8,128)(2,1)} %refs_2_.3) | copy-start | bytes 393220
  9.6 8.5 %copy-start.3 = (bf16[256,256]{1,0:T(8,128)(2,1)S(1)}, bf16[256,256]{1,0:T(8,128)(2,1)}, u32[]{:S(2)}) copy-start(bf16[256,256]{1,0:T(8,128)(2,1)} %refs_3_.3) | copy-start | bytes 393220
  9.6 8.5 %copy-start.4 = (bf16[256,256]{1,0:T(8,128)(2,1)S(1)}, bf16[256,256]{1,0:T(8,128)(2,1)}, u32[]{:S(2)}) copy-start(bf16[256,256]{1,0:T(8,128)(2,1)} %refs_4_.5) | copy-start | bytes 393220
  10.1 4.8 %collective-permute-start.2 = (bf16[192,256]{1,0:T(8,128)(2,1)S(1)}, bf16[192,256]{1,0:T(8,128)(2,1)S(1)}, u32[]{:S(2)}, u32[]{:S(2)}) collective-permute-start(bf16[192,256]{1,0:T(8,128)(2,1)S(1)} %get-tuple-element.46), channel_id=1, source_target_pairs={{0,4},{4,0},{8,12},{12,8},{1,5},{5,1},{9,13},{13,9},{2,6},{6,2},{1... | collective-permute-start | bytes 294920 | tf_op jit(solution)/shard_map/ppermute | solution.py:83
  11.3 6.9 %collective-permute-start.3 = (bf16[192,256]{1,0:T(8,128)(2,1)S(1)}, bf16[192,256]{1,0:T(8,128)(2,1)S(1)}, u32[]{:S(2)}, u32[]{:S(2)}) collective-permute-start(bf16[192,256]{1,0:T(8,128)(2,1)S(1)} %get-tuple-element.47), channel_id=1, source_target_pairs={{0,8},{4,12},{8,0},{12,4},{1,9},{5,13},{9,1},{13,5},{2,10},{6,14},... | collective-permute-start | bytes 294920 | tf_op jit(solution)/shard_map/ppermute | solution.py:83
  21.1 1.6 %collective-permute-start.12 = (bf16[512,256]{1,0:T(8,128)(2,1)S(1)}, bf16[512,256]{1,0:T(8,128)(2,1)S(1)}, u32[]{:S(2)}, u32[]{:S(2)}) collective-permute-start(bf16[512,256]{1,0:T(8,128)(2,1)S(1)} %get-tuple-element.64), channel_id=1, source_target_pairs={{0,1},{1,0},{2,3},{3,2},{4,5},{5,4},{6,7},{7,6},{8,9},{9,8},{10,11... | collective-permute-start | bytes 786440 | tf_op jit(solution)/shard_map/ppermute | solution.py:39
  22.8 5.6 %collective-permute-start.13 = (bf16[256,256]{1,0:T(8,128)(2,1)S(1)}, bf16[256,256]{1,0:T(8,128)(2,1)S(1)}, u32[]{:S(2)}, u32[]{:S(2)}) collective-permute-start(bf16[256,256]{1,0:T(8,128)(2,1)S(1)} %get-tuple-element.66), channel_id=1, source_target_pairs={{0,2},{1,3},{2,0},{3,1},{4,6},{5,7},{6,4},{7,5},{8,10},{9,11},{10,... | collective-permute-start | bytes 393224 | tf_op jit(solution)/shard_map/ppermute | solution.py:39
  24.9 7.3 %collective-permute-start.4 = (bf16[192,256]{1,0:T(8,128)(2,1)S(1)}, bf16[192,256]{1,0:T(8,128)(2,1)S(1)}, u32[]{:S(2)}, u32[]{:S(2)}) collective-permute-start(bf16[192,256]{1,0:T(8,128)(2,1)S(1)} %get-tuple-element.49), channel_id=1, source_target_pairs={{4,0},{0,4},{12,8},{8,12},{5,1},{1,5},{13,9},{9,13},{6,2},{2,6},{1... | collective-permute-start | bytes 294920 | tf_op jit(solution)/shard_map/ppermute | solution.py:83
  25.0 7.2 %collective-permute-start.5 = (bf16[192,256]{1,0:T(8,128)(2,1)S(1)}, bf16[192,256]{1,0:T(8,128)(2,1)S(1)}, u32[]{:S(2)}, u32[]{:S(2)}) collective-permute-start(bf16[192,256]{1,0:T(8,128)(2,1)S(1)} %get-tuple-element.50), channel_id=1, source_target_pairs={{8,0},{12,4},{0,8},{4,12},{9,1},{13,5},{1,9},{5,13},{10,2},{14,6},... | collective-permute-start | bytes 294920 | tf_op jit(solution)/shard_map/ppermute | solution.py:83
  28.4 6.1 %collective-permute-start.14 = (bf16[256,256]{1,0:T(8,128)(2,1)S(1)}, bf16[256,256]{1,0:T(8,128)(2,1)S(1)}, u32[]{:S(2)}, u32[]{:S(2)}) collective-permute-start(bf16[256,256]{1,0:T(8,128)(2,1)S(1)} %shard_map.164.refs_0_), channel_id=1, source_target_pairs={{0,4},{4,0},{8,12},{12,8},{1,5},{5,1},{9,13},{13,9},{2,6},{6,2},{1... | collective-permute-start | bytes 393224 | tf_op jit(solution)/shard_map/ppermute | solution.py:39
  32.7 3.4 %collective-permute-start.6 = (bf16[128,256]{1,0:T(8,128)(2,1)S(1)}, bf16[128,256]{1,0:T(8,128)(2,1)S(1)}, u32[]{:S(2)}, u32[]{:S(2)}) collective-permute-start(bf16[128,256]{1,0:T(8,128)(2,1)S(1)} %get-tuple-element.57), channel_id=1, source_target_pairs={{0,1},{1,0},{2,3},{3,2},{4,5},{5,4},{6,7},{7,6},{8,9},{9,8},{10,11... | collective-permute-start | bytes 196616 | tf_op jit(solution)/shard_map/ppermute | solution.py:39
  34.5 11.3 %collective-permute-start.15 = (bf16[256,256]{1,0:T(8,128)(2,1)S(1)}, bf16[256,256]{1,0:T(8,128)(2,1)S(1)}, u32[]{:S(2)}, u32[]{:S(2)}) collective-permute-start(bf16[256,256]{1,0:T(8,128)(2,1)S(1)} %shard_map.165.refs_0_), channel_id=1, source_target_pairs={{0,8},{4,12},{8,0},{12,4},{1,9},{5,13},{9,1},{13,5},{2,10},{6,14},... | collective-permute-start | bytes 393224 | tf_op jit(solution)/shard_map/ppermute | solution.py:39
  36.2 4.3 %collective-permute-start.7 = (bf16[128,256]{1,0:T(8,128)(2,1)S(1)}, bf16[128,256]{1,0:T(8,128)(2,1)S(1)}, u32[]{:S(2)}, u32[]{:S(2)}) collective-permute-start(bf16[128,256]{1,0:T(8,128)(2,1)S(1)} %shard_map.158.refs_0_), channel_id=1, source_target_pairs={{0,2},{1,3},{2,0},{3,1},{4,6},{5,7},{6,4},{7,5},{8,10},{9,11},{10,... | collective-permute-start | bytes 196616 | tf_op jit(solution)/shard_map/ppermute | solution.py:39
  40.5 5.9 %collective-permute-start.8 = (bf16[128,256]{1,0:T(8,128)(2,1)S(1)}, bf16[128,256]{1,0:T(8,128)(2,1)S(1)}, u32[]{:S(2)}, u32[]{:S(2)}) collective-permute-start(bf16[128,256]{1,0:T(8,128)(2,1)S(1)} %shard_map.159.refs_0_), channel_id=1, source_target_pairs={{0,4},{4,0},{8,12},{12,8},{1,5},{5,1},{9,13},{13,9},{2,6},{6,2},{1... | collective-permute-start | bytes 196616 | tf_op jit(solution)/shard_map/ppermute | solution.py:39
  42.0 6.1 %collective-permute-start.9 = (bf16[128,256]{1,0:T(8,128)(2,1)S(1)}, bf16[128,256]{1,0:T(8,128)(2,1)S(1)}, u32[]{:S(2)}, u32[]{:S(2)}) collective-permute-start(bf16[128,256]{1,0:T(8,128)(2,1)S(1)} %get-tuple-element.58), channel_id=1, source_target_pairs={{12,0},{0,4},{4,8},{8,12},{13,1},{1,5},{5,9},{9,13},{14,2},{2,6},{... | collective-permute-start | bytes 196616 | tf_op jit(solution)/shard_map/ppermute | solution.py:35
  42.6 5.5 %collective-permute-start.10 = (bf16[128,256]{1,0:T(8,128)(2,1)S(1)}, bf16[128,256]{1,0:T(8,128)(2,1)S(1)}, u32[]{:S(2)}, u32[]{:S(2)}) collective-permute-start(bf16[128,256]{1,0:T(8,128)(2,1)S(1)} %get-tuple-element.59), channel_id=1, source_target_pairs={{4,0},{8,4},{12,8},{0,12},{5,1},{9,5},{13,9},{1,13},{6,2},{10,6},{... | collective-permute-start | bytes 196616 | tf_op jit(solution)/shard_map/ppermute | solution.py:35
  45.9 7.4 %collective-permute-start.16 = (bf16[256,256]{1,0:T(8,128)(2,1)S(1)}, bf16[256,256]{1,0:T(8,128)(2,1)S(1)}, u32[]{:S(2)}, u32[]{:S(2)}) collective-permute-start(bf16[256,256]{1,0:T(8,128)(2,1)S(1)} %shard_map.166.own_ref), channel_id=1, source_target_pairs={{0,2},{1,3},{2,0},{3,1},{4,6},{5,7},{6,4},{7,5},{8,10},{9,11},{10,... | collective-permute-start | bytes 393224 | tf_op jit(solution)/shard_map/ppermute | solution.py:39
  48.1 5.2 %collective-permute-start.11 = (bf16[128,256]{1,0:T(8,128)(2,1)S(1)}, bf16[128,256]{1,0:T(8,128)(2,1)S(1)}, u32[]{:S(2)}, u32[]{:S(2)}) collective-permute-start(bf16[128,256]{1,0:T(8,128)(2,1)S(1)} %shard_map.160.term_a_ref), channel_id=1, source_target_pairs={{0,8},{4,12},{8,0},{12,4},{1,9},{5,13},{9,1},{13,5},{2,10},{6,14},... | collective-permute-start | bytes 196616 | tf_op jit(solution)/shard_map/ppermute | solution.py:39
  53.3 1.7 %collective-permute-start.17 = (bf16[640,256]{1,0:T(8,128)(2,1)S(1)}, bf16[640,256]{1,0:T(8,128)(2,1)S(1)}, u32[]{:S(2)}, u32[]{:S(2)}) collective-permute-start(bf16[640,256]{1,0:T(8,128)(2,1)S(1)} %shard_map.167.refs_1_), channel_id=1, source_target_pairs={{0,1},{1,0},{2,3},{3,2},{4,5},{5,4},{6,7},{7,6},{8,9},{9,8},{10,11... | collective-permute-start | bytes 983048 | tf_op jit(solution)/shard_map/ppermute | solution.py:39
  (4 other events, 4.2 us)

commit v5 on v4

--- a/solution.py
+++ b/solution.py
@@ -63,11 +63,11 @@
         self.window = 2 * self.radius + 1
         self.cap = max(2, 2 * members_dev // (JET_DEV * self.window))
         self.used = JET_DEV * self.cap
-        self.chunk = -(-(self.used + 1) // 16) * 16
+        self.chunk = -(-(self.used + 1) // 8) * 8
         self.slots = -(-self.window * self.cap // 64) * 64
         self.owned = JET_DEV * self.slots
         assert sectors % 2 == 0
-        self.hops = sorted((o ^ 1 for o in range(-self.radius, self.radius + 1)), key=abs)
+        self.hops = sorted((o ^ 1 for o in range(-self.radius, self.radius + 1)), key=lambda hop: (hop != 0, -abs(hop)))
 
     def seat(self, c, w):
         jet = sum((c >= t * self.cap).astype(jnp.int32) for t in range(1, JET_DEV))
@@ -157,12 +157,12 @@
     scale = 1.0 / math.sqrt(head)
 
     members = upstream = present = None
-    base = plan.used // 16 * 16
+    base = plan.used // 8 * 8
     for w in range(window):
         hot = jnp.where(iota((owned, count), 0) == plan.seat(iota((owned, count), 1), w), 1.0, 0.0)
         low = hot.astype(LOW)
         m, u = mm(low, chunk_refs[w][:count, :]), mm(low, chunk_refs[w][count:, :])
-        tail = chunk_refs[w][count + base : count + base + 16, :].astype(FULL)
+        tail = chunk_refs[w][count + base : count + base + 8, :].astype(FULL)
         row = jnp.sum(jnp.where(iota(tail.shape, 0) == plan.used - base, tail, 0.0), axis=0, keepdims=True)
         p = jnp.sum(hot * row[:, :count], axis=1, keepdims=True)
         members = m if members is None else members + m
@@ -187,23 +187,28 @@
             total = part if total is None else total + part
         return total
 
-    mixture, grad_q, grad_k, grad_v = [], [], [], []
-    for j in range(JET_DEV):
-        span = slice(j * slots, (j + 1) * slots)
-        q, k, v, g = queries[span], keys[span], vals[span], grad_mix[span]
-        here = present[span] > 0.5
-        q_wide, g_wide = spread(q), spread(g)
-        scores = jnp.where(here, mm_nt(k, q_wide) * scale, -1e30)
-        powers = jnp.exp(scores - jnp.max(scores, axis=0, keepdims=True))
+    jets = range(JET_DEV)
+    spans = [slice(j * slots, (j + 1) * slots) for j in jets]
+    q_wide, g_wide = [spread(queries[x]) for x in spans], [spread(grad_mix[x]) for x in spans]
+    scores = [mm_nt(keys[x], wide) for x, wide in zip(spans, q_wide)]
+    grad_chances = [mm_nt(vals[x], wide) for x, wide in zip(spans, g_wide)]
+    chances_low, grad_scores = [], []
+    for j in jets:
+        masked = jnp.where(present[spans[j]] > 0.5, scores[j] * scale, -1e30)
+        powers = jnp.exp(masked - jnp.max(masked, axis=0, keepdims=True))
         chances = powers * (1.0 / jnp.sum(powers, axis=0, keepdims=True))
-        chances_low = chances.astype(LOW)
-        grad_chances = mm_nt(v, g_wide)
-        inner = jnp.sum(chances * grad_chances, axis=0, keepdims=True)
-        grad_scores = (chances * (grad_chances - inner) * scale).astype(LOW)
-        mixture.append(merged(mm_tn(chances_low, v)).astype(LOW))
-        grad_q.append(merged(mm_tn(grad_scores, k)).astype(LOW))
-        grad_k.append(mm(grad_scores, q_wide).astype(LOW))
-        grad_v.append(mm(chances_low, g_wide).astype(LOW))
+        chances_low.append(chances.astype(LOW))
+        inner = jnp.sum(chances * grad_chances[j], axis=0, keepdims=True)
+        grad_scores.append((chances * (grad_chances[j] - inner) * scale).astype(LOW))
+    grad_k = [mm(grad_scores[j], q_wide[j]).astype(LOW) for j in jets]
+    grad_v = [mm(chances_low[j], g_wide[j]).astype(LOW) for j in jets]
+
+    def turned(wide):
+        tall = wide.T
+        return jnp.concatenate([tall[h * slots : (h + 1) * slots, :] for h in range(HEADS)], axis=1)
+
+    mixture = [mm(turned(chances_low[j]), spread(vals[spans[j]])).astype(LOW) for j in jets]
+    grad_q = [mm(turned(grad_scores[j]), spread(keys[spans[j]])).astype(LOW) for j in jets]
     mixture, grad_q, grad_k, grad_v = [jnp.concatenate(x, axis=0) for x in (mixture, grad_q, grad_k, grad_v)]
     parts_ref[0] = members
     parts_ref[1] = upstream
@@ -366,7 +371,6 @@
         [parts, *weights],
         micros=0.7,
     )
-    backs = plan.routed(backs, back=True)
     core, across = [((lax.axis_index("ev") >> b) & 1).astype(jnp.int32).reshape(1) for b in range(2)]
     a_send, a_keep = call(
         lambda *refs: term_kernel(channels, *refs),
@@ -375,6 +379,8 @@
         [parts],
     )
     a_came = swapped(a_send, "ev", 1)
+    a_came = lax.optimization_barrier((a_came, *backs))[0]
+    backs = plan.routed(backs, back=True)
     a_send, a_keep = call(halve_kernel, [((channels, channels), LOW), ((channels, channels), FULL)], [across], [a_keep, a_came])
     a_came = swapped(a_send, "ev", 2)
     half = channels // 2
@@ -405,12 +411,13 @@
     mask = 1
     while mask < plan.sectors:
         a_came = swapped(a_own, "phi", mask)
+        if mask == 1:
+            a_came = lax.optimization_barrier((a_came, m_own))[0]
         m_own = added(half, m_own, m_came)
-        if 2 * mask == plan.sectors:
-            m_own = lax.optimization_barrier((m_own, from_lower, from_upper))[0]
         m_came = swapped(m_own, "phi", mask)
         a_own = added(channels, a_own, a_came)
         mask *= 2
+    a_own = lax.optimization_barrier((a_own, from_lower, from_upper))[0]
     a_came = swapped(a_own, "ev", 2)
     (grad_cells,) = call(
         lambda *refs: edges_kernel(plan, *refs), [((per_device, channels), LOW)], [], [kept, from_lower, from_upper]

time: 56.4 us -> 53.6 us (0.950)
  waiting for transfers between devices: 23.4 us -> 17.2 us
  starting transfers between devices: 22.1 us -> 26.1 us
  Pallas kernels: 7 us -> 6.39 us
    ppermute x4, waiting for transfers between devices: 7.82 us -> 4.74 us  [routed(): moved.append(lax.ppermute(part, 'phi', route) if hop else part)]
    ppermute x10, starting transfers between devices: 7.31 us -> 9.86 us  [swapped(): lax.ppermute(block, axis, [(i, i ^ mask) for i in range(lax.axis_size(axi...]
    ppermute x10, waiting for transfers between devices: 12.7 us -> 10.7 us  [swapped(): lax.ppermute(block, axis, [(i, i ^ mask) for i in range(lax.axis_size(axi...]
    ppermute x4, starting transfers between devices: 5.83 us -> 7.25 us  [routed(): moved.append(lax.ppermute(part, 'phi', route) if hop else part)]
    ppermute x4, waiting for transfers between devices: 2.86 us -> 1.78 us  [shifted(): lax.ppermute(block, axis, [((i - distance) % count, i) for i in range(cou...]
    pallas_call x16, Pallas kernels: 7 us -> 6.39 us  [call(): pl.pallas_call(body, out_shape=[kind(shape, dtype) for shape, dtype in ou...]
  transfers between devices with their start and end apart: 18 -> 18, of which waited for: 13 -> 16; matrix products, arithmetic and copies ran while one was open for 2% -> 2% of each run, Pallas kernels for 4% -> 4%
where the time goes in v5:
time: 53.6 us; the launch traced here: 53.4 us
  starting transfers between devices  26.1 us (49%)
  waiting for transfers between devices  17.2 us (32%)
  Pallas kernels  6.39 us (12%)
  local copies, waits for them, and re-layouts  2.95 us (6%)
  between operations  0.8 us (1%)
    ppermute x10, waiting for transfers between devices, swapped(): lax.ppermute(block, axis, [(i, i ^ mask) for i in range(lax.axis_size(axi...  10.7 us
    ppermute x10, starting transfers between devices, swapped(): lax.ppermute(block, axis, [(i, i ^ mask) for i in range(lax.axis_size(axi...  9.86 us
    ppermute x4, starting transfers between devices, shifted(): lax.ppermute(block, axis, [((i - distance) % count, i) for i in range(cou...  8.99 us
    ppermute x4, starting transfers between devices, routed(): moved.append(lax.ppermute(part, 'phi', route) if hop else part)  7.25 us
    pallas_call x16, Pallas kernels, call(): pl.pallas_call(body, out_shape=[kind(shape, dtype) for shape, dtype in ou...  6.39 us
    ppermute x4, waiting for transfers between devices, routed(): moved.append(lax.ppermute(part, 'phi', route) if hop else part)  4.74 us
    unnamed x22, local copies, waits for them, and re-layouts  2.03 us
    ppermute x4, waiting for transfers between devices, shifted(): lax.ppermute(block, axis, [((i - distance) % count, i) for i in range(cou...  1.78 us
  transfers between devices with their start and end apart: 18, of which 16 were waited for; matrix products, arithmetic and copies ran while one was open for 2% of the time, Pallas kernels for 4%

profile of v5, /device:TPU:0, one launch (start us, length us, event | category | flops | bytes accessed | tf_op | source)
XLA Modules:
  0.0 53.4 jit_solution(8551622209463486018)
XLA Ops:
  0.6 0.9 %slice_bitcast_fusion = (bf16[128,256]{1,0:T(8,128)(2,1)S(1)}, bf16[128,256]{1,0:T(8,128)(2,1)S(1)}) fusion(bf16[1,256,256]{2,1,0:T(8,128)(2,1)} %param.10), kind=kLoop, calls=%fused_computation | loop fusion | bytes 262144 | tf_op jit(solution)/shard_map/slice | solution.py:342
  1.6 3.1 %collective-permute-start = (bf16[128,256]{1,0:T(8,128)(2,1)S(1)}, bf16[128,256]{1,0:T(8,128)(2,1)S(1)}, u32[]{:S(2)}, u32[]{:S(2)}) collective-permute-start(bf16[128,256]{1,0:T(8,128)(2,1)S(1)} %get-tuple-element.78), channel_id=1, source_target_pairs={{12,0},{0,4},{4,8},{8,12},{13,1},{1,5},{5,9},{9,13},{14,2},{2,6},{... | collective-permute-start | bytes 196616 | tf_op jit(solution)/shard_map/ppermute | solution.py:35
  4.6 2.1 %collective-permute-start.1 = (bf16[128,256]{1,0:T(8,128)(2,1)S(1)}, bf16[128,256]{1,0:T(8,128)(2,1)S(1)}, u32[]{:S(2)}, u32[]{:S(2)}) collective-permute-start(bf16[128,256]{1,0:T(8,128)(2,1)S(1)} %get-tuple-element.77), channel_id=1, source_target_pairs={{4,0},{8,4},{12,8},{0,12},{5,1},{9,5},{13,9},{1,13},{6,2},{10,6},{... | collective-permute-start | bytes 196616 | tf_op jit(solution)/shard_map/ppermute | solution.py:35
  7.4 1.0 %shard_map.153 = (bf16[264,256]{1,0:T(8,128)(2,1)S(1)}, bf16[256,264]{1,0:T(8,128)(2,1)S(1)}, f32[8,256]{1,0:T(8,128)S(1)}, bf16[88,256]{1,0:T(8,128)(2,1)S(1)},...) custom-call(s32[1]{0:T(128)} %bitcast.1.refs_0_, s32[2,4]{1,0:T(2,128)S(1)} %bitcast.18, ...), custom_call_target="tpu_custom_call" | custom-call | flops 500000000 | tf_op jit(solution)/shard_map/pallas_call | solution.py:22
  10.1 2.0 %collective-permute-start.2 = (bf16[176,256]{1,0:T(8,128)(2,1)S(1)}, bf16[176,256]{1,0:T(8,128)(2,1)S(1)}, u32[]{:S(2)}, u32[]{:S(2)}) collective-permute-start(bf16[176,256]{1,0:T(8,128)(2,1)S(1)} %get-tuple-element.48), channel_id=1, source_target_pairs={{0,8},{4,12},{8,0},{12,4},{1,9},{5,13},{9,1},{13,5},{2,10},{6,14},... | collective-permute-start | bytes 270344 | tf_op jit(solution)/shard_map/ppermute | solution.py:83
  12.0 1.9 %collective-permute-start.3 = (bf16[176,256]{1,0:T(8,128)(2,1)S(1)}, bf16[176,256]{1,0:T(8,128)(2,1)S(1)}, u32[]{:S(2)}, u32[]{:S(2)}) collective-permute-start(bf16[176,256]{1,0:T(8,128)(2,1)S(1)} %get-tuple-element.49), channel_id=1, source_target_pairs={{0,4},{4,0},{8,12},{12,8},{1,5},{5,1},{9,13},{13,9},{2,6},{6,2},{1... | collective-permute-start | bytes 270344 | tf_op jit(solution)/shard_map/ppermute | solution.py:83
  13.9 2.3 %collective-permute-done.2.refs_1_ = bf16[176,256]{1,0:T(8,128)(2,1)S(1)} collective-permute-done((bf16[176,256]{1,0:T(8,128)(2,1)S(1)}, bf16[176,256]{1,0:T(8,128)(2,1)S(1)}, u32[]{:S(2)}, u32[]{:S(2)}) %collective-permute-start.2) | collective-permute-done | bytes 90144 | tf_op jit(solution)/shard_map/ppermute | solution.py:83
  16.9 2.0 %shard_map.155.refs_0_.refs_1_ = bf16[6,256,256]{2,1,0:T(8,128)(2,1)S(1)} custom-call(bf16[176,256]{1,0:T(8,128)(2,1)S(1)} %get-tuple-element.47.refs_0_, bf16[176,256]{1,0:T(8,128)(2,1)S(1)} %collective-permute-done.2.refs_1_, bf16[176,256]{1,0:T(8,128)(2,1)S(1)} %collective-permute-done.3.refs_2_, bf16[256,256]{1,0:T(8,128)(2,1)S(1)} %copy-done.1, ...), custom_call_target="tpu_custom_call" | custom-call | flops 2500000000 | tf_op jit(solution)/shard_map/pallas_call | solution.py:22
  20.0 0.9 %collective-permute-done.12.came_ref = bf16[512,256]{1,0:T(8,128)(2,1)S(1)} collective-permute-done((bf16[512,256]{1,0:T(8,128)(2,1)S(1)}, bf16[512,256]{1,0:T(8,128)(2,1)S(1)}, u32[]{:S(2)}, u32[]{:S(2)}) %collective-permute-start.12) | collective-permute-done | bytes 262176 | tf_op jit(solution)/shard_map/ppermute | solution.py:39
  20.9 1.4 %collective-permute-start.13 = (bf16[256,256]{1,0:T(8,128)(2,1)S(1)}, bf16[256,256]{1,0:T(8,128)(2,1)S(1)}, u32[]{:S(2)}, u32[]{:S(2)}) collective-permute-start(bf16[256,256]{1,0:T(8,128)(2,1)S(1)} %get-tuple-element.68), channel_id=1, source_target_pairs={{0,2},{1,3},{2,0},{3,1},{4,6},{5,7},{6,4},{7,5},{8,10},{9,11},{10,... | collective-permute-start | bytes 393224 | tf_op jit(solution)/shard_map/ppermute | solution.py:39
  22.3 1.3 %collective-permute-start.4 = (bf16[176,256]{1,0:T(8,128)(2,1)S(1)}, bf16[176,256]{1,0:T(8,128)(2,1)S(1)}, u32[]{:S(2)}, u32[]{:S(2)}) collective-permute-start(bf16[176,256]{1,0:T(8,128)(2,1)S(1)} %get-tuple-element.51), channel_id=1, source_target_pairs={{8,0},{12,4},{0,8},{4,12},{9,1},{13,5},{1,9},{5,13},{10,2},{14,6},... | collective-permute-start | bytes 270344 | tf_op jit(solution)/shard_map/ppermute | solution.py:83
  23.6 2.1 %collective-permute-start.5 = (bf16[176,256]{1,0:T(8,128)(2,1)S(1)}, bf16[176,256]{1,0:T(8,128)(2,1)S(1)}, u32[]{:S(2)}, u32[]{:S(2)}) collective-permute-start(bf16[176,256]{1,0:T(8,128)(2,1)S(1)} %get-tuple-element.52), channel_id=1, source_target_pairs={{4,0},{0,4},{12,8},{8,12},{5,1},{1,5},{13,9},{9,13},{6,2},{2,6},{1... | collective-permute-start | bytes 270344 | tf_op jit(solution)/shard_map/ppermute | solution.py:83
  25.7 0.8 %collective-permute-done.13.refs_1_ = bf16[256,256]{1,0:T(8,128)(2,1)S(1)} collective-permute-done((bf16[256,256]{1,0:T(8,128)(2,1)S(1)}, bf16[256,256]{1,0:T(8,128)(2,1)S(1)}, u32[]{:S(2)}, u32[]{:S(2)}) %collective-permute-start.13) | collective-permute-done | bytes 131104 | tf_op jit(solution)/shard_map/ppermute | solution.py:39
  26.5 1.6 %collective-permute-start.14 = (bf16[256,256]{1,0:T(8,128)(2,1)S(1)}, bf16[256,256]{1,0:T(8,128)(2,1)S(1)}, u32[]{:S(2)}, u32[]{:S(2)}) collective-permute-start(bf16[256,256]{1,0:T(8,128)(2,1)S(1)} %shard_map.164.refs_0_), channel_id=1, source_target_pairs={{0,4},{4,0},{8,12},{12,8},{1,5},{5,1},{9,13},{13,9},{2,6},{6,2},{1... | collective-permute-start | bytes 393224 | tf_op jit(solution)/shard_map/ppermute | solution.py:39
  28.2 1.2 %collective-permute-done.4.refs_3_ = bf16[176,256]{1,0:T(8,128)(2,1)S(1)} collective-permute-done((bf16[176,256]{1,0:T(8,128)(2,1)S(1)}, bf16[176,256]{1,0:T(8,128)(2,1)S(1)}, u32[]{:S(2)}, u32[]{:S(2)}) %collective-permute-start.4) | collective-permute-done | bytes 90144 | tf_op jit(solution)/shard_map/ppermute | solution.py:83
  30.5 1.2 %collective-permute-done.6.refs_1_ = bf16[128,256]{1,0:T(8,128)(2,1)S(1)} collective-permute-done((bf16[128,256]{1,0:T(8,128)(2,1)S(1)}, bf16[128,256]{1,0:T(8,128)(2,1)S(1)}, u32[]{:S(2)}, u32[]{:S(2)}) %collective-permute-start.6) | collective-permute-done | bytes 65568 | tf_op jit(solution)/shard_map/ppermute | solution.py:39
  32.4 2.1 %collective-permute-start.15 = (bf16[256,256]{1,0:T(8,128)(2,1)S(1)}, bf16[256,256]{1,0:T(8,128)(2,1)S(1)}, u32[]{:S(2)}, u32[]{:S(2)}) collective-permute-start(bf16[256,256]{1,0:T(8,128)(2,1)S(1)} %shard_map.165.refs_0_), channel_id=1, source_target_pairs={{0,8},{4,12},{8,0},{12,4},{1,9},{5,13},{9,1},{13,5},{2,10},{6,14},... | collective-permute-start | bytes 393224 | tf_op jit(solution)/shard_map/ppermute | solution.py:39
  34.7 1.8 %collective-permute-start.10 = (bf16[128,256]{1,0:T(8,128)(2,1)S(1)}, bf16[128,256]{1,0:T(8,128)(2,1)S(1)}, u32[]{:S(2)}, u32[]{:S(2)}) collective-permute-start(bf16[128,256]{1,0:T(8,128)(2,1)S(1)} %get-tuple-element.61), channel_id=1, source_target_pairs={{12,0},{0,4},{4,8},{8,12},{13,1},{1,5},{5,9},{9,13},{14,2},{2,6},{... | collective-permute-start | bytes 196616 | tf_op jit(solution)/shard_map/ppermute | solution.py:35
  36.5 2.0 %collective-permute-start.11 = (bf16[128,256]{1,0:T(8,128)(2,1)S(1)}, bf16[128,256]{1,0:T(8,128)(2,1)S(1)}, u32[]{:S(2)}, u32[]{:S(2)}) collective-permute-start(bf16[128,256]{1,0:T(8,128)(2,1)S(1)} %get-tuple-element.62), channel_id=1, source_target_pairs={{4,0},{8,4},{12,8},{0,12},{5,1},{9,5},{13,9},{1,13},{6,2},{10,6},{... | collective-permute-start | bytes 196616 | tf_op jit(solution)/shard_map/ppermute | solution.py:35
  38.8 1.7 %collective-permute-start.8 = (bf16[128,256]{1,0:T(8,128)(2,1)S(1)}, bf16[128,256]{1,0:T(8,128)(2,1)S(1)}, u32[]{:S(2)}, u32[]{:S(2)}) collective-permute-start(bf16[128,256]{1,0:T(8,128)(2,1)S(1)} %shard_map.159.refs_0_), channel_id=1, source_target_pairs={{0,4},{4,0},{8,12},{12,8},{1,5},{5,1},{9,13},{13,9},{2,6},{6,2},{1... | collective-permute-start | bytes 196616 | tf_op jit(solution)/shard_map/ppermute | solution.py:39
  40.5 2.8 %collective-permute-done.15.refs_1_ = bf16[256,256]{1,0:T(8,128)(2,1)S(1)} collective-permute-done((bf16[256,256]{1,0:T(8,128)(2,1)S(1)}, bf16[256,256]{1,0:T(8,128)(2,1)S(1)}, u32[]{:S(2)}, u32[]{:S(2)}) %collective-permute-start.15) | collective-permute-done | bytes 131104 | tf_op jit(solution)/shard_map/ppermute | solution.py:39
  44.7 2.0 %collective-permute-start.9 = (bf16[128,256]{1,0:T(8,128)(2,1)S(1)}, bf16[128,256]{1,0:T(8,128)(2,1)S(1)}, u32[]{:S(2)}, u32[]{:S(2)}) collective-permute-start(bf16[128,256]{1,0:T(8,128)(2,1)S(1)} %shard_map.160.term_a_ref), channel_id=1, source_target_pairs={{0,8},{4,12},{8,0},{12,4},{1,9},{5,13},{9,1},{13,5},{2,10},{6,14},... | collective-permute-start | bytes 196616 | tf_op jit(solution)/shard_map/ppermute | solution.py:39
  46.7 3.7 %collective-permute-done.9.term_b_ref = bf16[128,256]{1,0:T(8,128)(2,1)S(1)} collective-permute-done((bf16[128,256]{1,0:T(8,128)(2,1)S(1)}, bf16[128,256]{1,0:T(8,128)(2,1)S(1)}, u32[]{:S(2)}, u32[]{:S(2)}) %collective-permute-start.9) | collective-permute-done | bytes 65568 | tf_op jit(solution)/shard_map/ppermute | solution.py:39
  52.2 1.2 %shard_map.168 = (f32[256,256]{1,0:T(8,128)}, f32[256,256]{1,0:T(8,128)}, f32[256,256]{1,0:T(8,128)}, f32[256,256]{1,0:T(8,128)}, f32[256,256]{1,0:T(8,128)}) custom-call(s32[1]{0:T(128)} %bitcast.refs_0_, bf16[640,256]{1,0:T(8,128)(2,1)S(1)} %shard_map.167.refs_1_, bf16[640,256]{1,0:T(8,128)(2,1)S(1)} %collective-permute-done.17.refs_2_), custom_call_target="tpu_custom_call" | custom-call | flops 100000000 | tf_op jit(solution)/shard_map/pallas_call | solution.py:22
  (51 shorter events, 9.5 us)
Async XLA Ops:
  0.6 6.1 %copy-start.5 = (bf16[1,256,256]{2,1,0:T(8,128)(2,1)S(1)}, bf16[1,256,256]{2,1,0:T(8,128)(2,1)}, u32[]{:S(2)}) copy-start(bf16[1,256,256]{2,1,0:T(8,128)(2,1)} %param.14) | copy-start | bytes 393220
  1.6 7.5 %collective-permute-start = (bf16[128,256]{1,0:T(8,128)(2,1)S(1)}, bf16[128,256]{1,0:T(8,128)(2,1)S(1)}, u32[]{:S(2)}, u32[]{:S(2)}) collective-permute-start(bf16[128,256]{1,0:T(8,128)(2,1)S(1)} %get-tuple-element.78), channel_id=1, source_target_pairs={{12,0},{0,4},{4,8},{8,12},{13,1},{1,5},{5,9},{9,13},{14,2},{2,6},{... | collective-permute-start | bytes 196616 | tf_op jit(solution)/shard_map/ppermute | solution.py:35
  4.6 5.0 %collective-permute-start.1 = (bf16[128,256]{1,0:T(8,128)(2,1)S(1)}, bf16[128,256]{1,0:T(8,128)(2,1)S(1)}, u32[]{:S(2)}, u32[]{:S(2)}) collective-permute-start(bf16[128,256]{1,0:T(8,128)(2,1)S(1)} %get-tuple-element.77), channel_id=1, source_target_pairs={{4,0},{8,4},{12,8},{0,12},{5,1},{9,5},{13,9},{1,13},{6,2},{10,6},{... | collective-permute-start | bytes 196616 | tf_op jit(solution)/shard_map/ppermute | solution.py:35
  7.4 2.2 %copy-start.6 = (bf16[256,256]{1,0:T(8,128)(2,1)S(1)}, bf16[256,256]{1,0:T(8,128)(2,1)}, u32[]{:S(2)}) copy-start(bf16[256,256]{1,0:T(8,128)(2,1)} %refs_10_.1) | copy-start | bytes 393220
  9.6 7.3 %copy-start.1 = (bf16[256,256]{1,0:T(8,128)(2,1)S(1)}, bf16[256,256]{1,0:T(8,128)(2,1)}, u32[]{:S(2)}) copy-start(bf16[256,256]{1,0:T(8,128)(2,1)} %refs_1_.1) | copy-start | bytes 393220
  9.6 7.3 %copy-start.2 = (bf16[256,256]{1,0:T(8,128)(2,1)S(1)}, bf16[256,256]{1,0:T(8,128)(2,1)}, u32[]{:S(2)}) copy-start(bf16[256,256]{1,0:T(8,128)(2,1)} %refs_2_.3) | copy-start | bytes 393220
  9.6 7.3 %copy-start.3 = (bf16[256,256]{1,0:T(8,128)(2,1)S(1)}, bf16[256,256]{1,0:T(8,128)(2,1)}, u32[]{:S(2)}) copy-start(bf16[256,256]{1,0:T(8,128)(2,1)} %refs_3_.3) | copy-start | bytes 393220
  9.6 7.3 %copy-start.4 = (bf16[256,256]{1,0:T(8,128)(2,1)S(1)}, bf16[256,256]{1,0:T(8,128)(2,1)}, u32[]{:S(2)}) copy-start(bf16[256,256]{1,0:T(8,128)(2,1)} %refs_4_.5) | copy-start | bytes 393220
  10.1 6.2 %collective-permute-start.2 = (bf16[176,256]{1,0:T(8,128)(2,1)S(1)}, bf16[176,256]{1,0:T(8,128)(2,1)S(1)}, u32[]{:S(2)}, u32[]{:S(2)}) collective-permute-start(bf16[176,256]{1,0:T(8,128)(2,1)S(1)} %get-tuple-element.48), channel_id=1, source_target_pairs={{0,8},{4,12},{8,0},{12,4},{1,9},{5,13},{9,1},{13,5},{2,10},{6,14},... | collective-permute-start | bytes 270344 | tf_op jit(solution)/shard_map/ppermute | solution.py:83
  12.0 4.8 %collective-permute-start.3 = (bf16[176,256]{1,0:T(8,128)(2,1)S(1)}, bf16[176,256]{1,0:T(8,128)(2,1)S(1)}, u32[]{:S(2)}, u32[]{:S(2)}) collective-permute-start(bf16[176,256]{1,0:T(8,128)(2,1)S(1)} %get-tuple-element.49), channel_id=1, source_target_pairs={{0,4},{4,0},{8,12},{12,8},{1,5},{5,1},{9,13},{13,9},{2,6},{6,2},{1... | collective-permute-start | bytes 270344 | tf_op jit(solution)/shard_map/ppermute | solution.py:83
  19.3 1.6 %collective-permute-start.12 = (bf16[512,256]{1,0:T(8,128)(2,1)S(1)}, bf16[512,256]{1,0:T(8,128)(2,1)S(1)}, u32[]{:S(2)}, u32[]{:S(2)}) collective-permute-start(bf16[512,256]{1,0:T(8,128)(2,1)S(1)} %get-tuple-element.65), channel_id=1, source_target_pairs={{0,1},{1,0},{2,3},{3,2},{4,5},{5,4},{6,7},{7,6},{8,9},{9,8},{10,11... | collective-permute-start | bytes 786440 | tf_op jit(solution)/shard_map/ppermute | solution.py:39
  20.9 5.6 %collective-permute-start.13 = (bf16[256,256]{1,0:T(8,128)(2,1)S(1)}, bf16[256,256]{1,0:T(8,128)(2,1)S(1)}, u32[]{:S(2)}, u32[]{:S(2)}) collective-permute-start(bf16[256,256]{1,0:T(8,128)(2,1)S(1)} %get-tuple-element.68), channel_id=1, source_target_pairs={{0,2},{1,3},{2,0},{3,1},{4,6},{5,7},{6,4},{7,5},{8,10},{9,11},{10,... | collective-permute-start | bytes 393224 | tf_op jit(solution)/shard_map/ppermute | solution.py:39
  22.3 7.0 %collective-permute-start.4 = (bf16[176,256]{1,0:T(8,128)(2,1)S(1)}, bf16[176,256]{1,0:T(8,128)(2,1)S(1)}, u32[]{:S(2)}, u32[]{:S(2)}) collective-permute-start(bf16[176,256]{1,0:T(8,128)(2,1)S(1)} %get-tuple-element.51), channel_id=1, source_target_pairs={{8,0},{12,4},{0,8},{4,12},{9,1},{13,5},{1,9},{5,13},{10,2},{14,6},... | collective-permute-start | bytes 270344 | tf_op jit(solution)/shard_map/ppermute | solution.py:83
  23.6 6.3 %collective-permute-start.5 = (bf16[176,256]{1,0:T(8,128)(2,1)S(1)}, bf16[176,256]{1,0:T(8,128)(2,1)S(1)}, u32[]{:S(2)}, u32[]{:S(2)}) collective-permute-start(bf16[176,256]{1,0:T(8,128)(2,1)S(1)} %get-tuple-element.52), channel_id=1, source_target_pairs={{4,0},{0,4},{12,8},{8,12},{5,1},{1,5},{13,9},{9,13},{6,2},{2,6},{1... | collective-permute-start | bytes 270344 | tf_op jit(solution)/shard_map/ppermute | solution.py:83
  26.5 5.8 %collective-permute-start.14 = (bf16[256,256]{1,0:T(8,128)(2,1)S(1)}, bf16[256,256]{1,0:T(8,128)(2,1)S(1)}, u32[]{:S(2)}, u32[]{:S(2)}) collective-permute-start(bf16[256,256]{1,0:T(8,128)(2,1)S(1)} %shard_map.164.refs_0_), channel_id=1, source_target_pairs={{0,4},{4,0},{8,12},{12,8},{1,5},{5,1},{9,13},{13,9},{2,6},{6,2},{1... | collective-permute-start | bytes 393224 | tf_op jit(solution)/shard_map/ppermute | solution.py:39
  30.4 1.3 %collective-permute-start.6 = (bf16[128,256]{1,0:T(8,128)(2,1)S(1)}, bf16[128,256]{1,0:T(8,128)(2,1)S(1)}, u32[]{:S(2)}, u32[]{:S(2)}) collective-permute-start(bf16[128,256]{1,0:T(8,128)(2,1)S(1)} %get-tuple-element.59), channel_id=1, source_target_pairs={{0,1},{1,0},{2,3},{3,2},{4,5},{5,4},{6,7},{7,6},{8,9},{9,8},{10,11... | collective-permute-start | bytes 196616 | tf_op jit(solution)/shard_map/ppermute | solution.py:39
  32.4 10.9 %collective-permute-start.15 = (bf16[256,256]{1,0:T(8,128)(2,1)S(1)}, bf16[256,256]{1,0:T(8,128)(2,1)S(1)}, u32[]{:S(2)}, u32[]{:S(2)}) collective-permute-start(bf16[256,256]{1,0:T(8,128)(2,1)S(1)} %shard_map.165.refs_0_), channel_id=1, source_target_pairs={{0,8},{4,12},{8,0},{12,4},{1,9},{5,13},{9,1},{13,5},{2,10},{6,14},... | collective-permute-start | bytes 393224 | tf_op jit(solution)/shard_map/ppermute | solution.py:39
  34.5 4.3 %collective-permute-start.7 = (bf16[128,256]{1,0:T(8,128)(2,1)S(1)}, bf16[128,256]{1,0:T(8,128)(2,1)S(1)}, u32[]{:S(2)}, u32[]{:S(2)}) collective-permute-start(bf16[128,256]{1,0:T(8,128)(2,1)S(1)} %shard_map.158.refs_0_), channel_id=1, source_target_pairs={{0,2},{1,3},{2,0},{3,1},{4,6},{5,7},{6,4},{7,5},{8,10},{9,11},{10,... | collective-permute-start | bytes 196616 | tf_op jit(solution)/shard_map/ppermute | solution.py:39
  34.7 8.7 %collective-permute-start.10 = (bf16[128,256]{1,0:T(8,128)(2,1)S(1)}, bf16[128,256]{1,0:T(8,128)(2,1)S(1)}, u32[]{:S(2)}, u32[]{:S(2)}) collective-permute-start(bf16[128,256]{1,0:T(8,128)(2,1)S(1)} %get-tuple-element.61), channel_id=1, source_target_pairs={{12,0},{0,4},{4,8},{8,12},{13,1},{1,5},{5,9},{9,13},{14,2},{2,6},{... | collective-permute-start | bytes 196616 | tf_op jit(solution)/shard_map/ppermute | solution.py:35
  36.5 7.4 %collective-permute-start.11 = (bf16[128,256]{1,0:T(8,128)(2,1)S(1)}, bf16[128,256]{1,0:T(8,128)(2,1)S(1)}, u32[]{:S(2)}, u32[]{:S(2)}) collective-permute-start(bf16[128,256]{1,0:T(8,128)(2,1)S(1)} %get-tuple-element.62), channel_id=1, source_target_pairs={{4,0},{8,4},{12,8},{0,12},{5,1},{9,5},{13,9},{1,13},{6,2},{10,6},{... | collective-permute-start | bytes 196616 | tf_op jit(solution)/shard_map/ppermute | solution.py:35
  38.8 5.9 %collective-permute-start.8 = (bf16[128,256]{1,0:T(8,128)(2,1)S(1)}, bf16[128,256]{1,0:T(8,128)(2,1)S(1)}, u32[]{:S(2)}, u32[]{:S(2)}) collective-permute-start(bf16[128,256]{1,0:T(8,128)(2,1)S(1)} %shard_map.159.refs_0_), channel_id=1, source_target_pairs={{0,4},{4,0},{8,12},{12,8},{1,5},{5,1},{9,13},{13,9},{2,6},{6,2},{1... | collective-permute-start | bytes 196616 | tf_op jit(solution)/shard_map/ppermute | solution.py:39
  43.9 6.5 %collective-permute-start.16 = (bf16[256,256]{1,0:T(8,128)(2,1)S(1)}, bf16[256,256]{1,0:T(8,128)(2,1)S(1)}, u32[]{:S(2)}, u32[]{:S(2)}) collective-permute-start(bf16[256,256]{1,0:T(8,128)(2,1)S(1)} %shard_map.166.own_ref), channel_id=1, source_target_pairs={{0,2},{1,3},{2,0},{3,1},{4,6},{5,7},{6,4},{7,5},{8,10},{9,11},{10,... | collective-permute-start | bytes 393224 | tf_op jit(solution)/shard_map/ppermute | solution.py:39
  44.7 5.8 %collective-permute-start.9 = (bf16[128,256]{1,0:T(8,128)(2,1)S(1)}, bf16[128,256]{1,0:T(8,128)(2,1)S(1)}, u32[]{:S(2)}, u32[]{:S(2)}) collective-permute-start(bf16[128,256]{1,0:T(8,128)(2,1)S(1)} %shard_map.160.term_a_ref), channel_id=1, source_target_pairs={{0,8},{4,12},{8,0},{12,4},{1,9},{5,13},{9,1},{13,5},{2,10},{6,14},... | collective-permute-start | bytes 196616 | tf_op jit(solution)/shard_map/ppermute | solution.py:39
  50.5 1.7 %collective-permute-start.17 = (bf16[640,256]{1,0:T(8,128)(2,1)S(1)}, bf16[640,256]{1,0:T(8,128)(2,1)S(1)}, u32[]{:S(2)}, u32[]{:S(2)}) collective-permute-start(bf16[640,256]{1,0:T(8,128)(2,1)S(1)} %shard_map.167.refs_1_), channel_id=1, source_target_pairs={{0,1},{1,0},{2,3},{3,2},{4,5},{5,4},{6,7},{7,6},{8,9},{9,8},{10,11... | collective-permute-start | bytes 983048 | tf_op jit(solution)/shard_map/ppermute | solution.py:39
  (4 other events, 4.2 us)

commit v6 on v5

--- a/solution.py
+++ b/solution.py
@@ -149,10 +149,10 @@
         chunk_refs[w][plan.chunk :, :] = cot_refs[w][...]
 
 
-def attend_kernel(plan, *refs):
+def attend_kernel(plan, bit_ref, *refs):
     window, count, slots, owned, channels = plan.window, plan.chunk, plan.slots, plan.owned, plan.channels
     chunk_refs = refs[:window]
-    wq_ref, wk_ref, wv_ref, wo_ref, parts_ref = refs[window:]
+    wq_ref, wk_ref, wv_ref, wo_ref, parts_ref, send_ref, keep_ref = refs[window:]
     head = channels // HEADS
     scale = 1.0 / math.sqrt(head)
 
@@ -216,6 +216,7 @@
     parts_ref[3] = grad_q
     parts_ref[4] = grad_k
     parts_ref[5] = grad_v
+    terms(channels, bit_ref, parts_ref, send_ref, keep_ref)
 
 
 def back_kernel(plan, parts_ref, wq_ref, wk_ref, wv_ref, wo_ref, *back_refs):
@@ -229,7 +230,7 @@
         back_refs[w][count:, :] = mm(hot, grad_members).astype(LOW)
 
 
-def term_kernel(channels, bit_ref, parts_ref, send_ref, keep_ref):
+def terms(channels, bit_ref, parts_ref, send_ref, keep_ref):
     bit = bit_ref[0]
     for half, ref in ((1 - bit, send_ref), (bit, keep_ref)):
         for t in range(2):
@@ -361,8 +362,13 @@
 
     chunks = plan.routed(chunks)
     weights = [query_weight, key_weight, value_weight, output_weight]
-    (parts,) = call(
-        lambda *refs: attend_kernel(plan, *refs), [((6, plan.owned, channels), LOW)], [], [*chunks, *weights], micros=2.5
+    core, across = [((lax.axis_index("ev") >> b) & 1).astype(jnp.int32).reshape(1) for b in range(2)]
+    parts, a_send, a_keep = call(
+        lambda *refs: attend_kernel(plan, *refs),
+        [((6, plan.owned, channels), LOW), ((2 * channels, channels), LOW), ((2 * channels, channels), FULL)],
+        [core],
+        [*chunks, *weights],
+        micros=2.5,
     )
     backs = call(
         lambda *refs: back_kernel(plan, *refs),
@@ -370,13 +376,6 @@
         [],
         [parts, *weights],
         micros=0.7,
-    )
-    core, across = [((lax.axis_index("ev") >> b) & 1).astype(jnp.int32).reshape(1) for b in range(2)]
-    a_send, a_keep = call(
-        lambda *refs: term_kernel(channels, *refs),
-        [((2 * channels, channels), LOW), ((2 * channels, channels), FULL)],
-        [core],
-        [parts],
     )
     a_came = swapped(a_send, "ev", 1)
     a_came = lax.optimization_barrier((a_came, *backs))[0]
@@ -408,15 +407,12 @@
     from_upper = shifted(first, "phi", -1)
     m_own = added(half, m_keep, m_came)
     m_came = swapped(m_own, "ev", 2)
-    mask = 1
-    while mask < plan.sectors:
-        a_came = swapped(a_own, "phi", mask)
-        if mask == 1:
-            a_came = lax.optimization_barrier((a_came, m_own))[0]
+    masks = [1 << bit for bit in range(plan.sectors.bit_length() - 1)]
+    for m_mask, a_mask in zip(masks[::-1], masks[::-1]):
+        a_came = swapped(a_own, "phi", a_mask)
         m_own = added(half, m_own, m_came)
-        m_came = swapped(m_own, "phi", mask)
+        m_came = swapped(m_own, "phi", m_mask)
         a_own = added(channels, a_own, a_came)
-        mask *= 2
     a_own = lax.optimization_barrier((a_own, from_lower, from_upper))[0]
     a_came = swapped(a_own, "ev", 2)
     (grad_cells,) = call(

time: 53.6 us -> 53.1 us (level)
  starting transfers between devices: 26.1 us -> 25 us
  waiting for transfers between devices: 17.2 us -> 17.8 us
    ppermute x10, starting transfers between devices: 9.86 us -> 8.77 us  [swapped(): lax.ppermute(block, axis, [(i, i ^ mask) for i in range(lax.axis_size(axi...]
    ppermute x4, waiting for transfers between devices: 1.78 us -> 2.58 us  [shifted(): lax.ppermute(block, axis, [((i - distance) % count, i) for i in range(cou...]
    pallas_call x16 -> x15, Pallas kernels: 6.39 us -> 6.36 us  [call(): pl.pallas_call(body, out_shape=[kind(shape, dtype) for shape, dtype in ou...]
  transfers between devices with their start and end apart: 18 -> 18, of which waited for: 16 -> 14; matrix products, arithmetic and copies ran while one was open for 2% -> 2% of each run, Pallas kernels for 4% -> 4%
where the time goes in v6:
time: 53.1 us; the launch traced here: 52.9 us
  starting transfers between devices  25 us (47%)
  waiting for transfers between devices  17.8 us (34%)
  Pallas kernels  6.36 us (12%)
  local copies, waits for them, and re-layouts  2.95 us (6%)
  between operations  0.81 us (2%)
    ppermute x10, waiting for transfers between devices, swapped(): lax.ppermute(block, axis, [(i, i ^ mask) for i in range(lax.axis_size(axi...  10.6 us
    ppermute x4, starting transfers between devices, shifted(): lax.ppermute(block, axis, [((i - distance) % count, i) for i in range(cou...  8.99 us
    ppermute x10, starting transfers between devices, swapped(): lax.ppermute(block, axis, [(i, i ^ mask) for i in range(lax.axis_size(axi...  8.77 us
    ppermute x4, starting transfers between devices, routed(): moved.append(lax.ppermute(part, 'phi', route) if hop else part)  7.25 us
    pallas_call x15, Pallas kernels, call(): pl.pallas_call(body, out_shape=[kind(shape, dtype) for shape, dtype in ou...  6.36 us
    ppermute x4, waiting for transfers between devices, routed(): moved.append(lax.ppermute(part, 'phi', route) if hop else part)  4.67 us
    ppermute x4, waiting for transfers between devices, shifted(): lax.ppermute(block, axis, [((i - distance) % count, i) for i in range(cou...  2.58 us
    unnamed x22, local copies, waits for them, and re-layouts  2.03 us
  transfers between devices with their start and end apart: 18, of which 14 were waited for; matrix products, arithmetic and copies ran while one was open for 2% of the time, Pallas kernels for 4%

profile of v6, /device:TPU:0, one launch (start us, length us, event | category | flops | bytes accessed | tf_op | source)
XLA Modules:
  0.0 52.9 jit_solution(8211270933957195581)
XLA Ops:
  0.6 0.9 %slice_bitcast_fusion = (bf16[128,256]{1,0:T(8,128)(2,1)S(1)}, bf16[128,256]{1,0:T(8,128)(2,1)S(1)}) fusion(bf16[1,256,256]{2,1,0:T(8,128)(2,1)} %param.10), kind=kLoop, calls=%fused_computation | loop fusion | bytes 262144 | tf_op jit(solution)/shard_map/slice | solution.py:343
  1.6 3.1 %collective-permute-start = (bf16[128,256]{1,0:T(8,128)(2,1)S(1)}, bf16[128,256]{1,0:T(8,128)(2,1)S(1)}, u32[]{:S(2)}, u32[]{:S(2)}) collective-permute-start(bf16[128,256]{1,0:T(8,128)(2,1)S(1)} %get-tuple-element.78), channel_id=1, source_target_pairs={{12,0},{0,4},{4,8},{8,12},{13,1},{1,5},{5,9},{9,13},{14,2},{2,6},{... | collective-permute-start | bytes 196616 | tf_op jit(solution)/shard_map/ppermute | solution.py:35
  4.6 2.1 %collective-permute-start.1 = (bf16[128,256]{1,0:T(8,128)(2,1)S(1)}, bf16[128,256]{1,0:T(8,128)(2,1)S(1)}, u32[]{:S(2)}, u32[]{:S(2)}) collective-permute-start(bf16[128,256]{1,0:T(8,128)(2,1)S(1)} %get-tuple-element.77), channel_id=1, source_target_pairs={{4,0},{8,4},{12,8},{0,12},{5,1},{9,5},{13,9},{1,13},{6,2},{10,6},{... | collective-permute-start | bytes 196616 | tf_op jit(solution)/shard_map/ppermute | solution.py:35
  7.4 1.0 %shard_map.153 = (bf16[264,256]{1,0:T(8,128)(2,1)S(1)}, bf16[256,264]{1,0:T(8,128)(2,1)S(1)}, f32[8,256]{1,0:T(8,128)S(1)}, bf16[88,256]{1,0:T(8,128)(2,1)S(1)},...) custom-call(s32[1]{0:T(128)} %bitcast.1.refs_0_, s32[2,4]{1,0:T(2,128)S(1)} %bitcast.18, ...), custom_call_target="tpu_custom_call" | custom-call | flops 500000000 | tf_op jit(solution)/shard_map/pallas_call | solution.py:22
  10.1 2.0 %collective-permute-start.2 = (bf16[176,256]{1,0:T(8,128)(2,1)S(1)}, bf16[176,256]{1,0:T(8,128)(2,1)S(1)}, u32[]{:S(2)}, u32[]{:S(2)}) collective-permute-start(bf16[176,256]{1,0:T(8,128)(2,1)S(1)} %get-tuple-element.48), channel_id=1, source_target_pairs={{0,8},{4,12},{8,0},{12,4},{1,9},{5,13},{9,1},{13,5},{2,10},{6,14},... | collective-permute-start | bytes 270344 | tf_op jit(solution)/shard_map/ppermute | solution.py:83
  12.0 1.9 %collective-permute-start.3 = (bf16[176,256]{1,0:T(8,128)(2,1)S(1)}, bf16[176,256]{1,0:T(8,128)(2,1)S(1)}, u32[]{:S(2)}, u32[]{:S(2)}) collective-permute-start(bf16[176,256]{1,0:T(8,128)(2,1)S(1)} %get-tuple-element.49), channel_id=1, source_target_pairs={{0,4},{4,0},{8,12},{12,8},{1,5},{5,1},{9,13},{13,9},{2,6},{6,2},{1... | collective-permute-start | bytes 270344 | tf_op jit(solution)/shard_map/ppermute | solution.py:83
  13.9 2.3 %collective-permute-done.2.refs_2_ = bf16[176,256]{1,0:T(8,128)(2,1)S(1)} collective-permute-done((bf16[176,256]{1,0:T(8,128)(2,1)S(1)}, bf16[176,256]{1,0:T(8,128)(2,1)S(1)}, u32[]{:S(2)}, u32[]{:S(2)}) %collective-permute-start.2) | collective-permute-done | bytes 90144 | tf_op jit(solution)/shard_map/ppermute | solution.py:83
  16.9 2.3 %shard_map.155 = (bf16[6,256,256]{2,1,0:T(8,128)(2,1)S(1)}, bf16[512,256]{1,0:T(8,128)(2,1)S(1)}, f32[512,256]{1,0:T(8,128)S(1)}) custom-call(s32[1]{0:T(128)} %bitcast.refs_0_, bf16[176,256]{1,0:T(8,128)(2,1)S(1)} %get-tuple-element.47.refs_1_, bf16[176,256]{1,0:T(8,128)(2,1)S(1)} %collective-permute-done.2.refs_2_, ...), custom_call_target="tpu_custom_call" | custom-call | flops 2500000000 | tf_op jit(solution)/shard_map/pallas_call | solution.py:22
  20.0 0.9 %collective-permute-done.12.came_ref = bf16[512,256]{1,0:T(8,128)(2,1)S(1)} collective-permute-done((bf16[512,256]{1,0:T(8,128)(2,1)S(1)}, bf16[512,256]{1,0:T(8,128)(2,1)S(1)}, u32[]{:S(2)}, u32[]{:S(2)}) %collective-permute-start.12) | collective-permute-done | bytes 262176 | tf_op jit(solution)/shard_map/ppermute | solution.py:39
  20.9 1.4 %collective-permute-start.13 = (bf16[256,256]{1,0:T(8,128)(2,1)S(1)}, bf16[256,256]{1,0:T(8,128)(2,1)S(1)}, u32[]{:S(2)}, u32[]{:S(2)}) collective-permute-start(bf16[256,256]{1,0:T(8,128)(2,1)S(1)} %get-tuple-element.69), channel_id=1, source_target_pairs={{0,2},{1,3},{2,0},{3,1},{4,6},{5,7},{6,4},{7,5},{8,10},{9,11},{10,... | collective-permute-start | bytes 393224 | tf_op jit(solution)/shard_map/ppermute | solution.py:39
  22.3 1.3 %collective-permute-start.4 = (bf16[176,256]{1,0:T(8,128)(2,1)S(1)}, bf16[176,256]{1,0:T(8,128)(2,1)S(1)}, u32[]{:S(2)}, u32[]{:S(2)}) collective-permute-start(bf16[176,256]{1,0:T(8,128)(2,1)S(1)} %get-tuple-element.52), channel_id=1, source_target_pairs={{8,0},{12,4},{0,8},{4,12},{9,1},{13,5},{1,9},{5,13},{10,2},{14,6},... | collective-permute-start | bytes 270344 | tf_op jit(solution)/shard_map/ppermute | solution.py:83
  23.6 2.1 %collective-permute-start.5 = (bf16[176,256]{1,0:T(8,128)(2,1)S(1)}, bf16[176,256]{1,0:T(8,128)(2,1)S(1)}, u32[]{:S(2)}, u32[]{:S(2)}) collective-permute-start(bf16[176,256]{1,0:T(8,128)(2,1)S(1)} %get-tuple-element.53), channel_id=1, source_target_pairs={{4,0},{0,4},{12,8},{8,12},{5,1},{1,5},{13,9},{9,13},{6,2},{2,6},{1... | collective-permute-start | bytes 270344 | tf_op jit(solution)/shard_map/ppermute | solution.py:83
  26.5 1.4 %collective-permute-start.14 = (bf16[256,256]{1,0:T(8,128)(2,1)S(1)}, bf16[256,256]{1,0:T(8,128)(2,1)S(1)}, u32[]{:S(2)}, u32[]{:S(2)}) collective-permute-start(bf16[256,256]{1,0:T(8,128)(2,1)S(1)} %shard_map.163.refs_0_), channel_id=1, source_target_pairs={{0,8},{4,12},{8,0},{12,4},{1,9},{5,13},{9,1},{13,5},{2,10},{6,14},... | collective-permute-start | bytes 393224 | tf_op jit(solution)/shard_map/ppermute | solution.py:39
  27.9 1.4 %collective-permute-done.4.refs_3_ = bf16[176,256]{1,0:T(8,128)(2,1)S(1)} collective-permute-done((bf16[176,256]{1,0:T(8,128)(2,1)S(1)}, bf16[176,256]{1,0:T(8,128)(2,1)S(1)}, u32[]{:S(2)}, u32[]{:S(2)}) %collective-permute-start.4) | collective-permute-done | bytes 90144 | tf_op jit(solution)/shard_map/ppermute | solution.py:83
  30.2 5.1 %collective-permute-done.14.refs_1_ = bf16[256,256]{1,0:T(8,128)(2,1)S(1)} collective-permute-done((bf16[256,256]{1,0:T(8,128)(2,1)S(1)}, bf16[256,256]{1,0:T(8,128)(2,1)S(1)}, u32[]{:S(2)}, u32[]{:S(2)}) %collective-permute-start.14) | collective-permute-done | bytes 131104 | tf_op jit(solution)/shard_map/ppermute | solution.py:39
  35.4 1.1 %collective-permute-start.7 = (bf16[128,256]{1,0:T(8,128)(2,1)S(1)}, bf16[128,256]{1,0:T(8,128)(2,1)S(1)}, u32[]{:S(2)}, u32[]{:S(2)}) collective-permute-start(bf16[128,256]{1,0:T(8,128)(2,1)S(1)} %shard_map.158.refs_0_), channel_id=1, source_target_pairs={{0,2},{1,3},{2,0},{3,1},{4,6},{5,7},{6,4},{7,5},{8,10},{9,11},{10,... | collective-permute-start | bytes 196616 | tf_op jit(solution)/shard_map/ppermute | solution.py:39
  36.5 2.0 %collective-permute-start.10 = (bf16[128,256]{1,0:T(8,128)(2,1)S(1)}, bf16[128,256]{1,0:T(8,128)(2,1)S(1)}, u32[]{:S(2)}, u32[]{:S(2)}) collective-permute-start(bf16[128,256]{1,0:T(8,128)(2,1)S(1)} %get-tuple-element.62), channel_id=1, source_target_pairs={{12,0},{0,4},{4,8},{8,12},{13,1},{1,5},{5,9},{9,13},{14,2},{2,6},{... | collective-permute-start | bytes 196616 | tf_op jit(solution)/shard_map/ppermute | solution.py:35
  38.5 1.8 %collective-permute-start.11 = (bf16[128,256]{1,0:T(8,128)(2,1)S(1)}, bf16[128,256]{1,0:T(8,128)(2,1)S(1)}, u32[]{:S(2)}, u32[]{:S(2)}) collective-permute-start(bf16[128,256]{1,0:T(8,128)(2,1)S(1)} %get-tuple-element.63), channel_id=1, source_target_pairs={{4,0},{8,4},{12,8},{0,12},{5,1},{9,5},{13,9},{1,13},{6,2},{10,6},{... | collective-permute-start | bytes 196616 | tf_op jit(solution)/shard_map/ppermute | solution.py:35
  40.4 2.1 %collective-permute-start.8 = (bf16[128,256]{1,0:T(8,128)(2,1)S(1)}, bf16[128,256]{1,0:T(8,128)(2,1)S(1)}, u32[]{:S(2)}, u32[]{:S(2)}) collective-permute-start(bf16[128,256]{1,0:T(8,128)(2,1)S(1)} %shard_map.159.refs_0_), channel_id=1, source_target_pairs={{0,8},{4,12},{8,0},{12,4},{1,9},{5,13},{9,1},{13,5},{2,10},{6,14},... | collective-permute-start | bytes 196616 | tf_op jit(solution)/shard_map/ppermute | solution.py:39
  42.5 0.9 %collective-permute-done.10.refs_1_ = bf16[128,256]{1,0:T(8,128)(2,1)S(1)} collective-permute-done((bf16[128,256]{1,0:T(8,128)(2,1)S(1)}, bf16[128,256]{1,0:T(8,128)(2,1)S(1)}, u32[]{:S(2)}, u32[]{:S(2)}) %collective-permute-start.10) | collective-permute-done | bytes 65568 | tf_op jit(solution)/shard_map/ppermute | solution.py:35
  43.9 1.0 %collective-permute-start.16 = (bf16[256,256]{1,0:T(8,128)(2,1)S(1)}, bf16[256,256]{1,0:T(8,128)(2,1)S(1)}, u32[]{:S(2)}, u32[]{:S(2)}) collective-permute-start(bf16[256,256]{1,0:T(8,128)(2,1)S(1)} %shard_map.165.own_ref), channel_id=1, source_target_pairs={{0,2},{1,3},{2,0},{3,1},{4,6},{5,7},{6,4},{7,5},{8,10},{9,11},{10,... | collective-permute-start | bytes 393224 | tf_op jit(solution)/shard_map/ppermute | solution.py:39
  45.6 1.5 %collective-permute-start.9 = (bf16[128,256]{1,0:T(8,128)(2,1)S(1)}, bf16[128,256]{1,0:T(8,128)(2,1)S(1)}, u32[]{:S(2)}, u32[]{:S(2)}) collective-permute-start(bf16[128,256]{1,0:T(8,128)(2,1)S(1)} %shard_map.160.term_a_ref), channel_id=1, source_target_pairs={{0,4},{4,0},{8,12},{12,8},{1,5},{5,1},{9,13},{13,9},{2,6},{6,2},{1... | collective-permute-start | bytes 196616 | tf_op jit(solution)/shard_map/ppermute | solution.py:39
  47.1 2.8 %collective-permute-done.9.term_b_ref = bf16[128,256]{1,0:T(8,128)(2,1)S(1)} collective-permute-done((bf16[128,256]{1,0:T(8,128)(2,1)S(1)}, bf16[128,256]{1,0:T(8,128)(2,1)S(1)}, u32[]{:S(2)}, u32[]{:S(2)}) %collective-permute-start.9) | collective-permute-done | bytes 65568 | tf_op jit(solution)/shard_map/ppermute | solution.py:39
  51.7 1.2 %shard_map.167 = (f32[256,256]{1,0:T(8,128)}, f32[256,256]{1,0:T(8,128)}, f32[256,256]{1,0:T(8,128)}, f32[256,256]{1,0:T(8,128)}, f32[256,256]{1,0:T(8,128)}) custom-call(s32[1]{0:T(128)} %bitcast.refs_0_, bf16[640,256]{1,0:T(8,128)(2,1)S(1)} %shard_map.166.refs_1_, bf16[640,256]{1,0:T(8,128)(2,1)S(1)} %collective-permute-done.17.refs_2_), custom_call_target="tpu_custom_call" | custom-call | flops 100000000 | tf_op jit(solution)/shard_map/pallas_call | solution.py:22
  (50 shorter events, 8.5 us)
Async XLA Ops:
  0.6 6.1 %copy-start.5 = (bf16[1,256,256]{2,1,0:T(8,128)(2,1)S(1)}, bf16[1,256,256]{2,1,0:T(8,128)(2,1)}, u32[]{:S(2)}) copy-start(bf16[1,256,256]{2,1,0:T(8,128)(2,1)} %param.14) | copy-start | bytes 393220
  1.6 7.5 %collective-permute-start = (bf16[128,256]{1,0:T(8,128)(2,1)S(1)}, bf16[128,256]{1,0:T(8,128)(2,1)S(1)}, u32[]{:S(2)}, u32[]{:S(2)}) collective-permute-start(bf16[128,256]{1,0:T(8,128)(2,1)S(1)} %get-tuple-element.78), channel_id=1, source_target_pairs={{12,0},{0,4},{4,8},{8,12},{13,1},{1,5},{5,9},{9,13},{14,2},{2,6},{... | collective-permute-start | bytes 196616 | tf_op jit(solution)/shard_map/ppermute | solution.py:35
  4.6 5.0 %collective-permute-start.1 = (bf16[128,256]{1,0:T(8,128)(2,1)S(1)}, bf16[128,256]{1,0:T(8,128)(2,1)S(1)}, u32[]{:S(2)}, u32[]{:S(2)}) collective-permute-start(bf16[128,256]{1,0:T(8,128)(2,1)S(1)} %get-tuple-element.77), channel_id=1, source_target_pairs={{4,0},{8,4},{12,8},{0,12},{5,1},{9,5},{13,9},{1,13},{6,2},{10,6},{... | collective-permute-start | bytes 196616 | tf_op jit(solution)/shard_map/ppermute | solution.py:35
  7.4 2.2 %copy-start.6 = (bf16[256,256]{1,0:T(8,128)(2,1)S(1)}, bf16[256,256]{1,0:T(8,128)(2,1)}, u32[]{:S(2)}) copy-start(bf16[256,256]{1,0:T(8,128)(2,1)} %refs_10_.1) | copy-start | bytes 393220
  9.6 7.3 %copy-start.1 = (bf16[256,256]{1,0:T(8,128)(2,1)S(1)}, bf16[256,256]{1,0:T(8,128)(2,1)}, u32[]{:S(2)}) copy-start(bf16[256,256]{1,0:T(8,128)(2,1)} %refs_1_.1) | copy-start | bytes 393220
  9.6 7.3 %copy-start.2 = (bf16[256,256]{1,0:T(8,128)(2,1)S(1)}, bf16[256,256]{1,0:T(8,128)(2,1)}, u32[]{:S(2)}) copy-start(bf16[256,256]{1,0:T(8,128)(2,1)} %refs_2_.3) | copy-start | bytes 393220
  9.6 7.3 %copy-start.3 = (bf16[256,256]{1,0:T(8,128)(2,1)S(1)}, bf16[256,256]{1,0:T(8,128)(2,1)}, u32[]{:S(2)}) copy-start(bf16[256,256]{1,0:T(8,128)(2,1)} %refs_3_.1) | copy-start | bytes 393220
  9.6 7.3 %copy-start.4 = (bf16[256,256]{1,0:T(8,128)(2,1)S(1)}, bf16[256,256]{1,0:T(8,128)(2,1)}, u32[]{:S(2)}) copy-start(bf16[256,256]{1,0:T(8,128)(2,1)} %refs_4_.5) | copy-start | bytes 393220
  10.1 6.2 %collective-permute-start.2 = (bf16[176,256]{1,0:T(8,128)(2,1)S(1)}, bf16[176,256]{1,0:T(8,128)(2,1)S(1)}, u32[]{:S(2)}, u32[]{:S(2)}) collective-permute-start(bf16[176,256]{1,0:T(8,128)(2,1)S(1)} %get-tuple-element.48), channel_id=1, source_target_pairs={{0,8},{4,12},{8,0},{12,4},{1,9},{5,13},{9,1},{13,5},{2,10},{6,14},... | collective-permute-start | bytes 270344 | tf_op jit(solution)/shard_map/ppermute | solution.py:83
  12.0 4.8 %collective-permute-start.3 = (bf16[176,256]{1,0:T(8,128)(2,1)S(1)}, bf16[176,256]{1,0:T(8,128)(2,1)S(1)}, u32[]{:S(2)}, u32[]{:S(2)}) collective-permute-start(bf16[176,256]{1,0:T(8,128)(2,1)S(1)} %get-tuple-element.49), channel_id=1, source_target_pairs={{0,4},{4,0},{8,12},{12,8},{1,5},{5,1},{9,13},{13,9},{2,6},{6,2},{1... | collective-permute-start | bytes 270344 | tf_op jit(solution)/shard_map/ppermute | solution.py:83
  19.2 1.6 %collective-permute-start.12 = (bf16[512,256]{1,0:T(8,128)(2,1)S(1)}, bf16[512,256]{1,0:T(8,128)(2,1)S(1)}, u32[]{:S(2)}, u32[]{:S(2)}) collective-permute-start(bf16[512,256]{1,0:T(8,128)(2,1)S(1)} %get-tuple-element.66), channel_id=1, source_target_pairs={{0,1},{1,0},{2,3},{3,2},{4,5},{5,4},{6,7},{7,6},{8,9},{9,8},{10,11... | collective-permute-start | bytes 786440 | tf_op jit(solution)/shard_map/ppermute | solution.py:39
  20.9 5.6 %collective-permute-start.13 = (bf16[256,256]{1,0:T(8,128)(2,1)S(1)}, bf16[256,256]{1,0:T(8,128)(2,1)S(1)}, u32[]{:S(2)}, u32[]{:S(2)}) collective-permute-start(bf16[256,256]{1,0:T(8,128)(2,1)S(1)} %get-tuple-element.69), channel_id=1, source_target_pairs={{0,2},{1,3},{2,0},{3,1},{4,6},{5,7},{6,4},{7,5},{8,10},{9,11},{10,... | collective-permute-start | bytes 393224 | tf_op jit(solution)/shard_map/ppermute | solution.py:39
  22.3 7.0 %collective-permute-start.4 = (bf16[176,256]{1,0:T(8,128)(2,1)S(1)}, bf16[176,256]{1,0:T(8,128)(2,1)S(1)}, u32[]{:S(2)}, u32[]{:S(2)}) collective-permute-start(bf16[176,256]{1,0:T(8,128)(2,1)S(1)} %get-tuple-element.52), channel_id=1, source_target_pairs={{8,0},{12,4},{0,8},{4,12},{9,1},{13,5},{1,9},{5,13},{10,2},{14,6},... | collective-permute-start | bytes 270344 | tf_op jit(solution)/shard_map/ppermute | solution.py:83
  23.6 6.0 %collective-permute-start.5 = (bf16[176,256]{1,0:T(8,128)(2,1)S(1)}, bf16[176,256]{1,0:T(8,128)(2,1)S(1)}, u32[]{:S(2)}, u32[]{:S(2)}) collective-permute-start(bf16[176,256]{1,0:T(8,128)(2,1)S(1)} %get-tuple-element.53), channel_id=1, source_target_pairs={{4,0},{0,4},{12,8},{8,12},{5,1},{1,5},{13,9},{9,13},{6,2},{2,6},{1... | collective-permute-start | bytes 270344 | tf_op jit(solution)/shard_map/ppermute | solution.py:83
  26.5 8.8 %collective-permute-start.14 = (bf16[256,256]{1,0:T(8,128)(2,1)S(1)}, bf16[256,256]{1,0:T(8,128)(2,1)S(1)}, u32[]{:S(2)}, u32[]{:S(2)}) collective-permute-start(bf16[256,256]{1,0:T(8,128)(2,1)S(1)} %shard_map.163.refs_0_), channel_id=1, source_target_pairs={{0,8},{4,12},{8,0},{12,4},{1,9},{5,13},{9,1},{13,5},{2,10},{6,14},... | collective-permute-start | bytes 393224 | tf_op jit(solution)/shard_map/ppermute | solution.py:39
  30.1 5.3 %collective-permute-start.6 = (bf16[128,256]{1,0:T(8,128)(2,1)S(1)}, bf16[128,256]{1,0:T(8,128)(2,1)S(1)}, u32[]{:S(2)}, u32[]{:S(2)}) collective-permute-start(bf16[128,256]{1,0:T(8,128)(2,1)S(1)} %get-tuple-element.60), channel_id=1, source_target_pairs={{0,1},{1,0},{2,3},{3,2},{4,5},{5,4},{6,7},{7,6},{8,9},{9,8},{10,11... | collective-permute-start | bytes 196616 | tf_op jit(solution)/shard_map/ppermute | solution.py:39
  35.3 7.2 %collective-permute-start.15 = (bf16[256,256]{1,0:T(8,128)(2,1)S(1)}, bf16[256,256]{1,0:T(8,128)(2,1)S(1)}, u32[]{:S(2)}, u32[]{:S(2)}) collective-permute-start(bf16[256,256]{1,0:T(8,128)(2,1)S(1)} %shard_map.164.refs_0_), channel_id=1, source_target_pairs={{0,4},{4,0},{8,12},{12,8},{1,5},{5,1},{9,13},{13,9},{2,6},{6,2},{1... | collective-permute-start | bytes 393224 | tf_op jit(solution)/shard_map/ppermute | solution.py:39
  35.4 4.9 %collective-permute-start.7 = (bf16[128,256]{1,0:T(8,128)(2,1)S(1)}, bf16[128,256]{1,0:T(8,128)(2,1)S(1)}, u32[]{:S(2)}, u32[]{:S(2)}) collective-permute-start(bf16[128,256]{1,0:T(8,128)(2,1)S(1)} %shard_map.158.refs_0_), channel_id=1, source_target_pairs={{0,2},{1,3},{2,0},{3,1},{4,6},{5,7},{6,4},{7,5},{8,10},{9,11},{10,... | collective-permute-start | bytes 196616 | tf_op jit(solution)/shard_map/ppermute | solution.py:39
  36.5 6.9 %collective-permute-start.10 = (bf16[128,256]{1,0:T(8,128)(2,1)S(1)}, bf16[128,256]{1,0:T(8,128)(2,1)S(1)}, u32[]{:S(2)}, u32[]{:S(2)}) collective-permute-start(bf16[128,256]{1,0:T(8,128)(2,1)S(1)} %get-tuple-element.62), channel_id=1, source_target_pairs={{12,0},{0,4},{4,8},{8,12},{13,1},{1,5},{5,9},{9,13},{14,2},{2,6},{... | collective-permute-start | bytes 196616 | tf_op jit(solution)/shard_map/ppermute | solution.py:35
  38.5 5.4 %collective-permute-start.11 = (bf16[128,256]{1,0:T(8,128)(2,1)S(1)}, bf16[128,256]{1,0:T(8,128)(2,1)S(1)}, u32[]{:S(2)}, u32[]{:S(2)}) collective-permute-start(bf16[128,256]{1,0:T(8,128)(2,1)S(1)} %get-tuple-element.63), channel_id=1, source_target_pairs={{4,0},{8,4},{12,8},{0,12},{5,1},{9,5},{13,9},{1,13},{6,2},{10,6},{... | collective-permute-start | bytes 196616 | tf_op jit(solution)/shard_map/ppermute | solution.py:35
  40.4 5.2 %collective-permute-start.8 = (bf16[128,256]{1,0:T(8,128)(2,1)S(1)}, bf16[128,256]{1,0:T(8,128)(2,1)S(1)}, u32[]{:S(2)}, u32[]{:S(2)}) collective-permute-start(bf16[128,256]{1,0:T(8,128)(2,1)S(1)} %shard_map.159.refs_0_), channel_id=1, source_target_pairs={{0,8},{4,12},{8,0},{12,4},{1,9},{5,13},{9,1},{13,5},{2,10},{6,14},... | collective-permute-start | bytes 196616 | tf_op jit(solution)/shard_map/ppermute | solution.py:39
  43.9 6.0 %collective-permute-start.16 = (bf16[256,256]{1,0:T(8,128)(2,1)S(1)}, bf16[256,256]{1,0:T(8,128)(2,1)S(1)}, u32[]{:S(2)}, u32[]{:S(2)}) collective-permute-start(bf16[256,256]{1,0:T(8,128)(2,1)S(1)} %shard_map.165.own_ref), channel_id=1, source_target_pairs={{0,2},{1,3},{2,0},{3,1},{4,6},{5,7},{6,4},{7,5},{8,10},{9,11},{10,... | collective-permute-start | bytes 393224 | tf_op jit(solution)/shard_map/ppermute | solution.py:39
  45.6 4.3 %collective-permute-start.9 = (bf16[128,256]{1,0:T(8,128)(2,1)S(1)}, bf16[128,256]{1,0:T(8,128)(2,1)S(1)}, u32[]{:S(2)}, u32[]{:S(2)}) collective-permute-start(bf16[128,256]{1,0:T(8,128)(2,1)S(1)} %shard_map.160.term_a_ref), channel_id=1, source_target_pairs={{0,4},{4,0},{8,12},{12,8},{1,5},{5,1},{9,13},{13,9},{2,6},{6,2},{1... | collective-permute-start | bytes 196616 | tf_op jit(solution)/shard_map/ppermute | solution.py:39
  50.0 1.7 %collective-permute-start.17 = (bf16[640,256]{1,0:T(8,128)(2,1)S(1)}, bf16[640,256]{1,0:T(8,128)(2,1)S(1)}, u32[]{:S(2)}, u32[]{:S(2)}) collective-permute-start(bf16[640,256]{1,0:T(8,128)(2,1)S(1)} %shard_map.166.refs_1_), channel_id=1, source_target_pairs={{0,1},{1,0},{2,3},{3,2},{4,5},{5,4},{6,7},{7,6},{8,9},{9,8},{10,11... | collective-permute-start | bytes 983048 | tf_op jit(solution)/shard_map/ppermute | solution.py:39
  (4 other events, 4.2 us)
